TPU v7x, 32 devices: a whole 2x2x4 slice. The times are simulated.
32 devices in a mesh: ctx: 8 (over y, x, core), sp: 4 (over z).
Axes of the slice: x: 2, y: 2, z: 4, core: 2. Of those that a mesh axis runs over, the one named last changes fastest.
Arguments:
- enc_in: bfloat16 [2048, 768], P(('ctx', 'sp')), may hold values from -6 to 6
- dec_in: bfloat16 [2048, 768], P(('ctx', 'sp')), may hold values from -6 to 6
- enc_cot: bfloat16 [2048, 768], P(('ctx', 'sp')), may hold values from -6 to 6
- dec_cot: bfloat16 [2048, 768], P(('ctx', 'sp')), may hold values from -6 to 6
- enc_segments: int32 [2048], replicated, may hold values from 0 to 15, as said below
- dec_segments: int32 [2048], replicated, may hold values from 0 to 15, as said below
- buckets: int32 [2, 257], replicated, may hold values from 0 to 31
- enc_norm1: bfloat16 [768], P('ctx'), may hold values from 0.5 to 1.5
- enc_query: bfloat16 [768, 768], P('ctx'), may hold values from -0.0546875 to 0.0546875
- enc_key: bfloat16 [768, 768], P('ctx'), may hold values from -0.21875 to 0.21875
- enc_value: bfloat16 [768, 768], P('ctx'), may hold values from -0.21875 to 0.21875
- enc_proj: bfloat16 [768, 768], P('ctx'), may hold values from -3 to 3
- enc_rel: bfloat16 [384], P('ctx'), may hold values from -4 to 4
- enc_norm2: bfloat16 [768], P('ctx'), may hold values from 0.5 to 1.5
- enc_gate: bfloat16 [768, 2048], P('ctx'), may hold values from -0.21875 to 0.21875
- enc_up: bfloat16 [768, 2048], P('ctx'), may hold values from -0.21875 to 0.21875
- enc_down: bfloat16 [2048, 768], P('ctx'), may hold values from -0.125 to 0.125
- enc_final: bfloat16 [768], P('ctx'), may hold values from 0.5 to 1.5
- dec_norm1: bfloat16 [768], P('ctx'), may hold values from 0.5 to 1.5
- dec_query: bfloat16 [768, 768], P('ctx'), may hold values from -0.0546875 to 0.0546875
- dec_key: bfloat16 [768, 768], P('ctx'), may hold values from -0.21875 to 0.21875
- dec_value: bfloat16 [768, 768], P('ctx'), may hold values from -0.21875 to 0.21875
- dec_proj: bfloat16 [768, 768], P('ctx'), may hold values from -3 to 3
- dec_rel: bfloat16 [384], P('ctx'), may hold values from -4 to 4
- dec_norm2: bfloat16 [768], P('ctx'), may hold values from 0.5 to 1.5
- cross_query: bfloat16 [768, 768], P('ctx'), may hold values from -0.0546875 to 0.0546875
- cross_key: bfloat16 [768, 768], P('ctx'), may hold values from -0.21875 to 0.21875
- cross_value: bfloat16 [768, 768], P('ctx'), may hold values from -0.21875 to 0.21875
- cross_proj: bfloat16 [768, 768], P('ctx'), may hold values from -3 to 3
- dec_norm3: bfloat16 [768], P('ctx'), may hold values from 0.5 to 1.5
- dec_gate: bfloat16 [768, 2048], P('ctx'), may hold values from -0.21875 to 0.21875
- dec_up: bfloat16 [768, 2048], P('ctx'), may hold values from -0.21875 to 0.21875
- dec_down: bfloat16 [2048, 768], P('ctx'), may hold values from -0.125 to 0.125
Outputs:
- enc_out: float32 [2048, 768], P(('ctx', 'sp'))
- dec_out: float32 [2048, 768], P(('ctx', 'sp'))
- enc_in_grad: float32 [2048, 768], P(('ctx', 'sp'))
- dec_in_grad: float32 [2048, 768], P(('ctx', 'sp'))
- enc_norm1_grad: float32 [768], P('ctx')
- enc_query_grad: float32 [768, 768], P('ctx')
- enc_key_grad: float32 [768, 768], P('ctx')
- enc_value_grad: float32 [768, 768], P('ctx')
- enc_proj_grad: float32 [768, 768], P('ctx')
- enc_rel_grad: float32 [384], P('ctx')
- enc_norm2_grad: float32 [768], P('ctx')
- enc_gate_grad: float32 [768, 2048], P('ctx')
- enc_up_grad: float32 [768, 2048], P('ctx')
- enc_down_grad: float32 [2048, 768], P('ctx')
- enc_final_grad: float32 [768], P('ctx')
- dec_norm1_grad: float32 [768], P('ctx')
- dec_query_grad: float32 [768, 768], P('ctx')
- dec_key_grad: float32 [768, 768], P('ctx')
- dec_value_grad: float32 [768, 768], P('ctx')
- dec_proj_grad: float32 [768, 768], P('ctx')
- dec_rel_grad: float32 [384], P('ctx')
- dec_norm2_grad: float32 [768], P('ctx')
- cross_query_grad: float32 [768, 768], P('ctx')
- cross_key_grad: float32 [768, 768], P('ctx')
- cross_value_grad: float32 [768, 768], P('ctx')
- cross_proj_grad: float32 [768, 768], P('ctx')
- dec_norm3_grad: float32 [768], P('ctx')
- dec_gate_grad: float32 [768, 2048], P('ctx')
- dec_up_grad: float32 [768, 2048], P('ctx')
- dec_down_grad: float32 [2048, 768], P('ctx')
Inputs may be any that keep to these rules, and one draw needn't show every extreme that they name: `enc_segments`: numbers never fall along a sequence and every number from 0 to 15 labels a nonempty document; one document starts within the first 256 tokens and ends within the last 256 tokens, and every other lies within the first or the last 256 tokens. `dec_segments`: as for enc_segments; a decoder token attends to the encoder tokens of the same number.
All inputs are finite; a program needn't handle non-finite values.
Results may differ from a plain program's by a relative error of at most 0.04.
Values may be sent and summed in bfloat16 or wider, within the bound.
A program may use at most 576 MiB of HBM per device.

v0:
```python
import math

import jax
import jax.numpy as jnp
from jax import lax
from jax.sharding import PartitionSpec as P

HEADS = 12
HD = 64


EPSILON = 1e-06
NEGATIVE = -1e30
HIGHEST = lax.Precision.HIGHEST


def rms_norm(values, norm_gain):
    return (
        values * lax.rsqrt(jnp.mean(values * values, axis=-1, keepdims=True) + EPSILON) * norm_gain
    )


def norm_pullback(values, norm_gain, grad_normed):
    _, pullback = jax.vjp(rms_norm, values, norm_gain)
    return pullback(grad_normed)


def gated(gate_val, up_val):
    return jax.nn.gelu(gate_val, approximate=True) * up_val


def project(left, right):
    return jnp.dot(left, right, preferred_element_type=jnp.float32)


def weight_grad(left, right):
    return jnp.einsum("td,te->de", left, right, preferred_element_type=jnp.float32)


def input_grad(grad_out, weight):
    return jnp.einsum("te,de->td", grad_out, weight, preferred_element_type=jnp.float32)


def head_table(relative, table_row, heads_here):
    bucket_count = relative.shape[0] // HEADS
    onehot = (table_row[:, None] == jnp.arange(bucket_count, dtype=jnp.int32)[None, :]).astype(
        jnp.float32
    )
    bias_grid = relative.astype(jnp.float32).reshape(bucket_count, HEADS)
    full_table = jnp.dot(onehot, bias_grid, precision=HIGHEST).T
    first_head = lax.axis_index("sp") * heads_here
    return (lax.dynamic_slice_in_dim(full_table, first_head, heads_here, 0), onehot)


def table_grad(grad_table, onehot, heads_here):
    full_grad = jnp.zeros((HEADS, onehot.shape[0]), jnp.float32)
    full_grad = lax.dynamic_update_slice_in_dim(
        full_grad, grad_table, lax.axis_index("sp") * heads_here, 0
    )
    return jnp.dot(onehot.T, full_grad.T, precision=HIGHEST).reshape(-1)


def bias_block(head_bias, pad_len, offset_q, rows, offset_k, cols):
    head_count, table_len = head_bias.shape
    reach_len = (table_len - 1) // 2
    left_edge = jnp.broadcast_to(head_bias[:, :1], (head_count, pad_len))
    right_edge = jnp.broadcast_to(head_bias[:, -1:], (head_count, pad_len))
    padded = jnp.concatenate([left_edge, head_bias, right_edge], axis=1)
    band_width = rows + cols - 1
    start = offset_k - offset_q - (rows - 1) + reach_len + pad_len
    band = lax.dynamic_slice_in_dim(padded, start, band_width, 1)
    tiled = jnp.broadcast_to(band[:, None, :], (head_count, rows, band_width)).reshape(
        head_count, rows * band_width
    )
    skewed = tiled[:, rows - 1 : rows - 1 + rows * (band_width - 1)].reshape(
        head_count, rows, band_width - 1
    )
    return skewed[:, :, :cols]


def make_frame(query_local, query_ids, key_ids, head_bias, causal):
    local_len = query_local.shape[0]
    heads_here = query_local.shape[1] // HD
    offset_q = lax.axis_index("ctx") * local_len
    ids_q = lax.dynamic_slice_in_dim(query_ids, offset_q, local_len, 0)
    row_ids = offset_q + jnp.arange(local_len, dtype=jnp.int32)
    query_heads = query_local.reshape(local_len, heads_here, HD)
    pad_len = query_ids.shape[0] + key_ids.shape[0]

    def bias_of(entries, offset_k, length):
        return bias_block(entries, pad_len, offset_q, local_len, offset_k, length)

    def scores_of(key_block, offset_k):
        length = key_block.shape[0]
        key_heads = key_block.reshape(length, heads_here, HD)
        raw_scores = jnp.einsum(
            "qhd,khd->hqk", query_heads, key_heads, preferred_element_type=jnp.float32
        )
        col_ids = offset_k + jnp.arange(length, dtype=jnp.int32)
        ids_k = lax.dynamic_slice_in_dim(key_ids, offset_k, length, 0)
        allowed = ids_q[:, None] == ids_k[None, :]
        if causal:
            allowed = allowed & (col_ids[None, :] <= row_ids[:, None])
        if head_bias is not None:
            raw_scores = raw_scores + bias_of(head_bias, offset_k, length)
        return (raw_scores, allowed)

    def touches(offset_k, length):
        first_id = lax.dynamic_slice_in_dim(key_ids, offset_k, 1, 0)[0]
        last_id = lax.dynamic_slice_in_dim(key_ids, offset_k + length - 1, 1, 0)[0]
        touched = (ids_q[0] <= last_id) & (first_id <= ids_q[-1])
        if causal:
            touched = touched & (offset_k <= offset_q + local_len - 1)
        return touched

    return (query_heads, scores_of, touches, bias_of)


def sweep(keys_gathered, local_len, step_fn, carry_state):
    key_all, value_all = keys_gathered
    block_len = local_len * math.gcd(4, lax.axis_size("ctx"))

    def sweep_loop_body(number, running):
        offset_k = number * block_len
        key_block = lax.dynamic_slice_in_dim(key_all, offset_k, block_len, 0)
        value_block = lax.dynamic_slice_in_dim(value_all, offset_k, block_len, 0)
        return step_fn(running, key_block, value_block, offset_k)

    return lax.fori_loop(0, key_all.shape[0] // block_len, sweep_loop_body, carry_state)


def whole_keys(key_local, value_local):
    return (
        lax.all_gather(key_local, "ctx", axis=0, tiled=True),
        lax.all_gather(value_local, "ctx", axis=0, tiled=True),
    )


def attention_forward(query_proj, key_proj, value_proj, query_ids, key_ids, head_bias, causal):
    query_local, key_local, value_local = (
        lax.all_to_all(query_proj, "sp", split_axis=1, concat_axis=0, tiled=True),
        lax.all_to_all(key_proj, "sp", split_axis=1, concat_axis=0, tiled=True),
        lax.all_to_all(value_proj, "sp", split_axis=1, concat_axis=0, tiled=True),
    )
    local_len = query_local.shape[0]
    heads_here = query_local.shape[1] // HD
    query_heads, scores_of, touches, _ = make_frame(
        query_local, query_ids, key_ids, head_bias, causal
    )
    key_block = lax.all_gather(key_local, "ctx", axis=0, tiled=True)
    value_block = lax.all_gather(value_local, "ctx", axis=0, tiled=True)
    offset_k = jnp.int32(0)
    length = key_block.shape[0]
    row_top = jnp.full((heads_here, local_len), NEGATIVE, jnp.float32)
    weighted = jnp.zeros((local_len, heads_here, HD), jnp.float32)
    raw_scores, allowed = scores_of(key_block, offset_k)
    masked = jnp.where(allowed[None], raw_scores, NEGATIVE)
    new_top = jnp.maximum(row_top, jnp.max(masked, axis=-1))
    weights = jnp.where(allowed[None], jnp.exp(masked - new_top[..., None]), 0.0)
    rescale = jnp.exp(row_top - new_top)
    value_heads = value_block.reshape(length, heads_here, HD)
    increment = jnp.einsum(
        "hqk,khd->qhd",
        weights.astype(jnp.bfloat16),
        value_heads,
        preferred_element_type=jnp.float32,
    )
    row_top, row_total, weighted = (
        new_top,
        jnp.sum(weights, axis=-1),
        weighted * rescale.T[:, :, None] + increment,
    )
    mixed_heads = weighted / row_total.T[:, :, None]
    log_total = row_top + jnp.log(row_total)
    mixed_low = mixed_heads.reshape(local_len, heads_here * HD).astype(jnp.bfloat16)
    mixed_tokens = lax.all_to_all(mixed_low, "sp", split_axis=0, concat_axis=1, tiled=True)
    retained = (
        query_local,
        key_local,
        value_local,
        mixed_heads,
        log_total,
        None,
        query_ids,
        key_ids,
        head_bias,
        causal,
    )
    return (mixed_tokens, retained)


def attention_backward(grad_mixed, retained):
    (
        query_local,
        key_local,
        value_local,
        mixed_heads,
        log_total,
        gathered,
        query_ids,
        key_ids,
        head_bias,
        causal,
    ) = retained
    grad_local = lax.all_to_all(grad_mixed, "sp", split_axis=1, concat_axis=0, tiled=True)
    local_len = query_local.shape[0]
    heads_here = query_local.shape[1] // HD
    width = heads_here * HD
    query_heads, scores_of, touches, bias_of = make_frame(
        query_local, query_ids, key_ids, head_bias, causal
    )
    grad_heads = grad_local.reshape(local_len, heads_here, HD)
    row_inner = jnp.einsum("qhd,qhd->hq", grad_heads.astype(jnp.float32), mixed_heads)
    gathered = whole_keys(key_local, value_local)
    table_zero = jnp.zeros(head_bias.shape if head_bias is not None else (1,), jnp.float32)

    def gradients_of(key_block, value_block, offset_k):
        length = key_block.shape[0]
        raw_scores, allowed = scores_of(key_block, offset_k)
        probabilities = jnp.where(allowed[None], jnp.exp(raw_scores - log_total[..., None]), 0.0)
        value_heads = value_block.reshape(length, heads_here, HD)
        grad_probs = jnp.einsum(
            "qhd,khd->hqk", grad_heads, value_heads, preferred_element_type=jnp.float32
        )
        grad_scores = (probabilities * (grad_probs - row_inner[..., None])).astype(jnp.bfloat16)
        return (probabilities, grad_scores)

    def table_part(grad_scores, offset_k, length):
        if head_bias is None:
            return table_zero
        _, pullback = jax.vjp(lambda entries: bias_of(entries, offset_k, length), head_bias)
        return pullback(grad_scores.astype(jnp.float32))[0]

    def key_terms_of(probabilities, grad_scores, length):
        grad_key = jnp.einsum(
            "hqk,qhd->khd", grad_scores, query_heads, preferred_element_type=jnp.float32
        )
        grad_value = jnp.einsum(
            "hqk,qhd->khd",
            probabilities.astype(jnp.bfloat16),
            grad_heads,
            preferred_element_type=jnp.float32,
        )
        return jnp.concatenate(
            [grad_key.reshape(length, width), grad_value.reshape(length, width)], axis=1
        )

    def query_part(grad_scores, key_block):
        length = key_block.shape[0]
        key_heads = key_block.reshape(length, heads_here, HD)
        return jnp.einsum(
            "hqk,khd->qhd", grad_scores, key_heads, preferred_element_type=jnp.float32
        )

    def query_step(running, key_block, value_block, offset_k):
        length = key_block.shape[0]
        grad_query, grad_table = running
        probabilities, grad_scores = gradients_of(key_block, value_block, offset_k)
        return (
            grad_query + query_part(grad_scores, key_block),
            grad_table + table_part(grad_scores, offset_k, length),
        )

    query_zero = jnp.zeros((local_len, heads_here, HD), jnp.float32)
    block_len = local_len * math.gcd(4, lax.axis_size("ctx"))
    grad_query, grad_table = sweep(gathered, local_len, query_step, (query_zero, table_zero))
    key_all, value_all = gathered
    step_len = math.gcd(lax.axis_size("ctx") * local_len, block_len)

    def term_loop_body(number, rows_acc):
        offset_b = number * step_len
        key_block = lax.dynamic_slice_in_dim(key_all, offset_b, step_len, 0)
        value_block = lax.dynamic_slice_in_dim(value_all, offset_b, step_len, 0)
        probabilities, grad_scores = gradients_of(key_block, value_block, offset_b)
        return lax.dynamic_update_slice_in_dim(
            rows_acc, key_terms_of(probabilities, grad_scores, step_len), number * step_len, 0
        )

    own_rows = lax.psum_scatter(
        lax.fori_loop(
            0,
            lax.axis_size("ctx") * local_len // step_len,
            term_loop_body,
            jnp.zeros((lax.axis_size("ctx") * local_len, 2 * width), jnp.float32),
        ),
        "ctx",
        scatter_dimension=0,
        tiled=True,
    )
    grad_q_low = grad_query.reshape(local_len, width).astype(jnp.bfloat16)
    grad_k_low = own_rows[:, :width].astype(jnp.bfloat16)
    grad_v_low = own_rows[:, width:].astype(jnp.bfloat16)
    grad_q_tok, grad_k_tok, grad_v_tok = (
        lax.all_to_all(grad_q_low, "sp", split_axis=0, concat_axis=1, tiled=True),
        lax.all_to_all(grad_k_low, "sp", split_axis=0, concat_axis=1, tiled=True),
        lax.all_to_all(grad_v_low, "sp", split_axis=0, concat_axis=1, tiled=True),
    )
    return (grad_q_tok, grad_k_tok, grad_v_tok, grad_table)


def attention_layer(
    residual,
    source,
    norm_gain,
    w_query,
    w_key,
    w_value,
    w_proj,
    query_ids,
    key_ids,
    head_bias,
    causal,
):
    normed = rms_norm(residual, norm_gain).astype(jnp.bfloat16)
    kv_input = normed if source is None else source
    query_proj = project(normed, w_query).astype(jnp.bfloat16)
    key_proj = project(kv_input, w_key).astype(jnp.bfloat16)
    value_proj = project(kv_input, w_value).astype(jnp.bfloat16)
    mixed_tokens, retained = attention_forward(
        query_proj, key_proj, value_proj, query_ids, key_ids, head_bias, causal
    )
    result = residual + project(mixed_tokens, w_proj)
    return (result, (residual, normed, kv_input, mixed_tokens, retained))


def attention_layer_back(grad_out, saved, norm_gain, w_query, w_key, w_value, w_proj, is_cross):
    residual, normed, kv_input, mixed_tokens, retained = saved
    grad_low = grad_out.astype(jnp.bfloat16)
    grad_proj = weight_grad(mixed_tokens, grad_low)
    grad_mixed = input_grad(grad_low, w_proj).astype(jnp.bfloat16)
    grad_q_tok, grad_k_tok, grad_v_tok, grad_table = attention_backward(grad_mixed, retained)
    grad_wq = weight_grad(normed, grad_q_tok)
    grad_wk = weight_grad(kv_input, grad_k_tok)
    grad_wv = weight_grad(kv_input, grad_v_tok)
    grad_source = input_grad(grad_k_tok, w_key) + input_grad(grad_v_tok, w_value)
    grad_normed = input_grad(grad_q_tok, w_query)
    if not is_cross:
        grad_normed = grad_normed + grad_source
        grad_source = None
    grad_resid, grad_gain = norm_pullback(residual, norm_gain, grad_normed)
    return (
        grad_out + grad_resid,
        grad_source,
        (grad_gain, grad_wq, grad_wk, grad_wv, grad_proj, grad_table),
    )


def feed_layer(residual, norm_gain, w_gate, w_up, w_down):
    normed = rms_norm(residual, norm_gain).astype(jnp.bfloat16)
    gate_val = project(normed, w_gate)
    up_val = project(normed, w_up)
    hidden = gated(gate_val, up_val).astype(jnp.bfloat16)
    return (residual + project(hidden, w_down), (residual, normed, gate_val, up_val, hidden))


def feed_layer_back(grad_out, saved, norm_gain, w_gate, w_up, w_down):
    residual, normed, gate_val, up_val, hidden = saved
    grad_low = grad_out.astype(jnp.bfloat16)
    grad_down = weight_grad(hidden, grad_low)
    grad_hidden = input_grad(grad_low, w_down)
    _, pullback = jax.vjp(gated, gate_val, up_val)
    grad_gate, grad_up = pullback(grad_hidden)
    grad_gate = grad_gate.astype(jnp.bfloat16)
    grad_up = grad_up.astype(jnp.bfloat16)
    grad_wg = weight_grad(normed, grad_gate)
    grad_wu = weight_grad(normed, grad_up)
    grad_normed = input_grad(grad_gate, w_gate) + input_grad(grad_up, w_up)
    grad_resid, grad_gain = norm_pullback(residual, norm_gain, grad_normed)
    return (grad_out + grad_resid, (grad_gain, grad_wg, grad_wu, grad_down))


def per_device(
    enc_in,
    dec_in,
    enc_cot,
    dec_cot,
    enc_segments,
    dec_segments,
    buckets,
    enc_norm1,
    enc_query,
    enc_key,
    enc_value,
    enc_proj,
    enc_rel,
    enc_norm2,
    enc_gate,
    enc_up,
    enc_down,
    enc_final,
    dec_norm1,
    dec_query,
    dec_key,
    dec_value,
    dec_proj,
    dec_rel,
    dec_norm2,
    cross_query,
    cross_key,
    cross_value,
    cross_proj,
    dec_norm3,
    dec_gate,
    dec_up,
    dec_down,
):
    (
        enc_norm1,
        enc_query,
        enc_key,
        enc_value,
        enc_proj,
        enc_rel,
        enc_norm2,
        enc_gate,
        enc_up,
        enc_down,
        enc_final,
        dec_norm1,
        dec_query,
        dec_key,
        dec_value,
        dec_proj,
        dec_rel,
        dec_norm2,
        cross_query,
        cross_key,
        cross_value,
        cross_proj,
        dec_norm3,
        dec_gate,
        dec_up,
        dec_down,
    ) = (
        lax.all_gather(enc_norm1, "ctx", axis=0, tiled=True),
        lax.all_gather(enc_query, "ctx", axis=0, tiled=True),
        lax.all_gather(enc_key, "ctx", axis=0, tiled=True),
        lax.all_gather(enc_value, "ctx", axis=0, tiled=True),
        lax.all_gather(enc_proj, "ctx", axis=0, tiled=True),
        lax.all_gather(enc_rel, "ctx", axis=0, tiled=True),
        lax.all_gather(enc_norm2, "ctx", axis=0, tiled=True),
        lax.all_gather(enc_gate, "ctx", axis=0, tiled=True),
        lax.all_gather(enc_up, "ctx", axis=0, tiled=True),
        lax.all_gather(enc_down, "ctx", axis=0, tiled=True),
        lax.all_gather(enc_final, "ctx", axis=0, tiled=True),
        lax.all_gather(dec_norm1, "ctx", axis=0, tiled=True),
        lax.all_gather(dec_query, "ctx", axis=0, tiled=True),
        lax.all_gather(dec_key, "ctx", axis=0, tiled=True),
        lax.all_gather(dec_value, "ctx", axis=0, tiled=True),
        lax.all_gather(dec_proj, "ctx", axis=0, tiled=True),
        lax.all_gather(dec_rel, "ctx", axis=0, tiled=True),
        lax.all_gather(dec_norm2, "ctx", axis=0, tiled=True),
        lax.all_gather(cross_query, "ctx", axis=0, tiled=True),
        lax.all_gather(cross_key, "ctx", axis=0, tiled=True),
        lax.all_gather(cross_value, "ctx", axis=0, tiled=True),
        lax.all_gather(cross_proj, "ctx", axis=0, tiled=True),
        lax.all_gather(dec_norm3, "ctx", axis=0, tiled=True),
        lax.all_gather(dec_gate, "ctx", axis=0, tiled=True),
        lax.all_gather(dec_up, "ctx", axis=0, tiled=True),
        lax.all_gather(dec_down, "ctx", axis=0, tiled=True),
    )
    enc_norm1 = enc_norm1.astype(jnp.float32)
    enc_norm2 = enc_norm2.astype(jnp.float32)
    enc_final = enc_final.astype(jnp.float32)
    dec_norm1 = dec_norm1.astype(jnp.float32)
    dec_norm2 = dec_norm2.astype(jnp.float32)
    dec_norm3 = dec_norm3.astype(jnp.float32)
    heads_here = HEADS // lax.axis_size("sp")
    enc_table, enc_onehot = head_table(enc_rel, buckets[0], heads_here)
    dec_table, dec_onehot = head_table(dec_rel, buckets[1], heads_here)
    enc_x = enc_in.astype(jnp.float32)
    enc_mid, enc_saved_a = attention_layer(
        enc_x,
        None,
        enc_norm1,
        enc_query,
        enc_key,
        enc_value,
        enc_proj,
        enc_segments,
        enc_segments,
        enc_table,
        False,
    )
    enc_result, enc_saved_f = feed_layer(enc_mid, enc_norm2, enc_gate, enc_up, enc_down)
    memory = rms_norm(enc_result, enc_final).astype(jnp.bfloat16)
    dec_x = dec_in.astype(jnp.float32)
    dec_mid, dec_saved_a = attention_layer(
        dec_x,
        None,
        dec_norm1,
        dec_query,
        dec_key,
        dec_value,
        dec_proj,
        dec_segments,
        dec_segments,
        dec_table,
        True,
    )
    dec_cross, dec_saved_c = attention_layer(
        dec_mid,
        memory,
        dec_norm2,
        cross_query,
        cross_key,
        cross_value,
        cross_proj,
        dec_segments,
        enc_segments,
        None,
        False,
    )
    dec_result, dec_saved_f = feed_layer(dec_cross, dec_norm3, dec_gate, dec_up, dec_down)
    grad_dec, dec_ff_grads = feed_layer_back(
        dec_cot.astype(jnp.float32), dec_saved_f, dec_norm3, dec_gate, dec_up, dec_down
    )
    grad_dec, grad_memory, cross_grads = attention_layer_back(
        grad_dec, dec_saved_c, dec_norm2, cross_query, cross_key, cross_value, cross_proj, True
    )
    grad_dec, _, dec_self_grads = attention_layer_back(
        grad_dec, dec_saved_a, dec_norm1, dec_query, dec_key, dec_value, dec_proj, False
    )
    grad_enc_out, grad_final = norm_pullback(enc_result, enc_final, grad_memory)
    grad_enc, enc_ff_grads = feed_layer_back(
        enc_cot.astype(jnp.float32) + grad_enc_out,
        enc_saved_f,
        enc_norm2,
        enc_gate,
        enc_up,
        enc_down,
    )
    grad_enc, _, enc_self_grads = attention_layer_back(
        grad_enc, enc_saved_a, enc_norm1, enc_query, enc_key, enc_value, enc_proj, False
    )
    e_gain1, e_wq, e_wk, e_wv, e_wo, e_table = enc_self_grads
    e_gain2, e_wg, e_wu, e_wd = enc_ff_grads
    d_gain1, d_wq, d_wk, d_wv, d_wo, d_table = dec_self_grads
    c_gain, c_wq, c_wk, c_wv, c_wo, _ = cross_grads
    d_gain3, d_wg, d_wu, d_wd = dec_ff_grads
    e_rel = table_grad(e_table, enc_onehot, heads_here)
    d_rel = table_grad(d_table, dec_onehot, heads_here)
    shards = (
        lax.psum_scatter(e_gain1, "ctx", scatter_dimension=0, tiled=True),
        lax.psum_scatter(e_wq, "ctx", scatter_dimension=0, tiled=True),
        lax.psum_scatter(e_wk, "ctx", scatter_dimension=0, tiled=True),
        lax.psum_scatter(e_wv, "ctx", scatter_dimension=0, tiled=True),
        lax.psum_scatter(e_wo, "ctx", scatter_dimension=0, tiled=True),
        lax.psum_scatter(e_rel, "ctx", scatter_dimension=0, tiled=True),
        lax.psum_scatter(e_gain2, "ctx", scatter_dimension=0, tiled=True),
        lax.psum_scatter(e_wg, "ctx", scatter_dimension=0, tiled=True),
        lax.psum_scatter(e_wu, "ctx", scatter_dimension=0, tiled=True),
        lax.psum_scatter(e_wd, "ctx", scatter_dimension=0, tiled=True),
        lax.psum_scatter(grad_final, "ctx", scatter_dimension=0, tiled=True),
        lax.psum_scatter(d_gain1, "ctx", scatter_dimension=0, tiled=True),
        lax.psum_scatter(d_wq, "ctx", scatter_dimension=0, tiled=True),
        lax.psum_scatter(d_wk, "ctx", scatter_dimension=0, tiled=True),
        lax.psum_scatter(d_wv, "ctx", scatter_dimension=0, tiled=True),
        lax.psum_scatter(d_wo, "ctx", scatter_dimension=0, tiled=True),
        lax.psum_scatter(d_rel, "ctx", scatter_dimension=0, tiled=True),
        lax.psum_scatter(c_gain, "ctx", scatter_dimension=0, tiled=True),
        lax.psum_scatter(c_wq, "ctx", scatter_dimension=0, tiled=True),
        lax.psum_scatter(c_wk, "ctx", scatter_dimension=0, tiled=True),
        lax.psum_scatter(c_wv, "ctx", scatter_dimension=0, tiled=True),
        lax.psum_scatter(c_wo, "ctx", scatter_dimension=0, tiled=True),
        lax.psum_scatter(d_gain3, "ctx", scatter_dimension=0, tiled=True),
        lax.psum_scatter(d_wg, "ctx", scatter_dimension=0, tiled=True),
        lax.psum_scatter(d_wu, "ctx", scatter_dimension=0, tiled=True),
        lax.psum_scatter(d_wd, "ctx", scatter_dimension=0, tiled=True),
    )
    (
        s_gain1,
        s_wq,
        s_wk,
        s_wv,
        s_wo,
        s_rel,
        s_gain2,
        s_wg,
        s_wu,
        s_wd,
        s_final,
        t_gain1,
        t_wq,
        t_wk,
        t_wv,
        t_wo,
        t_rel,
        t_gain2,
        t_cq,
        t_ck,
        t_cv,
        t_co,
        t_gain3,
        t_wg,
        t_wu,
        t_wd,
    ) = shards
    reduced = (
        lax.psum(s_gain1.astype(jnp.bfloat16), "sp").astype(jnp.float32),
        lax.psum(s_wq.astype(jnp.bfloat16), "sp").astype(jnp.float32),
        lax.psum(s_wk.astype(jnp.bfloat16), "sp").astype(jnp.float32),
        lax.psum(s_wv.astype(jnp.bfloat16), "sp").astype(jnp.float32),
        lax.psum(s_wo.astype(jnp.bfloat16), "sp").astype(jnp.float32),
        lax.psum(s_rel.astype(jnp.bfloat16), "sp").astype(jnp.float32),
        lax.psum(s_gain2.astype(jnp.bfloat16), "sp").astype(jnp.float32),
        lax.psum(s_wg.astype(jnp.bfloat16), "sp").astype(jnp.float32),
        lax.psum(s_wu.astype(jnp.bfloat16), "sp").astype(jnp.float32),
        lax.psum(s_wd.astype(jnp.bfloat16), "sp").astype(jnp.float32),
        lax.psum(s_final.astype(jnp.bfloat16), "sp").astype(jnp.float32),
        lax.psum(t_gain1.astype(jnp.bfloat16), "sp").astype(jnp.float32),
        lax.psum(t_wq.astype(jnp.bfloat16), "sp").astype(jnp.float32),
        lax.psum(t_wk.astype(jnp.bfloat16), "sp").astype(jnp.float32),
        lax.psum(t_wv.astype(jnp.bfloat16), "sp").astype(jnp.float32),
        lax.psum(t_wo.astype(jnp.bfloat16), "sp").astype(jnp.float32),
        lax.psum(t_rel.astype(jnp.bfloat16), "sp").astype(jnp.float32),
        lax.psum(t_gain2.astype(jnp.bfloat16), "sp").astype(jnp.float32),
        lax.psum(t_cq.astype(jnp.bfloat16), "sp").astype(jnp.float32),
        lax.psum(t_ck.astype(jnp.bfloat16), "sp").astype(jnp.float32),
        lax.psum(t_cv.astype(jnp.bfloat16), "sp").astype(jnp.float32),
        lax.psum(t_co.astype(jnp.bfloat16), "sp").astype(jnp.float32),
        lax.psum(t_gain3.astype(jnp.bfloat16), "sp").astype(jnp.float32),
        lax.psum(t_wg.astype(jnp.bfloat16), "sp").astype(jnp.float32),
        lax.psum(t_wu.astype(jnp.bfloat16), "sp").astype(jnp.float32),
        lax.psum(t_wd.astype(jnp.bfloat16), "sp").astype(jnp.float32),
    )
    return (enc_result, dec_result, grad_enc, grad_dec) + tuple(reduced)


def solution(mesh):
    placed = (
        P(("ctx", "sp"), None),
        P(("ctx", "sp"), None),
        P(("ctx", "sp"), None),
        P(("ctx", "sp"), None),
        P(),
        P(),
        P(),
        P("ctx"),
        P("ctx", None),
        P("ctx", None),
        P("ctx", None),
        P("ctx", None),
        P("ctx"),
        P("ctx"),
        P("ctx", None),
        P("ctx", None),
        P("ctx", None),
        P("ctx"),
        P("ctx"),
        P("ctx", None),
        P("ctx", None),
        P("ctx", None),
        P("ctx", None),
        P("ctx"),
        P("ctx"),
        P("ctx", None),
        P("ctx", None),
        P("ctx", None),
        P("ctx", None),
        P("ctx"),
        P("ctx", None),
        P("ctx", None),
        P("ctx", None),
    )
    return jax.shard_map(
        per_device,
        mesh=mesh,
        in_specs=placed,
        out_specs=(
            P(("ctx", "sp"), None),
            P(("ctx", "sp"), None),
            P(("ctx", "sp"), None),
            P(("ctx", "sp"), None),
            P("ctx"),
            P("ctx", None),
            P("ctx", None),
            P("ctx", None),
            P("ctx", None),
            P("ctx"),
            P("ctx"),
            P("ctx", None),
            P("ctx", None),
            P("ctx", None),
            P("ctx"),
            P("ctx"),
            P("ctx", None),
            P("ctx", None),
            P("ctx", None),
            P("ctx", None),
            P("ctx"),
            P("ctx"),
            P("ctx", None),
            P("ctx", None),
            P("ctx", None),
            P("ctx", None),
            P("ctx"),
            P("ctx", None),
            P("ctx", None),
            P("ctx", None),
        ),
        check_vma=False,
    )
```

profile of v0, /device:TPU:0, one launch (start us, length us, event | category | flops | bytes accessed | tf_op | source)
XLA Modules:
  0.0 2060.1 jit_solution(12964039507855952862)
XLA Ops:
  22.9 26.4 %all-reduce.25 = (bf16[768]{0:T(1024)(128)(2,1)S(1)}, bf16[384]{0:T(512)(128)(2,1)S(1)}, bf16[768]{0:T(1024)(128)(2,1)S(1)}, bf16[768]{0:T(1024)(128)(2,1)S(1)},...) all-reduce(bf16[768]{0:T(1024)(128)(2,1)S(1)} %dynamic-update-slice, ...), channel_id=1, replica_groups=mesh['ctx'=8,'sp'=4] {'ctx'}, use_global_device_ids=true, to_apply=%add.8 | all-reduce | flops 5376 | bytes 21504
  54.4 15.1 reshape.1077
  80.9 16.5 reshape.1078
  101.1 15.1 reshape.1083
  127.9 16.4 reshape.1084
  202.2 12.3 all_gather.108
  237.2 11.7 all_gather.117
  319.8 30.7 %all-gather.31.cloned.1.call-done = bf16[2048,768]{1,0:T(8,128)(2,1)} async-done(((bf16[256,768]{1,0:T(8,128)(2,1)}), bf16[2048,768]{1,0:T(8,128)(2,1)}) %all-gather.31.cloned.1.call-update) | async-done | bytes 3145744 | tf_op jit(solution)/shard_map/all_gather | solution.py:444
  353.2 23.2 %all-gather.43.cloned.1.call-done = bf16[768,768]{1,0:T(8,128)(2,1)} async-done(((bf16[96,768]{1,0:T(8,128)(2,1)}), bf16[768,768]{1,0:T(8,128)(2,1)}) %all-gather.43.cloned.1.call-update) | async-done | bytes 1179664 | tf_op jit(solution)/shard_map/all_gather | solution.py:454
  383.4 18.8 all-gather.45.cloned.1.call-done
  409.3 12.5 all_gather.126
  423.0 12.2 all_gather.128
  466.8 30.7 %all-gather.51.cloned.1.call-done = bf16[768,2048]{1,0:T(8,128)(2,1)} async-done(((bf16[96,2048]{1,0:T(8,128)(2,1)}), bf16[768,2048]{1,0:T(8,128)(2,1)}) %all-gather.51.cloned.1.call-update) | async-done | bytes 3145744 | tf_op jit(solution)/shard_map/all_gather | solution.py:459
  500.9 30.7 %all-gather.53.cloned.1.call-done = bf16[2048,768]{1,0:T(8,128)(2,1)} async-done(((bf16[256,768]{1,0:T(8,128)(2,1)}), bf16[2048,768]{1,0:T(8,128)(2,1)}) %all-gather.53.cloned.1.call-update) | async-done | bytes 3145744 | tf_op jit(solution)/shard_map/all_gather | solution.py:460
  556.2 25.1 %while.105 = (s32[]{:T(128)}, f32[2048,384]{1,0:T(8,128)}, s32[256]{0:T(256)S(1)}, s32[2048]{0:T(1024)S(1)}, bf16[2048,192]{0,1:T(8,128)(2,1)}, /*index=5*/bf16[...) while((s32[]{:T(128)}, f32[2048,384]{1,0:T(8,128)}, ...), condition=%wide.region_14.15_spmd, body=%wide.region_13.14_spmd.sunk | while | flops 409600000 | bytes 24008904 | solution.py:280
  581.3 15.1 while.108
  644.4 95.1 %while.109 = (s32[]{:T(128)}, f32[2048,384]{1,0:T(8,128)}, s32[256]{0:T(256)}, s32[2048]{0:T(1024)}, bf16[2048,192]{0,1:T(8,128)(2,1)}, /*index=5*/bf16[256,3,64...) while((s32[]{:T(128)}, f32[2048,384]{1,0:T(8,128)}, ...), condition=%wide.region_36.37_spmd.clone.clone, body=%wide.region_35.36_spmd.clone.clone.sunk | while | flops 409339136 | bytes 71284336 | solution.py:280
  767.6 93.5 %while.106 = (s32[]{:T(128)}, f32[2048,384]{1,0:T(8,128)}, s32[256]{0:T(256)}, s32[2048]{0:T(1024)S(1)}, bf16[2048,192]{0,1:T(8,128)(2,1)}, /*index=5*/bf16[256,...) while((s32[]{:T(128)}, f32[2048,384]{1,0:T(8,128)}, ...), condition=%wide.region_24.25_spmd, body=%wide.region_23.24_spmd.sunk | while | flops 408813568 | bytes 71274080 | solution.py:280
  868.4 185.3 %while.110 = (s32[]{:T(128)}, f32[256,3,64]{0,2,1:T(8,128)}, f32[3,257]{0,1:T(8,128)}, bf16[2048,192]{0,1:T(8,128)(2,1)}, s32[256]{0:T(256)S(1)}, /*index=5*/s32...) while((s32[]{:T(128)}, f32[256,3,64]{0,2,1:T(8,128)}, ...), condition=%wide.region_34.35_spmd.clone.clone.clone, body=%wide.region_30.34_spmd.clone.clone.clone.sunk | while | flops 309582848 | bytes 105597736 | solution.py:129
  1073.5 157.1 %while.107 = (s32[]{:T(128)}, f32[256,3,64]{0,2,1:T(8,128)}, f32[3,257]{0,1:T(8,128)}, bf16[2048,192]{0,1:T(8,128)(2,1)}, s32[256]{0:T(256)}, /*index=5*/s32[204...) while((s32[]{:T(128)}, f32[256,3,64]{0,2,1:T(8,128)}, ...), condition=%wide.region_22.23_spmd.clone, body=%wide.region_18.22_spmd.clone.sunk | while | flops 309057280 | bytes 105558824 | solution.py:129
  1339.8 44.2 %reduce-scatter.46.cloned.1.call-done = f32[96,768]{1,0:T(8,128)} async-done(((f32[768,768]{1,0:T(8,128)}), f32[96,768]{1,0:T(8,128)}) %reduce-scatter.46.cloned.1.call-update) | async-done | bytes 294928 | tf_op jit(solution)/shard_map/reduce_scatter | solution.py:558
  1385.7 63.9 %reduce-scatter.58.cloned.1.call-done = f32[96,2048]{1,0:T(8,128)} async-done(((f32[768,2048]{1,0:T(8,128)}), f32[96,2048]{1,0:T(8,128)}) %reduce-scatter.58.cloned.1.call-update) | async-done | bytes 786448 | tf_op jit(solution)/shard_map/reduce_scatter | solution.py:567
  1451.5 63.1 %reduce-scatter.60.cloned.1.call-done = f32[96,2048]{1,0:T(8,128)} async-done(((f32[768,2048]{1,0:T(8,128)}), f32[96,2048]{1,0:T(8,128)}) %reduce-scatter.60.cloned.1.call-update) | async-done | bytes 786448 | tf_op jit(solution)/shard_map/reduce_scatter | solution.py:568
  1516.5 63.7 %reduce-scatter.62.cloned.1.call-done = f32[256,768]{1,0:T(8,128)} async-done(((f32[2048,768]{1,0:T(8,128)}), f32[256,768]{1,0:T(8,128)}) %reduce-scatter.62.cloned.1.call-update) | async-done | bytes 786448 | tf_op jit(solution)/shard_map/reduce_scatter | solution.py:569
  1582.1 43.9 %reduce-scatter.30.cloned.1.call-done = f32[96,768]{1,0:T(8,128)} async-done(((f32[768,768]{1,0:T(8,128)}), f32[96,768]{1,0:T(8,128)}) %reduce-scatter.30.cloned.1.call-update) | async-done | bytes 294928 | tf_op jit(solution)/shard_map/reduce_scatter | solution.py:546
  1627.7 44.4 %reduce-scatter.32.cloned.1.call-done = f32[96,768]{1,0:T(8,128)} async-done(((f32[768,768]{1,0:T(8,128)}), f32[96,768]{1,0:T(8,128)}) %reduce-scatter.32.cloned.1.call-update) | async-done | bytes 294928 | tf_op jit(solution)/shard_map/reduce_scatter | solution.py:547
  1673.7 63.3 %reduce-scatter.36.cloned.1.call-done = f32[96,2048]{1,0:T(8,128)} async-done(((f32[768,2048]{1,0:T(8,128)}), f32[96,2048]{1,0:T(8,128)}) %reduce-scatter.36.cloned.1.call-update) | async-done | bytes 786448 | tf_op jit(solution)/shard_map/reduce_scatter | solution.py:551
  1739.0 63.6 %reduce-scatter.38.cloned.1.call-done = f32[96,2048]{1,0:T(8,128)} async-done(((f32[768,2048]{1,0:T(8,128)}), f32[96,2048]{1,0:T(8,128)}) %reduce-scatter.38.cloned.1.call-update) | async-done | bytes 786448 | tf_op jit(solution)/shard_map/reduce_scatter | solution.py:552
  1804.5 63.1 %reduce-scatter.40.cloned.1.call-done = f32[256,768]{1,0:T(8,128)} async-done(((f32[2048,768]{1,0:T(8,128)}), f32[256,768]{1,0:T(8,128)}) %reduce-scatter.40.cloned.1.call-update) | async-done | bytes 786448 | tf_op jit(solution)/shard_map/reduce_scatter | solution.py:553
  1884.6 24.4 %all-reduce.24 = (bf16[768]{0:T(1024)(128)(2,1)S(1)}, bf16[384]{0:T(512)(128)(2,1)S(1)}, bf16[768]{0:T(1024)(128)(2,1)S(1)}, bf16[768]{0:T(1024)(128)(2,1)S(1)},...) all-reduce(f32[768]{0:T(1024)S(1)} %get-tuple-element.2526, ...), channel_id=5, replica_groups=mesh['ctx'=8,'sp'=4] {'ctx'}, use_global_device_ids=true, to_apply=%region_40.41.clone | all-reduce | flops 5376 | bytes 32256
  1909.6 12.6 all-reduce.26
  1927.1 106.5 %all-reduce.30.cloned.1.call-done = (bf16[96,768]{1,0:T(8,128)(2,1)}, bf16[96,768]{1,0:T(8,128)(2,1)}, bf16[96,768]{1,0:T(8,128)(2,1)}, bf16[96,768]{1,0:T(8,128...) async-done(((bf16[96,768]{1,0:T(8,128)(2,1)}, ...) | async-done | bytes 4128784 | tf_op jit(solution)/shard_map/psum | solution.py:601
  (1147 shorter events, 1064.9 us)
Async XLA Ops:
  10.7 157.6 %all-gather.37.cloned.1.call-start = ((), (), s32[]{:S(2)}) async-start(), calls=%async_computation.54 | async-start | bytes 1327104 | tf_op jit(solution)/shard_map/all_gather | solution.py:449
  11.3 277.0 %all-gather.25.cloned.1.call-start = ((), (), s32[]{:S(2)}) async-start(), calls=%async_computation.48 | async-start | bytes 1327104 | tf_op jit(solution)/shard_map/all_gather | solution.py:439
  12.0 282.6 %all-gather.39.cloned.1.call-start = ((), (), s32[]{:S(2)}) async-start(), calls=%async_computation.55 | async-start | bytes 1327104 | tf_op jit(solution)/shard_map/all_gather | solution.py:450
  12.8 283.7 %all-gather.41.cloned.1.call-start = ((), (), s32[]{:S(2)}) async-start(), calls=%async_computation.56 | async-start | bytes 1327104 | tf_op jit(solution)/shard_map/all_gather | solution.py:453
  13.5 295.7 %all-gather.27.cloned.1.call-start = ((), (), s32[]{:S(2)}) async-start(), calls=%async_computation.49 | async-start | bytes 3538944 | tf_op jit(solution)/shard_map/all_gather | solution.py:442
  14.1 302.2 %all-gather.29.cloned.1.call-start = ((), (), s32[]{:S(2)}) async-start(), calls=%async_computation.50 | async-start | bytes 3538944 | tf_op jit(solution)/shard_map/all_gather | solution.py:443
  14.8 335.6 %all-gather.31.cloned.1.call-start = ((), (), s32[]{:S(2)}) async-start(), calls=%async_computation.51 | async-start | bytes 3538944 | tf_op jit(solution)/shard_map/all_gather | solution.py:444
  15.4 361.0 %all-gather.43.cloned.1.call-start = ((), (), s32[]{:S(2)}) async-start(), calls=%async_computation.57 | async-start | bytes 1327104 | tf_op jit(solution)/shard_map/all_gather | solution.py:454
  16.1 386.1 %all-gather.45.cloned.1.call-start = ((), (), s32[]{:S(2)}) async-start(), calls=%async_computation.58 | async-start | bytes 1327104 | tf_op jit(solution)/shard_map/all_gather | solution.py:455
  16.7 440.2 %all-gather.47.cloned.1.call-start = ((), (), s32[]{:S(2)}) async-start(), calls=%async_computation.59 | async-start | bytes 1327104 | tf_op jit(solution)/shard_map/all_gather | solution.py:456
  17.3 446.2 %all-gather.49.cloned.1.call-start = ((), (), s32[]{:S(2)}) async-start(), calls=%async_computation.60 | async-start | bytes 3538944 | tf_op jit(solution)/shard_map/all_gather | solution.py:458
  17.9 479.7 %all-gather.51.cloned.1.call-start = ((), (), s32[]{:S(2)}) async-start(), calls=%async_computation.61 | async-start | bytes 3538944 | tf_op jit(solution)/shard_map/all_gather | solution.py:459
  18.5 513.2 %all-gather.53.cloned.1.call-start = ((), (), s32[]{:S(2)}) async-start(), calls=%async_computation.62 | async-start | bytes 3538944 | tf_op jit(solution)/shard_map/all_gather | solution.py:460
  642.5 601.3 %reduce-scatter.26.cloned.1.call-start = ((), (), s32[]{:S(2)}) async-start(), calls=%async_computation.65 | async-start | bytes 3538944 | tf_op jit(solution)/shard_map/reduce_scatter | solution.py:279
  759.3 520.2 %reduce-scatter.24.cloned.1.call-start = ((), (), s32[]{:S(2)}) async-start(), calls=%async_computation.64 | async-start | bytes 3538944 | tf_op jit(solution)/shard_map/reduce_scatter | solution.py:279
  861.2 455.3 %reduce-scatter.56.cloned.1.call-start = ((), (), s32[]{:S(2)}) async-start(), calls=%async_computation.80 | async-start | bytes 2654208 | tf_op jit(solution)/shard_map/reduce_scatter | solution.py:565
  864.1 454.0 %reduce-scatter.48.cloned.1.call-start = ((), (), s32[]{:S(2)}) async-start(), calls=%async_computation.76 | async-start | bytes 2654208 | tf_op jit(solution)/shard_map/reduce_scatter | solution.py:559
  866.2 453.6 %reduce-scatter.50.cloned.1.call-start = ((), (), s32[]{:S(2)}) async-start(), calls=%async_computation.77 | async-start | bytes 2654208 | tf_op jit(solution)/shard_map/reduce_scatter | solution.py:562
  868.3 453.2 %reduce-scatter.42.cloned.1.call-start = ((), (), s32[]{:S(2)}) async-start(), calls=%async_computation.73 | async-start | bytes 2654208 | tf_op jit(solution)/shard_map/reduce_scatter | solution.py:556
  1067.5 255.7 %reduce-scatter.34.cloned.1.call-start = ((), (), s32[]{:S(2)}) async-start(), calls=%async_computation.69 | async-start | bytes 2654208 | tf_op jit(solution)/shard_map/reduce_scatter | solution.py:548
  1069.4 255.3 %reduce-scatter.52.cloned.1.call-start = ((), (), s32[]{:S(2)}) async-start(), calls=%async_computation.78 | async-start | bytes 2654208 | tf_op jit(solution)/shard_map/reduce_scatter | solution.py:563
  1071.4 255.0 %reduce-scatter.54.cloned.1.call-start = ((), (), s32[]{:S(2)}) async-start(), calls=%async_computation.79 | async-start | bytes 2654208 | tf_op jit(solution)/shard_map/reduce_scatter | solution.py:564
  1073.5 254.6 %reduce-scatter.28.cloned.1.call-start = ((), (), s32[]{:S(2)}) async-start(), calls=%async_computation.66 | async-start | bytes 2654208 | tf_op jit(solution)/shard_map/reduce_scatter | solution.py:545
  1266.4 183.2 %reduce-scatter.58.cloned.1.call-start = ((), (), s32[]{:S(2)}) async-start(), calls=%async_computation.81 | async-start | bytes 7077888 | tf_op jit(solution)/shard_map/reduce_scatter | solution.py:567
  1270.2 244.4 %reduce-scatter.60.cloned.1.call-start = ((), (), s32[]{:S(2)}) async-start(), calls=%async_computation.82 | async-start | bytes 7077888 | tf_op jit(solution)/shard_map/reduce_scatter | solution.py:568
  1274.8 305.4 %reduce-scatter.62.cloned.1.call-start = ((), (), s32[]{:S(2)}) async-start(), calls=%async_computation.83 | async-start | bytes 7077888 | tf_op jit(solution)/shard_map/reduce_scatter | solution.py:569
  1279.5 346.6 %reduce-scatter.30.cloned.1.call-start = ((), (), s32[]{:S(2)}) async-start(), calls=%async_computation.67 | async-start | bytes 2654208 | tf_op jit(solution)/shard_map/reduce_scatter | solution.py:546
  1291.5 380.6 %reduce-scatter.32.cloned.1.call-start = ((), (), s32[]{:S(2)}) async-start(), calls=%async_computation.68 | async-start | bytes 2654208 | tf_op jit(solution)/shard_map/reduce_scatter | solution.py:547
  1303.4 433.6 %reduce-scatter.36.cloned.1.call-start = ((), (), s32[]{:S(2)}) async-start(), calls=%async_computation.70 | async-start | bytes 7077888 | tf_op jit(solution)/shard_map/reduce_scatter | solution.py:551
  1307.2 495.4 %reduce-scatter.38.cloned.1.call-start = ((), (), s32[]{:S(2)}) async-start(), calls=%async_computation.71 | async-start | bytes 7077888 | tf_op jit(solution)/shard_map/reduce_scatter | solution.py:552
  1311.8 555.8 %reduce-scatter.40.cloned.1.call-start = ((), (), s32[]{:S(2)}) async-start(), calls=%async_computation.72 | async-start | bytes 7077888 | tf_op jit(solution)/shard_map/reduce_scatter | solution.py:553
  1316.4 717.2 %all-reduce.30.cloned.1.call-start = ((), (), s32[]{:S(2)}) async-start(), calls=%async_computation.84 | async-start | bytes 8257536 | tf_op jit(solution)/shard_map/psum | solution.py:601
  (259 other events, 4932.1 us)
Sparse Core Ops, SparseCore 0:
  10.0 26.9 all-gather.18
  168.4 24.7 all-gather.24
  221.3 25.4 all-gather.40
  248.5 33.0 all-gather.26
  283.5 32.7 all-gather.28
  318.1 32.3 all-gather.30
  404.0 25.2 all-gather.46
  431.0 32.4 all-gather.48
  465.2 32.3 all-gather.50
  499.3 32.3 all-gather.52
  581.4 44.5 reduce-scatter.21
  739.7 46.6 reduce-scatter.25
  861.3 44.3 reduce-scatter.23
  909.4 42.4 reduce-scatter.55
  955.3 42.5 reduce-scatter.47
  1001.4 42.4 reduce-scatter.49
  1067.6 40.5 reduce-scatter.41
  1111.8 42.4 reduce-scatter.33
  1157.5 42.4 reduce-scatter.51
  1203.7 42.4 reduce-scatter.53
  1249.6 42.4 reduce-scatter.27
  1295.7 42.4 reduce-scatter.43
  1341.5 42.4 reduce-scatter.45
  1387.8 61.7 reduce-scatter.57
  1452.8 61.7 reduce-scatter.59
  1518.4 61.7 reduce-scatter.61
  1583.5 42.4 reduce-scatter.29
  1629.6 42.4 reduce-scatter.31
  1675.3 61.7 reduce-scatter.35
  1740.8 61.7 reduce-scatter.37
  1805.8 61.7 reduce-scatter.39
  1874.2 159.3 all-reduce.29
  (8 shorter events, 192.3 us)
where the time goes:
time: 2070 us; the launch traced here: 2060 us
  waiting for transfers between devices  831 us (40%)
  local copies, waits for them, and re-layouts  542 us (26%)
  matrix products  211 us (10%)
  blocking collectives  196 us (9%)
  other arithmetic  135 us (7%)
  starting transfers between devices  79.3 us (4%)
  loops' own time  45.9 us (2%)
    reshape x14, local copies, waits for them, and re-layouts, bias_block(): jnp.broadcast_to(band[:, None, :], (head_count, rows, band_width))  141 us
    reshape x14, local copies, waits for them, and re-layouts, bias_block(): tiled[:, rows - 1:rows - 1 + rows * (band_width - 1)]  123 us
    psum x1, waiting for transfers between devices, per_device(): lax.psum(s_wq.astype(jnp.bfloat16), 'sp').astype(jnp.float32)  106 us
    slice x10, local copies, waits for them, and re-layouts, bias_block(): tiled[:, rows - 1:rows - 1 + rows * (band_width - 1)]  81 us
    reduce_scatter x1, waiting for transfers between devices, per_device(): lax.psum_scatter(d_wg, 'ctx', scatter_dimension=0, tiled=True)  63.9 us
    reduce_scatter x1, waiting for transfers between devices, per_device(): lax.psum_scatter(d_wd, 'ctx', scatter_dimension=0, tiled=True)  63.7 us
    reduce_scatter x1, waiting for transfers between devices, per_device(): lax.psum_scatter(e_wu, 'ctx', scatter_dimension=0, tiled=True)  63.6 us
    reduce_scatter x1, waiting for transfers between devices, per_device(): lax.psum_scatter(e_wg, 'ctx', scatter_dimension=0, tiled=True)  63.3 us
  transfers between devices with their start and end apart: 57, of which 27 were waited for; matrix products, arithmetic and copies ran while one was open for 39% of the time, Pallas kernels for 0%

commit v1 on v0

--- a/solution.py
+++ b/solution.py
@@ -2,7 +2,11 @@
 
 import jax
 import jax.numpy as jnp
+import numpy as np
 from jax import lax
+from jax.experimental import pallas as pl
+from jax.experimental.pallas import tpu as pltpu
+from jax.sharding import Mesh
 from jax.sharding import PartitionSpec as P
 
 HEADS = 12
@@ -627,7 +631,469 @@
     return (enc_result, dec_result, grad_enc, grad_dec) + tuple(reduced)
 
 
-def solution(mesh):
+HG, CORE, SP = "hg", "core", "sp"
+BLOCK_PAD = 128
+
+
+def nt(left, right):
+    return lax.dot_general(left, right, (((1,), (1,)), ((), ())), preferred_element_type=jnp.float32)
+
+
+def tn(left, right):
+    return lax.dot_general(left, right, (((0,), (0,)), ((), ())), preferred_element_type=jnp.float32)
+
+
+def nn(left, right):
+    return jnp.dot(left, right, preferred_element_type=jnp.float32)
+
+
+def identity(size):
+    rows = lax.broadcasted_iota(jnp.int32, (size, size), 0)
+    cols = lax.broadcasted_iota(jnp.int32, (size, size), 1)
+    return jnp.where(rows == cols, 1.0, 0.0).astype(jnp.bfloat16)
+
+
+def only_head(array, head):
+    lanes = lax.broadcasted_iota(jnp.int32, array.shape, 1)
+    keep = (lanes >= head * HD) & (lanes < (head + 1) * HD)
+    return jnp.where(keep, array, jnp.zeros_like(array))
+
+
+def bias_mask_kernel(heads, block, causal, starts_ref, tables_ref, kdoc_ref, qdoc_ref, qpos_ref, qstart_ref, out_ref):
+    rows_total, lanes = out_ref.shape[1], out_ref.shape[2]
+    key_len = kdoc_ref.shape[0]
+    strip = block + 2 * BLOCK_PAD
+    for head in range(heads):
+        if tables_ref is not None:
+            row = tables_ref[head : head + 1, :]
+            width = row.shape[1]
+            left, right = tables_ref[head : head + 1, width - 2 : width - 1], tables_ref[head : head + 1, 0:1]
+            places = lax.broadcasted_iota(jnp.int32, (rows_total, lanes), 0)
+            fill = jnp.where(places < qstart_ref[...], left, right)
+            out_ref[head] = fill.astype(jnp.bfloat16)
+            wide = jnp.broadcast_to(row, (strip, width))
+            for number in range(lanes // block):
+                at = (number * block) % 128
+                turned = pltpu.roll(wide, (width - (strip - 1) + at) % width, 1, stride=1, stride_axis=0)
+                out_ref[head, pl.ds(pl.multiple_of(starts_ref[number], block), strip), number * block : (number + 1) * block] = turned[:, at : at + block].astype(jnp.bfloat16)
+        allowed = kdoc_ref[...] == qdoc_ref[...]
+        if causal:
+            places = lax.broadcasted_iota(jnp.int32, (key_len, lanes), 0)
+            allowed = allowed & (places <= qpos_ref[...])
+        inside = pl.ds(BLOCK_PAD, key_len)
+        if tables_ref is not None:
+            out_ref[head, inside, :] = jnp.where(allowed, out_ref[head, inside, :].astype(jnp.float32), NEGATIVE).astype(jnp.bfloat16)
+        else:
+            out_ref[head, inside, :] = jnp.where(allowed, 0.0, NEGATIVE).astype(jnp.bfloat16)
+
+
+def bias_mask(starts, tables, kdoc, qdoc, qpos, block, causal):
+    key_len, lanes = kdoc.shape[0], qdoc.shape[1]
+    heads = tables.shape[0] if tables is not None else 1
+    qstart = jnp.repeat(starts, block)[None, :]
+    operands = [starts] + ([tables] if tables is not None else []) + [kdoc, qdoc, qpos, qstart]
+
+    def body(*refs):
+        refs = list(refs)
+        if tables is None:
+            refs.insert(1, None)
+        bias_mask_kernel(heads, block, causal, *refs)
+
+    return pl.pallas_call(
+        body,
+        out_shape=jax.ShapeDtypeStruct((heads, key_len + 2 * BLOCK_PAD, lanes), jnp.bfloat16),
+        in_specs=[pl.BlockSpec(memory_space=pltpu.SMEM)] + [pl.BlockSpec(memory_space=pltpu.VMEM)] * (len(operands) - 1),
+        out_specs=pl.BlockSpec(memory_space=pltpu.VMEM),
+        compiler_params=pltpu.CompilerParams(vmem_limit_bytes=VMEM_BYTES),
+    )(*operands)
+
+
+VMEM_BYTES = 56 << 20
+ROWS = 512
+
+
+def head_scores(k_ref, masked_q, bm_ref, head, at):
+    bias_head = head if bm_ref.shape[0] > 1 else 0
+    bias = bm_ref[bias_head, pl.ds(pl.multiple_of(BLOCK_PAD + at, 128), ROWS), :].astype(jnp.float32)
+    return nt(k_ref[pl.ds(at, ROWS), :], masked_q) + bias
+
+
+def mix_kernel(q_ref, k_ref, v_ref, bm_ref, o_ref, lse_ref, s_ref, p_ref, ot_ref):
+    key_len, width = k_ref.shape
+    lanes = q_ref.shape[0]
+    vt = nt(identity(width), v_ref[...]).astype(jnp.bfloat16)
+    for head in range(width // HD):
+        masked_q = only_head(q_ref[...], head)
+
+        def first(number, top):
+            at = pl.multiple_of(number * ROWS, ROWS)
+            scores = head_scores(k_ref, masked_q, bm_ref, head, at)
+            s_ref[pl.ds(at, ROWS), :] = scores
+            return jnp.maximum(top, jnp.max(scores, axis=0, keepdims=True))
+
+        top = lax.fori_loop(0, key_len // ROWS, first, jnp.full((1, lanes), NEGATIVE, jnp.float32))
+
+        def second(number, total):
+            at = pl.multiple_of(number * ROWS, ROWS)
+            weights = jnp.exp(s_ref[pl.ds(at, ROWS), :] - top)
+            p_ref[pl.ds(at, ROWS), :] = weights.astype(jnp.bfloat16)
+            return total + jnp.sum(weights, axis=0, keepdims=True)
+
+        total = lax.fori_loop(0, key_len // ROWS, second, jnp.zeros((1, lanes), jnp.float32))
+        lse_ref[:, head * lanes : (head + 1) * lanes] = top + jnp.log(total)
+        mixed = nn(vt[head * HD : (head + 1) * HD], p_ref[...])
+        ot_ref[head * HD : (head + 1) * HD, :] = (mixed / total).astype(jnp.bfloat16)
+    o_ref[...] = nt(identity(lanes), ot_ref[...]).astype(jnp.bfloat16)
+
+
+def mix(q, k, v, bm):
+    lanes, width = q.shape
+    heads = width // HD
+    return pl.pallas_call(
+        mix_kernel,
+        out_shape=(
+            jax.ShapeDtypeStruct((lanes, width), jnp.bfloat16),
+            jax.ShapeDtypeStruct((1, heads * lanes), jnp.float32),
+        ),
+        in_specs=[pl.BlockSpec(memory_space=pltpu.VMEM)] * 4,
+        out_specs=(pl.BlockSpec(memory_space=pltpu.VMEM),) * 2,
+        scratch_shapes=[
+            pltpu.VMEM((k.shape[0], lanes), jnp.float32),
+            pltpu.VMEM((k.shape[0], lanes), jnp.bfloat16),
+            pltpu.VMEM((width, lanes), jnp.bfloat16),
+        ],
+        compiler_params=pltpu.CompilerParams(vmem_limit_bytes=VMEM_BYTES),
+    )(q, k, v, bm)
+
+
+def mix_back_kernel(block, starts_ref, q_ref, k_ref, v_ref, do_ref, lse_ref, bm_ref, qstart_ref, dq_ref, dk_ref, dv_ref, strip_ref, edge_ref, p_ref, dp_ref, ds_ref, pb_ref, ot_ref):
+    key_len, width = k_ref.shape
+    lanes = q_ref.shape[0]
+    heads = width // HD
+    biased = strip_ref is not None
+    strip = block + 2 * BLOCK_PAD
+    kt = nt(identity(width), k_ref[...]).astype(jnp.bfloat16)
+    if biased:
+        none = jnp.zeros((BLOCK_PAD, heads * lanes), jnp.bfloat16)
+        ds_ref[0:BLOCK_PAD, :] = none
+        ds_ref[BLOCK_PAD + key_len :, :] = none
+    for head in range(heads):
+        masked_q = only_head(q_ref[...], head)
+        masked_do = only_head(do_ref[...], head)
+        across = slice(head * lanes, (head + 1) * lanes)
+
+        def first(number, inner):
+            at = pl.multiple_of(number * ROWS, ROWS)
+            p = jnp.exp(head_scores(k_ref, masked_q, bm_ref, head, at) - lse_ref[:, across])
+            dp = nt(v_ref[pl.ds(at, ROWS), :], masked_do)
+            p_ref[pl.ds(at, ROWS), :] = p
+            dp_ref[pl.ds(at, ROWS), :] = dp
+            pb_ref[pl.ds(at, ROWS), across] = p.astype(jnp.bfloat16)
+            return inner + jnp.sum(p * dp, axis=0, keepdims=True)
+
+        inner = lax.fori_loop(0, key_len // ROWS, first, jnp.zeros((1, lanes), jnp.float32))
+
+        def second(number, sums):
+            at = pl.multiple_of(number * ROWS, ROWS)
+            ds = (p_ref[pl.ds(at, ROWS), :] * (dp_ref[pl.ds(at, ROWS), :] - inner)).astype(jnp.bfloat16)
+            ds_ref[pl.ds(BLOCK_PAD + at, ROWS), across] = ds
+            if not biased:
+                return sums
+            wide = ds.astype(jnp.float32)
+            places = lax.broadcasted_iota(jnp.int32, wide.shape, 0) + (at + BLOCK_PAD)
+            left = jnp.sum(jnp.where(places < qstart_ref[...], wide, 0.0), axis=0, keepdims=True)
+            right = jnp.sum(jnp.where(places >= qstart_ref[...] + strip, wide, 0.0), axis=0, keepdims=True)
+            return (sums[0] + left, sums[1] + right)
+
+        nothing = jnp.zeros((1, lanes), jnp.float32)
+        left, right = lax.fori_loop(0, key_len // ROWS, second, (nothing, nothing))
+        if biased:
+            edge_ref[2 * head : 2 * head + 1, :] = left
+            edge_ref[2 * head + 1 : 2 * head + 2, :] = right
+            total = jnp.zeros((strip, block), jnp.float32)
+            for number in range(lanes // block):
+                low = head * lanes + number * block
+                rows = pl.ds(pl.multiple_of(starts_ref[number], block), strip)
+                total = total + ds_ref[rows, low : low + block].astype(jnp.float32)
+            strip_ref[head] = total
+        back = nn(kt[head * HD : (head + 1) * HD], ds_ref[BLOCK_PAD : BLOCK_PAD + key_len, across])
+        ot_ref[head * HD : (head + 1) * HD, :] = back.astype(jnp.bfloat16)
+    dq_ref[...] = nt(identity(lanes), ot_ref[...]).astype(jnp.bfloat16)
+    stacked_q = jnp.concatenate([only_head(q_ref[...], head) for head in range(heads)], axis=0)
+    stacked_do = jnp.concatenate([only_head(do_ref[...], head) for head in range(heads)], axis=0)
+
+    @pl.loop(0, key_len // ROWS)
+    def _(number):
+        at = pl.multiple_of(number * ROWS, ROWS)
+        dk_ref[pl.ds(at, ROWS), :] = nn(ds_ref[pl.ds(BLOCK_PAD + at, ROWS), :], stacked_q).astype(dk_ref.dtype)
+        dv_ref[pl.ds(at, ROWS), :] = nn(pb_ref[pl.ds(at, ROWS), :], stacked_do).astype(dv_ref.dtype)
+
+
+def mix_back(starts, q, k, v, do, lse, bm, block, biased):
+    lanes, width = q.shape
+    key_len = k.shape[0]
+    heads = width // HD
+    qstart = jnp.repeat(starts, block)[None, :]
+    shapes = [
+        jax.ShapeDtypeStruct((lanes, width), jnp.bfloat16),
+        jax.ShapeDtypeStruct((key_len, width), jnp.bfloat16),
+        jax.ShapeDtypeStruct((key_len, width), jnp.bfloat16),
+    ]
+    if biased:
+        shapes.append(jax.ShapeDtypeStruct((heads, block + 2 * BLOCK_PAD, block), jnp.float32))
+        shapes.append(jax.ShapeDtypeStruct((2 * heads, lanes), jnp.float32))
+
+    def body(*refs):
+        refs = list(refs)
+        if not biased:
+            refs[11:11] = [None, None]
+        mix_back_kernel(block, *refs)
+
+    return pl.pallas_call(
+        body,
+        out_shape=tuple(shapes),
+        in_specs=[pl.BlockSpec(memory_space=pltpu.SMEM)] + [pl.BlockSpec(memory_space=pltpu.VMEM)] * 7,
+        out_specs=(pl.BlockSpec(memory_space=pltpu.VMEM),) * len(shapes),
+        scratch_shapes=[
+            pltpu.VMEM((key_len, lanes), jnp.float32),
+            pltpu.VMEM((key_len, lanes), jnp.float32),
+            pltpu.VMEM((key_len + 2 * BLOCK_PAD, heads * lanes), jnp.bfloat16),
+            pltpu.VMEM((key_len, heads * lanes), jnp.bfloat16),
+            pltpu.VMEM((width, lanes), jnp.bfloat16),
+        ],
+        compiler_params=pltpu.CompilerParams(vmem_limit_bytes=VMEM_BYTES),
+    )(starts, q, k, v, do, lse, bm, qstart)
+
+
+def fast_device(
+    enc_in, dec_in, enc_cot, dec_cot, enc_segments, dec_segments, buckets,
+    enc_norm1, enc_query, enc_key, enc_value, enc_proj, enc_rel, enc_norm2, enc_gate, enc_up, enc_down, enc_final,
+    dec_norm1, dec_query, dec_key, dec_value, dec_proj, dec_rel, dec_norm2, cross_query, cross_key, cross_value, cross_proj,
+    dec_norm3, dec_gate, dec_up, dec_down,
+):
+    groups, cores, parts = lax.axis_size(HG), lax.axis_size(CORE), lax.axis_size(SP)
+    my_group, my_core, my_part = lax.axis_index(HG), lax.axis_index(CORE), lax.axis_index(SP)
+    block, model = enc_in.shape
+    share = model // (groups * cores)
+    width = HEADS // groups * HD
+    heads = HEADS // groups
+    reach = (buckets.shape[1] - 1) // 2
+    bf16, f32 = jnp.bfloat16, jnp.float32
+
+    def columns(*weights):
+        cut = [w.reshape(w.shape[0], groups, w.shape[1] // groups) for w in weights]
+        packed = jnp.concatenate(cut, axis=2).transpose(1, 0, 2)
+        moved = lax.all_to_all(packed, HG, split_axis=0, concat_axis=0, tiled=True)
+        both = lax.all_gather(moved, CORE, axis=1)
+        return both.reshape(model, -1)
+
+    def both_rows(weight):
+        return lax.all_gather(weight, CORE, axis=0, tiled=True)
+
+    self_cols = columns(enc_query, enc_key, enc_value, dec_query, dec_key, dec_value)
+    enc_qkv, dec_qkv = self_cols[:, : 3 * width], self_cols[:, 3 * width :]
+    enc_gu = columns(enc_gate, enc_up)
+    cross_qkv = columns(cross_query, cross_key, cross_value)
+    cross_q, cross_kv = cross_qkv[:, :width], cross_qkv[:, width:]
+    dec_gu = columns(dec_gate, dec_up)
+    enc_wo, dec_wo, cross_wo = both_rows(enc_proj), both_rows(dec_proj), both_rows(cross_proj)
+    enc_wd, dec_wd = both_rows(enc_down), both_rows(dec_down)
+    small = jnp.concatenate([enc_norm1, enc_norm2, enc_final, dec_norm1, dec_norm2, dec_norm3, enc_rel, dec_rel])
+    small = lax.all_gather(small, (HG, CORE), axis=0)
+    gains = [small[:, i * share : (i + 1) * share].reshape(1, model).astype(f32) for i in range(6)]
+    g_e1, g_e2, g_ef, g_d1, g_d2, g_d3 = gains
+    rel_len = enc_rel.shape[0]
+    rels = [small[:, 6 * share + i * rel_len : 6 * share + (i + 1) * rel_len].reshape(-1, HEADS).astype(f32) for i in range(2)]
+
+    def table_of(relative, row):
+        onehot = (row[:, None] == jnp.arange(relative.shape[0], dtype=jnp.int32)[None, :]).astype(f32)
+        full = jnp.dot(onehot, relative, precision=HIGHEST).T
+        here = lax.dynamic_slice_in_dim(full, my_group * heads, heads, 0)
+        return here, onehot
+
+    def turned(table):
+        edge = block - 1
+        long = jnp.concatenate(
+            [jnp.broadcast_to(table[:, :1], (heads, edge)), table, jnp.broadcast_to(table[:, -1:], (heads, edge))], axis=1
+        )
+        flipped = long[:, ::-1]
+        pad = -flipped.shape[1] % 128
+        return jnp.pad(flipped, ((0, 0), (0, pad)))
+
+    enc_table, enc_onehot = table_of(rels[0], buckets[0])
+    dec_table, dec_onehot = table_of(rels[1], buckets[1])
+    firsts = ((cores * jnp.arange(groups, dtype=jnp.int32) + my_core) * parts + my_part) * block
+    qpos = (firsts[:, None] + jnp.arange(block, dtype=jnp.int32)[None, :]).reshape(1, -1)
+
+    def mine(ids):
+        return lax.dynamic_index_in_dim(
+            lax.dynamic_index_in_dim(ids.reshape(groups, cores, parts, block), my_core, 1, False), my_part, 1, False
+        ).reshape(1, -1)
+
+    enc_q_ids, dec_q_ids = mine(enc_segments), mine(dec_segments)
+    enc_k_ids, dec_k_ids = enc_segments[:, None], dec_segments[:, None]
+    enc_bm = bias_mask(firsts, turned(enc_table), enc_k_ids, enc_q_ids, qpos, block, False)
+    dec_bm = bias_mask(firsts, turned(dec_table), dec_k_ids, dec_q_ids, qpos, block, True)
+    cross_bm = bias_mask(firsts, None, enc_k_ids, dec_q_ids, qpos, block, False)
+
+    def spread(own):
+        return lax.all_gather(own, HG, axis=0, tiled=True)
+
+    def collect(partial):
+        return lax.psum_scatter(partial.astype(bf16), HG, scatter_dimension=0, tiled=True).astype(f32)
+
+    def all_keys(kv):
+        every = lax.all_gather(kv, (CORE, SP), axis=0)
+        every = every.reshape(cores, parts, groups, block, -1).transpose(2, 0, 1, 3, 4)
+        return every.reshape(cores * parts * groups * block, -1)
+
+    def own_keys(dkv):
+        cut = dkv.reshape(groups, cores, parts, block, -1).transpose(1, 2, 0, 3, 4)
+        return lax.psum_scatter(cut.reshape(cores * parts * groups * block, -1), (CORE, SP), scatter_dimension=0, tiled=True)
+
+    def attend(n_query, w_query, kv, bm):
+        q = nn(n_query, w_query).astype(bf16)
+        every = all_keys(kv)
+        k, v = every[:, :width], every[:, width:]
+        o, lse = mix(q, k, v, bm)
+        return o, (q, k, v, o, lse)
+
+    def attend_back(dyb, kept, bm, w_proj, biased):
+        q, k, v, o, lse = kept
+        do = nt(dyb, w_proj).astype(bf16)
+        d_proj = tn(o, dyb)
+        got = mix_back(firsts, q, k, v, do, lse, bm, block, biased)
+        dq, dk, dv = got[:3]
+        dkv = own_keys(jnp.concatenate([dk, dv], axis=1)).astype(bf16)
+        return d_proj, dq, dkv, got[3:]
+
+    def normed(x, g):
+        return rms_norm(x, g).astype(bf16)
+
+    def norm_back(x, g, dn):
+        r = lax.rsqrt(jnp.mean(x * x, axis=-1, keepdims=True) + EPSILON)
+        w = dn * g
+        dx = r * w - x * (r * r * r) * jnp.mean(w * x, axis=-1, keepdims=True)
+        return dx, jnp.sum(dn * x * r, axis=0)
+
+    enc_x, dec_x = enc_in.astype(f32), dec_in.astype(f32)
+    en1, dn1 = spread(normed(enc_x, g_e1)), spread(normed(dec_x, g_d1))
+    enc_o, enc_kept = attend(en1, enc_qkv[:, :width], nn(en1, enc_qkv[:, width:]).astype(bf16), enc_bm)
+    dec_o, dec_kept = attend(dn1, dec_qkv[:, :width], nn(dn1, dec_qkv[:, width:]).astype(bf16), dec_bm)
+    ex = enc_x + collect(nn(enc_o, enc_wo))
+    dx = dec_x + collect(nn(dec_o, dec_wo))
+    hidden = enc_wd.shape[0]
+
+    def feed(n, w_gu, w_d):
+        gu = nn(n, w_gu)
+        g, u = gu[:, :hidden], gu[:, hidden:]
+        h = gated(g, u).astype(bf16)
+        return g, u, h, collect(nn(h, w_d))
+
+    def feed_back(n, g, u, h, dyb, w_gu, w_d):
+        dh = nt(dyb, w_d)
+        d_down = tn(h, dyb)
+        _, pullback = jax.vjp(gated, g, u)
+        dg, du = pullback(dh)
+        dgu = jnp.concatenate([dg, du], axis=1).astype(bf16)
+        return tn(n, dgu), d_down, collect(nt(dgu, w_gu))
+
+    en2 = spread(normed(ex, g_e2))
+    e_g, e_u, e_h, y = feed(en2, enc_gu, enc_wd)
+    enc_out = ex + y
+    memory = spread(normed(enc_out, g_ef))
+    dn2 = spread(normed(dx, g_d2))
+    cross_o, cross_kept = attend(dn2, cross_q, nn(memory, cross_kv).astype(bf16), cross_bm)
+    cx = dx + collect(nn(cross_o, cross_wo))
+    dn3 = spread(normed(cx, g_d3))
+    d_g, d_u, d_h, y = feed(dn3, dec_gu, dec_wd)
+    dec_out = cx + y
+
+    d_cot, e_cot = dec_cot.astype(f32), enc_cot.astype(f32)
+    dyb = spread(dec_cot)
+    dw_dgu, dw_ddown, dn = feed_back(dn3, d_g, d_u, d_h, dyb, dec_gu, dec_wd)
+    back, dg_d3 = norm_back(cx, g_d3, dn)
+    grad_dec = d_cot + back
+    dyb = spread(grad_dec.astype(bf16))
+    dw_cproj, dq, dkv, _ = attend_back(dyb, cross_kept, cross_bm, cross_wo, False)
+    dw_cq = tn(dn2, dq)
+    dw_ckv = tn(memory, dkv)
+    dn, dmem = collect(nt(dq, cross_q)), collect(nt(dkv, cross_kv))
+    back, dg_d2 = norm_back(dx, g_d2, dn)
+    grad_dec = grad_dec + back
+    dyb = spread(grad_dec.astype(bf16))
+    dw_dproj, dq, dkv, dec_tab = attend_back(dyb, dec_kept, dec_bm, dec_wo, True)
+    dqkv = jnp.concatenate([dq, dkv], axis=1)
+    dw_dqkv = tn(dn1, dqkv)
+    back, dg_d1 = norm_back(dec_x, g_d1, collect(nt(dqkv, dec_qkv)))
+    dec_in_grad = grad_dec + back
+    back, dg_ef = norm_back(enc_out, g_ef, dmem)
+    grad_enc = e_cot + back
+    dyb = spread(grad_enc.astype(bf16))
+    dw_egu, dw_edown, dn = feed_back(en2, e_g, e_u, e_h, dyb, enc_gu, enc_wd)
+    back, dg_e2 = norm_back(ex, g_e2, dn)
+    grad_enc = grad_enc + back
+    dyb = spread(grad_enc.astype(bf16))
+    dw_eproj, dq, dkv, enc_tab = attend_back(dyb, enc_kept, enc_bm, enc_wo, True)
+    dqkv = jnp.concatenate([dq, dkv], axis=1)
+    dw_eqkv = tn(en1, dqkv)
+    back, dg_e1 = norm_back(enc_x, g_e1, collect(nt(dqkv, enc_qkv)))
+    enc_in_grad = grad_enc + back
+
+    def rows_back(grad, pieces):
+        n = grad.shape[1]
+        cut = grad.reshape(groups, cores, share, n).transpose(1, 0, 2, 3).reshape(cores * groups * share, n)
+        half = lax.psum_scatter(cut.astype(bf16), CORE, scatter_dimension=0, tiled=True).reshape(groups, share, n)
+        moved = lax.all_to_all(half, HG, split_axis=0, concat_axis=0, tiled=True)
+        whole = lax.psum(moved, SP).astype(f32)
+        each = n // pieces
+        return [whole[:, :, i * each : (i + 1) * each].transpose(1, 0, 2).reshape(share, groups * each) for i in range(pieces)]
+
+    def rows_kept(grad):
+        half = lax.psum_scatter(grad.astype(bf16), CORE, scatter_dimension=0, tiled=True)
+        return lax.psum(half, SP).astype(f32)
+
+    e_wq, e_wk, e_wv = rows_back(dw_eqkv, 3)
+    e_wg, e_wu = rows_back(dw_egu, 2)
+    d_wq, d_wk, d_wv = rows_back(dw_dqkv, 3)
+    c_wq, c_wk, c_wv = rows_back(jnp.concatenate([dw_cq, dw_ckv], axis=1), 3)
+    d_wg, d_wu = rows_back(dw_dgu, 2)
+    e_wo, d_wo, c_wo = rows_kept(dw_eproj), rows_kept(dw_dproj), rows_kept(dw_cproj)
+    e_wd, d_wd = rows_kept(dw_edown), rows_kept(dw_ddown)
+
+    def fold(tab, onehot):
+        strips, edges = tab
+        keys = strips.shape[1]
+        flipped = strips[:, :, ::-1].transpose(0, 2, 1)
+        span = keys + block
+        wide = jnp.pad(flipped, ((0, 0), (0, 0), (0, block)))
+        flat = wide.reshape(heads, block * span)[:, : block * (span - 1)]
+        by_distance = jnp.sum(flat.reshape(heads, block, span - 1), axis=1)
+        shift = block - 1 + BLOCK_PAD - reach
+        size = 2 * reach + 1
+        inner = by_distance[:, shift : shift + size]
+        low = jnp.sum(by_distance[:, :shift], axis=1)
+        high = jnp.sum(by_distance[:, shift + size :], axis=1)
+        sides = jnp.sum(edges, axis=1).reshape(heads, 2)
+        inner = inner.at[:, 0].add(low + sides[:, 0]).at[:, -1].add(high + sides[:, 1])
+        full = jnp.zeros((HEADS, size), f32)
+        full = lax.dynamic_update_slice_in_dim(full, inner, my_group * heads, 0)
+        return jnp.dot(onehot.T, full.T, precision=HIGHEST).reshape(-1)
+
+    small_grads = [dg_e1, dg_e2, dg_ef, dg_d1, dg_d2, dg_d3, fold(enc_tab, enc_onehot), fold(dec_tab, dec_onehot)]
+    packed = jnp.concatenate([v.reshape(groups * cores, -1) for v in small_grads], axis=1)
+    summed = lax.psum(packed, (HG, CORE, SP))
+    own = lax.dynamic_index_in_dim(summed, my_group * cores + my_core, 0, False)
+    s = [own[i * share : (i + 1) * share] for i in range(6)]
+    e_rel, d_rel = own[6 * share : 6 * share + rel_len], own[6 * share + rel_len :]
+    return (
+        enc_out, dec_out, enc_in_grad, dec_in_grad,
+        s[0], e_wq, e_wk, e_wv, e_wo, e_rel, s[1], e_wg, e_wu, e_wd, s[2],
+        s[3], d_wq, d_wk, d_wv, d_wo, d_rel, s[4], c_wq, c_wk, c_wv, c_wo, s[5], d_wg, d_wu, d_wd,
+    )
+
+
+def general_plan(mesh):
     placed = (
         P(("ctx", "sp"), None),
         P(("ctx", "sp"), None),
@@ -701,3 +1167,25 @@
         ),
         check_vma=False,
     )
+
+
+def split_plan(mesh, groups):
+    cut = Mesh(np.asarray(mesh.devices).reshape(groups, 2, mesh.shape["sp"]), (HG, CORE, SP))
+    tokens, rows, gain, same = P((HG, CORE, SP), None), P((HG, CORE), None), P((HG, CORE)), P()
+    attention = (gain, rows, rows, rows, rows, gain)
+    feed = (gain, rows, rows, rows)
+    weights = attention + feed + (gain,) + attention + (gain, rows, rows, rows, rows) + feed
+    return jax.shard_map(
+        fast_device,
+        mesh=cut,
+        in_specs=(tokens,) * 4 + (same,) * 3 + weights,
+        out_specs=(tokens,) * 4 + weights,
+        check_vma=False,
+    )
+
+
+def solution(mesh):
+    groups, odd = divmod(mesh.shape["ctx"], 2)
+    if odd or HEADS % groups:
+        return general_plan(mesh)
+    return split_plan(mesh, groups)

time: 2070 us -> 977 us (0.47)
  local copies, waits for them, and re-layouts: 542 us -> 89.7 us
  waiting for transfers between devices: 831 us -> 431 us
  matrix products: 211 us -> 43.2 us
  other arithmetic: 135 us -> 44.5 us
  Pallas kernels: 0 us -> 83.9 us
  starting transfers between devices: 79.3 us -> 23.1 us
  loops' own time: 45.9 us -> 0 us
  blocking collectives: 196 us -> 234 us
    reduce_scatter x21 -> x24, waiting for transfers between devices: 533 us -> 277 us  [the longest x11 148 us: collect(): lax.psum_scatter(partial.astype(bf16), HG, scatter_dimension=0, tiled=True)]
    reshape x38 -> x51, local copies, waits for them, and re-layouts: 267 us -> 32.8 us  [the longest x13 12.5 us: rows_back(): whole[:, :, i * each:(i + 1) * each].transpose(1, 0, 2)]
    dot_general x98 -> x39, matrix products: 211 us -> 43.2 us  [the longest x13 17.8 us: nn(): return jnp.dot(left, right, preferred_element_type=jnp.float32)]
    all_gather x18 -> x6, waiting for transfers between devices: 143 us -> 10.8 us  [the longest x3 10.7 us: all_keys(): every = lax.all_gather(kv, (CORE, SP), axis=0)]
    slice x32 -> x10, local copies, waits for them, and re-layouts: 97.6 us -> 7.05 us  [the longest x3 5.39 us: attend(): k, v = (every[:, :width], every[:, width:])]
    pallas_call x0 -> x9, Pallas kernels: none -> 83.9 us  [the longest x3 41.4 us: mix_back(): pl.pallas_call(body, out_shape=tuple(shapes), in_specs=[pl.BlockSpec(memo...]
    all_to_all x17 -> x6, starting transfers between devices: 77.6 us -> 21 us  [the longest x3 10.6 us: columns(): moved = lax.all_to_all(packed, HG, split_axis=0, concat_axis=0, tiled=True)]
    all_gather x6 -> x17, blocking collectives: 71.3 us -> 123 us  [the longest x11 108 us: spread(): return lax.all_gather(own, HG, axis=0, tiled=True)]
  transfers between devices with their start and end apart: 57 -> 37, of which waited for: 27 -> 23; matrix products, arithmetic and copies ran while one was open for 39% -> 12% of each run, Pallas kernels for 0% -> 7%
where the time goes in v1:
time: 977 us; the launch traced here: 967 us
  waiting for transfers between devices  431 us (44%)
  blocking collectives  234 us (24%)
  local copies, waits for them, and re-layouts  89.7 us (9%)
  Pallas kernels  83.9 us (9%)
  other arithmetic  44.5 us (5%)
  matrix products  43.2 us (4%)
  starting transfers between devices  23.1 us (2%)
  between operations  17.5 us (2%)
    reduce_scatter x11, waiting for transfers between devices, collect(): lax.psum_scatter(partial.astype(bf16), HG, scatter_dimension=0, tiled=True)  148 us
    psum x1, waiting for transfers between devices, rows_back(): whole = lax.psum(moved, SP).astype(f32)  119 us
    all_gather x11, blocking collectives, spread(): return lax.all_gather(own, HG, axis=0, tiled=True)  108 us
    reduce_scatter x3, waiting for transfers between devices, own_keys(): lax.psum_scatter(cut.reshape(cores * parts * groups * block, -1), (CORE,...  74.7 us
    reduce_scatter x5, waiting for transfers between devices, rows_kept(): lax.psum_scatter(grad.astype(bf16), CORE, scatter_dimension=0, tiled=True)  52.3 us
    psum x1, blocking collectives, fast_device(): summed = lax.psum(packed, (HG, CORE, SP))  43.2 us
    pallas_call x3, Pallas kernels, mix_back(): pl.pallas_call(body, out_shape=tuple(shapes), in_specs=[pl.BlockSpec(memo...  41.4 us
    pallas_call x3, Pallas kernels, mix(): pl.pallas_call(mix_kernel, out_shape=(jax.ShapeDtypeStruct((lanes, width)...  28.2 us
  transfers between devices with their start and end apart: 37, of which 23 were waited for; matrix products, arithmetic and copies ran while one was open for 12% of the time, Pallas kernels for 7%

profile of v1, /device:TPU:0, one launch (start us, length us, event | category | flops | bytes accessed | tf_op | source)
XLA Modules:
  0.0 967.2 jit_solution(7753530329620194461)
XLA Ops:
  14.8 17.4 %all_to_all.45 = bf16[4,96,1152]{2,1,0:T(8,128)(2,1)S(1)} all-to-all(bf16[4,96,1152]{2,1,0:T(8,128)(2,1)S(1)} %copy.216), channel_id=1, replica_groups=mesh['hg'=4,'core'=2,'sp'=4] {'hg'}, dimensions={0} | all-to-all | bytes 1769472 | tf_op jit(solution)/shard_map/all_to_all | solution.py:886
  35.4 22.3 %all-reduce.4 = bf16[5376]{0:T(1024)(128)(2,1)S(1)} all-reduce(bf16[5376]{0:T(1024)(128)(2,1)S(1)} %dynamic-update-slice.12), channel_id=2, replica_groups=mesh['hg'=4,'core'=2,'sp'=4] {'hg','core'}, use_global_device_ids=true, to_apply=%add.4 | all-reduce | flops 5376 | bytes 21504
  104.1 9.9 %shard_map.545 = (bf16[256,192]{1,0:T(8,128)(2,1)}, f32[1,768]{1,0:T(1,128)}) custom-call(bf16[256,192]{1,0:T(8,128)(2,1)} %convolution_convert_fusion.27.q_ref.refs_1_, bf16[2048,192]{1,0:T(8,128)(2,1)} %get-tuple-element.167.k_ref.refs_2_, bf16[2048,192]{1,0:T(8,128)(2,1)} %get-tuple-element.166.v_ref.refs_3_, bf16[3,2304,256]{2,1,0:T(8,128)(2,1)} %shard_map.544.bm_ref.refs_6_), custom_call_target="tpu_custom_call" | custom-call | tf_op jit(solution)/shard_map/pallas_call | solution.py:752
  116.9 10.1 %all_gather.108 = bf16[256,768]{1,0:T(8,128)(2,1)S(1)} all-gather(bf16[64,768]{1,0:T(8,128)(2,1)S(1)} %fusion.67), channel_id=1, replica_groups=mesh['hg'=4,'core'=2,'sp'=4] {'hg'}, dimensions={0}, use_global_device_ids=true | all-gather | bytes 491520 | tf_op jit(solution)/shard_map/all_gather | solution.py:940
  154.6 9.9 %all_gather.104 = bf16[256,768]{1,0:T(8,128)(2,1)S(1)} all-gather(bf16[64,768]{1,0:T(8,128)(2,1)S(1)} %multiply_convert_fusion.7), channel_id=1, replica_groups=mesh['hg'=4,'core'=2,'sp'=4] {'hg'}, dimensions={0}, use_global_device_ids=true | all-gather | bytes 491520 | tf_op jit(solution)/shard_map/all_gather | solution.py:940
  185.7 10.4 %reduce-scatter.27.cloned.1.call-done = bf16[64,768]{1,0:T(8,128)(2,1)} async-done(((bf16[256,768]{1,0:T(8,128)(2,1)}), bf16[64,768]{1,0:T(8,128)(2,1)}) %reduce-scatter.27.cloned.1.call-update) | async-done | bytes 98320 | tf_op jit(solution)/shard_map/reduce_scatter | solution.py:943
  197.9 9.7 %all_gather.115 = bf16[256,768]{1,0:T(8,128)(2,1)S(1)} all-gather(bf16[64,768]{1,0:T(8,128)(2,1)S(1)} %multiply_convert_fusion.5), channel_id=1, replica_groups=mesh['hg'=4,'core'=2,'sp'=4] {'hg'}, dimensions={0}, use_global_device_ids=true | all-gather | bytes 491520 | tf_op jit(solution)/shard_map/all_gather | solution.py:940
  230.0 9.9 %all_gather.112 = bf16[256,768]{1,0:T(8,128)(2,1)S(1)} all-gather(bf16[64,768]{1,0:T(8,128)(2,1)S(1)} %multiply_convert_fusion.6), channel_id=1, replica_groups=mesh['hg'=4,'core'=2,'sp'=4] {'hg'}, dimensions={0}, use_global_device_ids=true | all-gather | bytes 491520 | tf_op jit(solution)/shard_map/all_gather | solution.py:940
  241.6 10.7 %all-gather.23.cloned.1.call-done = bf16[2048,384]{1,0:T(8,128)(2,1)} async-done(((bf16[256,384]{1,0:T(8,128)(2,1)}), bf16[2048,384]{1,0:T(8,128)(2,1)}) %all-gather.23.cloned.1.call-update) | async-done | bytes 1572880 | tf_op jit(solution)/shard_map/all_gather | solution.py:946
  266.6 10.4 %all_gather.123 = bf16[256,768]{1,0:T(8,128)(2,1)} all-gather(bf16[64,768]{1,0:T(8,128)(2,1)S(1)} %copy-done.49), channel_id=1, replica_groups=mesh['hg'=4,'core'=2,'sp'=4] {'hg'}, dimensions={0}, use_global_device_ids=true | all-gather | bytes 491520 | tf_op jit(solution)/shard_map/all_gather | solution.py:940
  281.5 11.2 %reduce-scatter.31.cloned.1.call-done = bf16[64,768]{1,0:T(8,128)(2,1)} async-done(((bf16[256,768]{1,0:T(8,128)(2,1)}), bf16[64,768]{1,0:T(8,128)(2,1)}) %reduce-scatter.31.cloned.1.call-update) | async-done | bytes 98320 | tf_op jit(solution)/shard_map/reduce_scatter | solution.py:943
  295.3 9.7 %all_gather.119 = bf16[256,768]{1,0:T(8,128)(2,1)S(1)} all-gather(bf16[64,768]{1,0:T(8,128)(2,1)S(1)} %multiply_convert_fusion.4), channel_id=1, replica_groups=mesh['hg'=4,'core'=2,'sp'=4] {'hg'}, dimensions={0}, use_global_device_ids=true | all-gather | bytes 491520 | tf_op jit(solution)/shard_map/all_gather | solution.py:940
  310.2 24.3 %reduce-scatter.35.cloned.1.call-done = bf16[64,768]{1,0:T(8,128)(2,1)} async-done(((bf16[256,768]{1,0:T(8,128)(2,1)}), bf16[64,768]{1,0:T(8,128)(2,1)}) %reduce-scatter.35.cloned.1.call-update) | async-done | bytes 98320 | tf_op jit(solution)/shard_map/reduce_scatter | solution.py:943
  347.9 12.1 %shard_map.550 = (bf16[256,192]{1,0:T(8,128)(2,1)}, bf16[2048,192]{1,0:T(8,128)(2,1)}, bf16[2048,192]{1,0:T(8,128)(2,1)}) custom-call(s32[4]{0:T(128)} %copy-done.101, bf16[256,192]{1,0:T(8,128)(2,1)} %convolution_convert_fusion.25.q_ref.refs_1_, bf16[2048,192]{1,0:T(8,128)(2,1)} %get-tuple-element.163.k_ref.refs_2_, ...), custom_call_target="tpu_custom_call" | custom-call | tf_op jit(solution)/shard_map/pallas_call | solution.py:852
  365.8 37.4 %reduce-scatter.37.cloned.1.call-done = bf16[256,384]{1,0:T(8,128)(2,1)} async-done(((bf16[2048,384]{1,0:T(8,128)(2,1)}), bf16[256,384]{1,0:T(8,128)(2,1)}) %reduce-scatter.37.cloned.1.call-update) | async-done | bytes 196624 | tf_op jit(solution)/shard_map/reduce_scatter | solution.py:952
  407.9 22.5 %reduce-scatter.47.cloned.1.call-done = bf16[64,768]{1,0:T(8,128)(2,1)} async-done(((bf16[256,768]{1,0:T(8,128)(2,1)}), bf16[64,768]{1,0:T(8,128)(2,1)}) %reduce-scatter.47.cloned.1.call-update) | async-done | bytes 98320 | tf_op jit(solution)/shard_map/reduce_scatter | solution.py:943
  432.0 26.1 %reduce-scatter.39.cloned.1.call-done = bf16[64,768]{1,0:T(8,128)(2,1)} async-done(((bf16[256,768]{1,0:T(8,128)(2,1)}), bf16[64,768]{1,0:T(8,128)(2,1)}) %reduce-scatter.39.cloned.1.call-update) | async-done | bytes 98320 | tf_op jit(solution)/shard_map/reduce_scatter | solution.py:943
  460.7 10.7 %all_gather.125 = bf16[256,768]{1,0:T(8,128)(2,1)S(1)} all-gather(bf16[64,768]{1,0:T(8,128)(2,1)S(1)} %fusion.98), channel_id=1, replica_groups=mesh['hg'=4,'core'=2,'sp'=4] {'hg'}, dimensions={0}, use_global_device_ids=true | all-gather | bytes 491520 | tf_op jit(solution)/shard_map/all_gather | solution.py:940
  475.6 10.1 %reduce-scatter.33.cloned.1.call-done = bf16[64,768]{1,0:T(8,128)(2,1)} async-done(((bf16[256,768]{1,0:T(8,128)(2,1)}), bf16[64,768]{1,0:T(8,128)(2,1)}) %reduce-scatter.33.cloned.1.call-update) | async-done | bytes 98320 | tf_op jit(solution)/shard_map/reduce_scatter | solution.py:943
  498.2 14.7 %shard_map.552 = (bf16[256,192]{1,0:T(8,128)(2,1)}, bf16[2048,192]{1,0:T(8,128)(2,1)}, bf16[2048,192]{1,0:T(8,128)(2,1)}, f32[3,320,64]{2,1,0:T(8,128)}, f32[6,256]{1,0:T(8,128)}) custom-call(s32[4]{0:T(128)} %copy-done.101, bf16[256,192]{1,0:T(8,128)(2,1)} %convolution_convert_fusion.26.q_ref.refs_1_, bf16[2048,192]{1,0:T(8,128)(2,1)} %get-tuple-element.165.k_ref.refs_2_, ...), custom_call_target="tpu_custom_call" | custom-call | tf_op jit(solution)/shard_map/pallas_call | solution.py:852
  529.4 14.6 %shard_map.551 = (bf16[256,192]{1,0:T(8,128)(2,1)}, bf16[2048,192]{1,0:T(8,128)(2,1)}, bf16[2048,192]{1,0:T(8,128)(2,1)}, f32[3,320,64]{2,1,0:T(8,128)}, f32[6,256]{1,0:T(8,128)}) custom-call(s32[4]{0:T(128)} %copy-done.101, bf16[256,192]{1,0:T(8,128)(2,1)} %convolution_convert_fusion.27.q_ref.refs_1_, bf16[2048,192]{1,0:T(8,128)(2,1)} %get-tuple-element.167.k_ref.refs_2_, ...), custom_call_target="tpu_custom_call" | custom-call | tf_op jit(solution)/shard_map/pallas_call | solution.py:852
  561.9 35.3 %reduce-scatter.43.cloned.1.call-done = bf16[256,384]{1,0:T(8,128)(2,1)} async-done(((bf16[2048,384]{1,0:T(8,128)(2,1)}), bf16[256,384]{1,0:T(8,128)(2,1)}) %reduce-scatter.43.cloned.1.call-update) | async-done | bytes 196624 | tf_op jit(solution)/shard_map/reduce_scatter | solution.py:952
  607.9 16.3 %all_to_all.46 = bf16[4,96,1024]{2,1,0:T(8,128)(2,1)} all-to-all(bf16[4,96,1024]{2,1,0:T(8,128)(2,1)} %bitcast.226), channel_id=1, replica_groups=mesh['hg'=4,'core'=2,'sp'=4] {'hg'}, dimensions={0} | all-to-all | bytes 1572864 | tf_op jit(solution)/shard_map/all_to_all | solution.py:1047
  634.8 11.2 %all_to_all.47 = bf16[4,96,576]{2,1,0:T(8,128)(2,1)} all-to-all(bf16[4,96,576]{2,1,0:T(8,128)(2,1)} %bitcast.234), channel_id=1, replica_groups=mesh['hg'=4,'core'=2,'sp'=4] {'hg'}, dimensions={0} | all-to-all | bytes 884736 | tf_op jit(solution)/shard_map/all_to_all | solution.py:1047
  668.0 12.4 %reduce-scatter.71.cloned.1.call-done = bf16[256,768]{1,0:T(8,128)(2,1)} async-done(((bf16[512,768]{1,0:T(8,128)(2,1)}), bf16[256,768]{1,0:T(8,128)(2,1)}) %reduce-scatter.71.cloned.1.call-update) | async-done | bytes 393232 | tf_op jit(solution)/shard_map/reduce_scatter | solution.py:1053
  680.3 11.6 %reduce-scatter.63.cloned.1.call-done = bf16[96,768]{1,0:T(8,128)(2,1)} async-done(((bf16[192,768]{1,0:T(8,128)(2,1)}), bf16[96,768]{1,0:T(8,128)(2,1)}) %reduce-scatter.63.cloned.1.call-update) | async-done | bytes 147472 | tf_op jit(solution)/shard_map/reduce_scatter | solution.py:1053
  691.9 11.5 %reduce-scatter.55.cloned.1.call-done = bf16[96,768]{1,0:T(8,128)(2,1)} async-done(((bf16[192,768]{1,0:T(8,128)(2,1)}), bf16[96,768]{1,0:T(8,128)(2,1)}) %reduce-scatter.55.cloned.1.call-update) | async-done | bytes 147472 | tf_op jit(solution)/shard_map/reduce_scatter | solution.py:1053
  703.4 12.3 %reduce-scatter.59.cloned.1.call-done = bf16[256,768]{1,0:T(8,128)(2,1)} async-done(((bf16[512,768]{1,0:T(8,128)(2,1)}), bf16[256,768]{1,0:T(8,128)(2,1)}) %reduce-scatter.59.cloned.1.call-update) | async-done | bytes 393232 | tf_op jit(solution)/shard_map/reduce_scatter | solution.py:1053
  721.7 22.6 %reduce-scatter.51.cloned.1.call-done = bf16[64,768]{1,0:T(8,128)(2,1)} async-done(((bf16[256,768]{1,0:T(8,128)(2,1)}), bf16[64,768]{1,0:T(8,128)(2,1)}) %reduce-scatter.51.cloned.1.call-update) | async-done | bytes 98320 | tf_op jit(solution)/shard_map/reduce_scatter | solution.py:943
  750.6 21.1 %reduce-scatter.45.cloned.1.call-done = bf16[64,768]{1,0:T(8,128)(2,1)} async-done(((bf16[256,768]{1,0:T(8,128)(2,1)}), bf16[64,768]{1,0:T(8,128)(2,1)}) %reduce-scatter.45.cloned.1.call-update) | async-done | bytes 98320 | tf_op jit(solution)/shard_map/reduce_scatter | solution.py:943
  772.9 43.2 %psum.77 = f32[8,672]{1,0:T(8,128)S(1)} all-reduce(f32[8,672]{1,0:T(8,128)S(1)} %concatenate.73), channel_id=1, replica_groups=mesh['hg'=4,'core'=2,'sp'=4] {'hg','core','sp'}, use_global_device_ids=true, to_apply=%region_41.42 | all-reduce | flops 5376 | bytes 43008 | tf_op jit(solution)/shard_map/psum | solution.py:1085
  819.0 119.5 %all-reduce.8.cloned.1.call-done = (bf16[4,96,576]{2,1,0:T(8,128)(2,1)}, bf16[96,768]{1,0:T(8,128)(2,1)}, bf16[4,96,1024]{2,1,0:T(8,128)(2,1)}, bf16[256,768]{1,...) async-done(((bf16[4,96,576]{2,1,0:T(8,128)(2,1)}, ...) | async-done | bytes 4128784 | tf_op jit(solution)/shard_map/psum | solution.py:1048
  (649 shorter events, 318.4 us)
Async XLA Ops:
  7.2 61.6 %all-gather.15.cloned.1.call-start = ((), (), s32[]{:S(2)}) async-start(), calls=%async_computation.57 | async-start | bytes 2654208 | tf_op jit(solution)/shard_map/all_gather | solution.py:887
  33.7 67.1 %all-gather.17.cloned.1.call-start = ((), (), s32[]{:S(2)}) async-start(), calls=%async_computation.58 | async-start | bytes 1769472 | tf_op jit(solution)/shard_map/all_gather | solution.py:946
  77.6 72.1 %all-gather.19.cloned.1.call-start = ((), (), s32[]{:S(2)}) async-start(), calls=%async_computation.59 | async-start | bytes 2359296 | tf_op jit(solution)/shard_map/all_gather | solution.py:887
  87.1 64.9 %reduce-scatter.25.cloned.1.call-start = ((), (), s32[]{:S(2)}) async-start(), calls=%async_computation.33 | async-start | bytes 491520 | tf_op jit(solution)/shard_map/reduce_scatter | solution.py:943
  116.0 54.8 %all-gather.21.cloned.1.call-start = ((), (), s32[]{:S(2)}) async-start(), calls=%async_computation.60 | async-start | bytes 1769472 | tf_op jit(solution)/shard_map/all_gather | solution.py:946
  133.3 62.8 %reduce-scatter.27.cloned.1.call-start = ((), (), s32[]{:S(2)}) async-start(), calls=%async_computation.34 | async-start | bytes 491520 | tf_op jit(solution)/shard_map/reduce_scatter | solution.py:943
  168.2 59.3 %reduce-scatter.29.cloned.1.call-start = ((), (), s32[]{:S(2)}) async-start(), calls=%async_computation.35 | async-start | bytes 491520 | tf_op jit(solution)/shard_map/reduce_scatter | solution.py:943
  185.6 66.7 %all-gather.23.cloned.1.call-start = ((), (), s32[]{:S(2)}) async-start(), calls=%async_computation.61 | async-start | bytes 1769472 | tf_op jit(solution)/shard_map/all_gather | solution.py:946
  216.3 63.2 %all-gather.25.cloned.1.call-start = ((), (), s32[]{:S(2)}) async-start(), calls=%async_computation.62 | async-start | bytes 2359296 | tf_op jit(solution)/shard_map/all_gather | solution.py:887
  227.4 65.3 %reduce-scatter.31.cloned.1.call-start = ((), (), s32[]{:S(2)}) async-start(), calls=%async_computation.36 | async-start | bytes 491520 | tf_op jit(solution)/shard_map/reduce_scatter | solution.py:943
  266.5 68.0 %reduce-scatter.35.cloned.1.call-start = ((), (), s32[]{:S(2)}) async-start(), calls=%async_computation.38 | async-start | bytes 491520 | tf_op jit(solution)/shard_map/reduce_scatter | solution.py:943
  309.9 93.3 %reduce-scatter.37.cloned.1.call-start = ((), (), s32[]{:S(2)}) async-start(), calls=%async_computation.39 | async-start | bytes 1769472 | tf_op jit(solution)/shard_map/reduce_scatter | solution.py:952
  363.5 66.9 %reduce-scatter.47.cloned.1.call-start = ((), (), s32[]{:S(2)}) async-start(), calls=%async_computation.44 | async-start | bytes 491520 | tf_op jit(solution)/shard_map/reduce_scatter | solution.py:943
  365.8 92.3 %reduce-scatter.39.cloned.1.call-start = ((), (), s32[]{:S(2)}) async-start(), calls=%async_computation.40 | async-start | bytes 491520 | tf_op jit(solution)/shard_map/reduce_scatter | solution.py:943
  405.4 80.3 %reduce-scatter.33.cloned.1.call-start = ((), (), s32[]{:S(2)}) async-start(), calls=%async_computation.37 | async-start | bytes 491520 | tf_op jit(solution)/shard_map/reduce_scatter | solution.py:943
  407.8 108.8 %reduce-scatter.41.cloned.1.call-start = ((), (), s32[]{:S(2)}) async-start(), calls=%async_computation.41 | async-start | bytes 491520 | tf_op jit(solution)/shard_map/reduce_scatter | solution.py:943
  475.6 80.6 %reduce-scatter.49.cloned.1.call-start = ((), (), s32[]{:S(2)}) async-start(), calls=%async_computation.45 | async-start | bytes 1769472 | tf_op jit(solution)/shard_map/reduce_scatter | solution.py:952
  516.5 80.7 %reduce-scatter.43.cloned.1.call-start = ((), (), s32[]{:S(2)}) async-start(), calls=%async_computation.42 | async-start | bytes 1769472 | tf_op jit(solution)/shard_map/reduce_scatter | solution.py:952
  547.6 60.3 %reduce-scatter.69.cloned.1.call-start = ((), (), s32[]{:S(2)}) async-start(), calls=%async_computation.55 | async-start | bytes 2359296 | tf_op jit(solution)/shard_map/reduce_scatter | solution.py:1046
  550.7 73.6 %reduce-scatter.65.cloned.1.call-start = ((), (), s32[]{:S(2)}) async-start(), calls=%async_computation.53 | async-start | bytes 1474560 | tf_op jit(solution)/shard_map/reduce_scatter | solution.py:1046
  554.1 80.7 %reduce-scatter.61.cloned.1.call-start = ((), (), s32[]{:S(2)}) async-start(), calls=%async_computation.51 | async-start | bytes 1474560 | tf_op jit(solution)/shard_map/reduce_scatter | solution.py:1046
  559.5 86.5 %reduce-scatter.57.cloned.1.call-start = ((), (), s32[]{:S(2)}) async-start(), calls=%async_computation.49 | async-start | bytes 2359296 | tf_op jit(solution)/shard_map/reduce_scatter | solution.py:1046
  561.9 97.7 %reduce-scatter.53.cloned.1.call-start = ((), (), s32[]{:S(2)}) async-start(), calls=%async_computation.47 | async-start | bytes 1474560 | tf_op jit(solution)/shard_map/reduce_scatter | solution.py:1046
  600.5 67.4 %reduce-scatter.67.cloned.1.call-start = ((), (), s32[]{:S(2)}) async-start(), calls=%async_computation.54 | async-start | bytes 442368 | tf_op jit(solution)/shard_map/reduce_scatter | solution.py:1053
  601.6 78.7 %reduce-scatter.71.cloned.1.call-start = ((), (), s32[]{:S(2)}) async-start(), calls=%async_computation.56 | async-start | bytes 1179648 | tf_op jit(solution)/shard_map/reduce_scatter | solution.py:1053
  603.0 88.9 %reduce-scatter.63.cloned.1.call-start = ((), (), s32[]{:S(2)}) async-start(), calls=%async_computation.52 | async-start | bytes 442368 | tf_op jit(solution)/shard_map/reduce_scatter | solution.py:1053
  604.1 99.3 %reduce-scatter.55.cloned.1.call-start = ((), (), s32[]{:S(2)}) async-start(), calls=%async_computation.48 | async-start | bytes 442368 | tf_op jit(solution)/shard_map/reduce_scatter | solution.py:1053
  605.1 110.5 %reduce-scatter.59.cloned.1.call-start = ((), (), s32[]{:S(2)}) async-start(), calls=%async_computation.50 | async-start | bytes 1179648 | tf_op jit(solution)/shard_map/reduce_scatter | solution.py:1053
  627.7 116.6 %reduce-scatter.51.cloned.1.call-start = ((), (), s32[]{:S(2)}) async-start(), calls=%async_computation.46 | async-start | bytes 491520 | tf_op jit(solution)/shard_map/reduce_scatter | solution.py:943
  649.5 122.1 %reduce-scatter.45.cloned.1.call-start = ((), (), s32[]{:S(2)}) async-start(), calls=%async_computation.43 | async-start | bytes 491520 | tf_op jit(solution)/shard_map/reduce_scatter | solution.py:943
  659.5 56.1 %all-to-all-start.4 = ((bf16[4,96,576]{2,1,0:T(8,128)(2,1)}), bf16[4,96,576]{2,1,0:T(8,128)(2,1)S(1)}, u32[]{:S(2)}, u32[]{:S(2)}) async-start(bf16[4,96,576]{2,1,0:T(8,128)(2,1)} %bitcast.232), calls=%async_computation.19 | async-start | bytes 983040 | tf_op jit(solution)/shard_map/all_to_all | solution.py:1047
  663.0 275.4 %all-reduce.8.cloned.1.call-start = ((), (), s32[]{:S(2)}) async-start(), calls=%async_computation.63 | async-start | bytes 8552448 | tf_op jit(solution)/shard_map/psum | solution.py:1048
  (150 other events, 1794.4 us)
Sparse Core Ops, SparseCore 0:
  33.8 9.7 all-gather.14
  72.0 25.4 all-gather.16
  99.5 9.2 all-gather.18
  116.1 25.5 reduce-scatter.24
  143.8 25.0 all-gather.20
  172.1 23.9 reduce-scatter.26
  199.5 26.4 reduce-scatter.28
  228.2 24.1 all-gather.22
  254.5 9.3 all-gather.24
  267.1 25.5 reduce-scatter.30
  310.1 24.4 reduce-scatter.34
  363.6 39.5 reduce-scatter.36
  406.6 23.7 reduce-scatter.46
  433.6 24.3 reduce-scatter.38
  461.3 24.4 reduce-scatter.32
  489.0 24.4 reduce-scatter.40
  516.6 39.4 reduce-scatter.48
  558.3 38.8 reduce-scatter.42
  599.5 8.4 reduce-scatter.68
  610.1 9.6 reduce-scatter.64
  622.1 9.6 reduce-scatter.60
  634.1 10.1 reduce-scatter.56
  646.6 9.6 reduce-scatter.52
  659.1 8.8 reduce-scatter.66
  670.9 9.3 reduce-scatter.70
  683.0 8.8 reduce-scatter.62
  694.5 8.8 reduce-scatter.54
  706.2 9.4 reduce-scatter.58
  718.7 25.5 reduce-scatter.50
  747.2 24.4 reduce-scatter.44
  776.3 162.0 all-reduce.7

commit v2 on v1

--- a/solution.py
+++ b/solution.py
@@ -1,3 +1,4 @@
+import functools
 import math
 
 import jax
@@ -865,6 +866,204 @@
     )(starts, q, k, v, do, lse, bm, qstart)
 
 
+def send(src, dst, send_sem, recv_sem, to):
+    copy = pltpu.make_async_remote_copy(
+        src_ref=src, dst_ref=dst, send_sem=send_sem, recv_sem=recv_sem, device_id=to, device_id_type=pl.DeviceIdType.MESH
+    )
+    copy.start()
+    return copy
+
+
+def arrived(dst, send_sem, recv_sem, to):
+    pltpu.make_async_remote_copy(
+        src_ref=dst, dst_ref=dst, send_sem=send_sem, recv_sem=recv_sem, device_id=to, device_id_type=pl.DeviceIdType.MESH
+    ).wait_recv()
+
+
+class Place:
+    def __init__(self, groups, cores, parts):
+        self.groups, self.cores, self.parts = groups, cores, parts
+        self.group, self.core, self.part = lax.axis_index(HG), lax.axis_index(CORE), lax.axis_index(SP)
+
+    def ahead(self, step):
+        return lax.rem(self.group + step, self.groups)
+
+    def behind(self, step):
+        return lax.rem(self.group + self.groups - step, self.groups)
+
+    def chip(self, group):
+        return (group, self.core, self.part)
+
+    def sibling(self):
+        return (self.group, 1 - self.core, self.part)
+
+    def plane(self, step):
+        return lax.rem(self.part + step, self.parts)
+
+    def plane_behind(self, step):
+        return lax.rem(self.part + self.parts - step, self.parts)
+
+    def at_plane(self, part):
+        return (self.group, self.core, part)
+
+    def greet(self, chips=True, sibling=True, planes=False):
+        barrier = pltpu.get_barrier_semaphore()
+        partners = []
+        if chips:
+            partners += [self.chip(self.ahead(step)) for step in range(1, self.groups)]
+        if sibling:
+            partners.append(self.sibling())
+        if planes:
+            partners += [self.at_plane(self.plane(step)) for step in range(1, self.parts)]
+        for partner in partners:
+            pl.semaphore_signal(barrier, inc=1, device_id=partner, device_id_type=pl.DeviceIdType.MESH)
+        pl.semaphore_wait(barrier, len(partners))
+
+
+def recut_kernel(sizes, counts, *refs):
+    cols, rows = counts
+    col_refs, refs = refs[:cols], refs[cols:]
+    row_refs, refs = refs[:rows], refs[rows:]
+    col_outs, refs = refs[:cols], refs[cols:]
+    row_outs, refs = refs[:rows], refs[rows:]
+    sent, got, relay_sent, relay_got, pair_sent, pair_got, local = refs
+    place = Place(*sizes)
+    group, core = place.group, place.core
+    place.greet()
+    pending, copies = [], []
+    for index in range(cols):
+        out = col_outs[index]
+        for step in range(1, place.groups):
+            to = place.ahead(step)
+            pending.append(send(col_refs[index].at[to], out.at[group, core], sent.at[index, step], got.at[index, step], place.chip(to)))
+        pending.append(
+            send(col_refs[index].at[group], out.at[group, core], relay_sent.at[index, 0], relay_got.at[index, 0], place.sibling())
+        )
+        copies.append(pltpu.make_async_copy(col_refs[index].at[group], out.at[group, core], local.at[index]))
+        copies[-1].start()
+    for index in range(rows):
+        out = row_outs[index]
+        pending.append(send(row_refs[index], out.at[core], pair_sent.at[index], pair_got.at[index], place.sibling()))
+        copies.append(pltpu.make_async_copy(row_refs[index], out.at[core], local.at[cols + index]))
+        copies[-1].start()
+    for index in range(cols):
+        out = col_outs[index]
+        for step in range(1, place.groups):
+            source = place.behind(step)
+            slot = out.at[source, core]
+            arrived(slot, sent.at[index, step], got.at[index, step], place.chip(source))
+            pending.append(send(slot, slot, relay_sent.at[index, step], relay_got.at[index, step], place.sibling()))
+    for index in range(cols):
+        out = col_outs[index]
+        for step in range(place.groups):
+            slot = out.at[place.behind(step), 1 - core]
+            arrived(slot, relay_sent.at[index, step], relay_got.at[index, step], place.sibling())
+    for index in range(rows):
+        arrived(row_outs[index].at[1 - core], pair_sent.at[index], pair_got.at[index], place.sibling())
+    for copy in copies:
+        copy.wait()
+    for copy in pending:
+        copy.wait_send()
+
+
+def recut(sizes, collective_id, col_packs, row_packs):
+    groups, cores, _ = sizes
+    cols, rows = len(col_packs), len(row_packs)
+    anywhere = pl.BlockSpec(memory_space=pl.ANY)
+    shapes = [jax.ShapeDtypeStruct((groups, cores) + w.shape[1:], w.dtype) for w in col_packs]
+    shapes += [jax.ShapeDtypeStruct((cores,) + w.shape, w.dtype) for w in row_packs]
+    dma = pltpu.SemaphoreType.DMA
+    got = pl.pallas_call(
+        functools.partial(recut_kernel, sizes, (cols, rows)),
+        out_shape=tuple(shapes),
+        in_specs=[anywhere] * (cols + rows),
+        out_specs=(anywhere,) * (cols + rows),
+        scratch_shapes=[
+            dma((cols, groups)), dma((cols, groups)), dma((cols, groups)), dma((cols, groups)),
+            dma((rows,)), dma((rows,)), dma((cols + rows,)),
+        ],
+        compiler_params=pltpu.CompilerParams(collective_id=collective_id, has_side_effects=True, vmem_limit_bytes=VMEM_BYTES),
+    )(*col_packs, *row_packs)
+    whole_cols = [w.reshape(groups * cores * w.shape[2], w.shape[3]) for w in got[:cols]]
+    return whole_cols, [w.reshape(cores * w.shape[1], w.shape[2]) for w in got[cols:]]
+
+
+def give_rows_kernel(sizes, counts, *refs):
+    cols, rows = counts
+    col_refs, refs = refs[:cols], refs[cols:]
+    row_refs, refs = refs[:rows], refs[rows:]
+    col_outs, refs = refs[:cols], refs[cols:]
+    row_outs, refs = refs[:rows], refs[rows:]
+    col_sibs, refs = refs[:cols], refs[cols:]
+    col_sums, refs = refs[:cols], refs[cols:]
+    row_sibs, refs = refs[:rows], refs[rows:]
+    sent, got, pair_sent, pair_got, row_sent, row_got = refs
+    place = Place(*sizes)
+    group, core = place.group, place.core
+    place.greet()
+    pending = []
+    for index in range(cols):
+        for step in range(place.groups):
+            to = place.ahead(step)
+            pending.append(
+                send(
+                    col_refs[index].at[to, 1 - core], col_sibs[index].at[to],
+                    pair_sent.at[index, step], pair_got.at[index, step], place.sibling(),
+                )
+            )
+    for index in range(rows):
+        pending.append(
+            send(row_refs[index].at[1 - core], row_sibs[index], row_sent.at[index], row_got.at[index], place.sibling())
+        )
+    for index in range(cols):
+        for step in list(range(1, place.groups)) + [0]:
+            to = place.ahead(step)
+            arrived(col_sibs[index].at[to], pair_sent.at[index, step], pair_got.at[index, step], place.sibling())
+            both = col_refs[index][to, core].astype(jnp.float32) + col_sibs[index][to].astype(jnp.float32)
+            if step:
+                col_sums[index][to] = both.astype(jnp.bfloat16)
+                pending.append(
+                    send(
+                        col_sums[index].at[to], col_outs[index].at[group],
+                        sent.at[index, step], got.at[index, step], place.chip(to),
+                    )
+                )
+            else:
+                col_outs[index][group] = both.astype(jnp.bfloat16)
+    for index in range(rows):
+        arrived(row_sibs[index], row_sent.at[index], row_got.at[index], place.sibling())
+        both = row_refs[index][core].astype(jnp.float32) + row_sibs[index][...].astype(jnp.float32)
+        row_outs[index][...] = both.astype(jnp.bfloat16)
+    for index in range(cols):
+        for step in range(1, place.groups):
+            source = place.behind(step)
+            arrived(col_outs[index].at[source], sent.at[index, step], got.at[index, step], place.chip(source))
+    for copy in pending:
+        copy.wait_send()
+
+
+def give_rows(sizes, collective_id, col_grads, row_grads):
+    groups, cores, _ = sizes
+    cols, rows = len(col_grads), len(row_grads)
+    vmem = pl.BlockSpec(memory_space=pltpu.VMEM)
+    col_in = [w.reshape(groups, cores, w.shape[0] // (groups * cores), w.shape[1]) for w in col_grads]
+    row_in = [w.reshape(cores, w.shape[0] // cores, w.shape[1]) for w in row_grads]
+    col_own = [(groups,) + w.shape[2:] for w in col_in]
+    row_own = [w.shape[1:] for w in row_in]
+    dma = pltpu.SemaphoreType.DMA
+    got = pl.pallas_call(
+        functools.partial(give_rows_kernel, sizes, (cols, rows)),
+        out_shape=tuple(jax.ShapeDtypeStruct(s, jnp.bfloat16) for s in col_own + row_own),
+        in_specs=[vmem] * (cols + rows),
+        out_specs=(vmem,) * (cols + rows),
+        scratch_shapes=[pltpu.VMEM(s, jnp.bfloat16) for s in col_own + col_own + row_own]
+        + [dma((cols, groups))] * 4
+        + [dma((rows,))] * 2,
+        compiler_params=pltpu.CompilerParams(collective_id=collective_id, has_side_effects=True, vmem_limit_bytes=VMEM_BYTES),
+    )(*col_in, *row_in)
+    return got[:cols], got[cols:]
+
+
 def fast_device(
     enc_in, dec_in, enc_cot, dec_cot, enc_segments, dec_segments, buckets,
     enc_norm1, enc_query, enc_key, enc_value, enc_proj, enc_rel, enc_norm2, enc_gate, enc_up, enc_down, enc_final,
@@ -880,24 +1079,27 @@
     reach = (buckets.shape[1] - 1) // 2
     bf16, f32 = jnp.bfloat16, jnp.float32
 
-    def columns(*weights):
+    sizes = (groups, cores, parts)
+
+    def packed(*weights):
         cut = [w.reshape(w.shape[0], groups, w.shape[1] // groups) for w in weights]
-        packed = jnp.concatenate(cut, axis=2).transpose(1, 0, 2)
-        moved = lax.all_to_all(packed, HG, split_axis=0, concat_axis=0, tiled=True)
-        both = lax.all_gather(moved, CORE, axis=1)
-        return both.reshape(model, -1)
-
-    def both_rows(weight):
-        return lax.all_gather(weight, CORE, axis=0, tiled=True)
-
-    self_cols = columns(enc_query, enc_key, enc_value, dec_query, dec_key, dec_value)
-    enc_qkv, dec_qkv = self_cols[:, : 3 * width], self_cols[:, 3 * width :]
-    enc_gu = columns(enc_gate, enc_up)
-    cross_qkv = columns(cross_query, cross_key, cross_value)
+        return jnp.concatenate(cut, axis=2).transpose(1, 0, 2)
+
+    cols, rows = recut(
+        sizes,
+        1,
+        [
+            packed(enc_query, enc_key, enc_value),
+            packed(dec_query, dec_key, dec_value),
+            packed(enc_gate, enc_up),
+            packed(cross_query, cross_key, cross_value),
+            packed(dec_gate, dec_up),
+        ],
+        [enc_proj, dec_proj, cross_proj, enc_down, dec_down],
+    )
+    enc_qkv, dec_qkv, enc_gu, cross_qkv, dec_gu = cols
+    enc_wo, dec_wo, cross_wo, enc_wd, dec_wd = rows
     cross_q, cross_kv = cross_qkv[:, :width], cross_qkv[:, width:]
-    dec_gu = columns(dec_gate, dec_up)
-    enc_wo, dec_wo, cross_wo = both_rows(enc_proj), both_rows(dec_proj), both_rows(cross_proj)
-    enc_wd, dec_wd = both_rows(enc_down), both_rows(dec_down)
     small = jnp.concatenate([enc_norm1, enc_norm2, enc_final, dec_norm1, dec_norm2, dec_norm3, enc_rel, dec_rel])
     small = lax.all_gather(small, (HG, CORE), axis=0)
     gains = [small[:, i * share : (i + 1) * share].reshape(1, model).astype(f32) for i in range(6)]
@@ -1040,26 +1242,26 @@
     back, dg_e1 = norm_back(enc_x, g_e1, collect(nt(dqkv, enc_qkv)))
     enc_in_grad = grad_enc + back
 
-    def rows_back(grad, pieces):
-        n = grad.shape[1]
-        cut = grad.reshape(groups, cores, share, n).transpose(1, 0, 2, 3).reshape(cores * groups * share, n)
-        half = lax.psum_scatter(cut.astype(bf16), CORE, scatter_dimension=0, tiled=True).reshape(groups, share, n)
-        moved = lax.all_to_all(half, HG, split_axis=0, concat_axis=0, tiled=True)
-        whole = lax.psum(moved, SP).astype(f32)
-        each = n // pieces
+    def summed_rows(collective_id, col_grads, row_grads):
+        mine_cols, mine_rows = give_rows(
+            sizes, collective_id, [g.astype(bf16) for g in col_grads], [g.astype(bf16) for g in row_grads]
+        )
+        return [lax.psum(g, SP) for g in mine_cols], [lax.psum(g, SP).astype(f32) for g in mine_rows]
+
+    def unpacked(whole, pieces):
+        each = whole.shape[2] // pieces
+        whole = whole.astype(f32)
         return [whole[:, :, i * each : (i + 1) * each].transpose(1, 0, 2).reshape(share, groups * each) for i in range(pieces)]
 
-    def rows_kept(grad):
-        half = lax.psum_scatter(grad.astype(bf16), CORE, scatter_dimension=0, tiled=True)
-        return lax.psum(half, SP).astype(f32)
-
-    e_wq, e_wk, e_wv = rows_back(dw_eqkv, 3)
-    e_wg, e_wu = rows_back(dw_egu, 2)
-    d_wq, d_wk, d_wv = rows_back(dw_dqkv, 3)
-    c_wq, c_wk, c_wv = rows_back(jnp.concatenate([dw_cq, dw_ckv], axis=1), 3)
-    d_wg, d_wu = rows_back(dw_dgu, 2)
-    e_wo, d_wo, c_wo = rows_kept(dw_eproj), rows_kept(dw_dproj), rows_kept(dw_cproj)
-    e_wd, d_wd = rows_kept(dw_edown), rows_kept(dw_ddown)
+    (dgu_rows,), (d_wd,) = summed_rows(2, [dw_dgu], [dw_ddown])
+    (cross_rows,), (c_wo,) = summed_rows(3, [jnp.concatenate([dw_cq, dw_ckv], axis=1)], [dw_cproj])
+    (egu_rows, dqkv_rows), (d_wo, e_wd) = summed_rows(4, [dw_egu, dw_dqkv], [dw_dproj, dw_edown])
+    (eqkv_rows,), (e_wo,) = summed_rows(5, [dw_eqkv], [dw_eproj])
+    e_wq, e_wk, e_wv = unpacked(eqkv_rows, 3)
+    e_wg, e_wu = unpacked(egu_rows, 2)
+    d_wq, d_wk, d_wv = unpacked(dqkv_rows, 3)
+    c_wq, c_wk, c_wv = unpacked(cross_rows, 3)
+    d_wg, d_wu = unpacked(dgu_rows, 2)
 
     def fold(tab, onehot):
         strips, edges = tab

time: 977 us -> 908 us (0.929)
  Pallas kernels: 83.9 us -> 215 us
  waiting for transfers between devices: 431 us -> 321 us
  blocking collectives: 234 us -> 176 us
  local copies, waits for them, and re-layouts: 89.7 us -> 64.6 us
  starting transfers between devices: 23.1 us -> 0.96 us
  matrix products: 43.2 us -> 54.1 us
    pallas_call x0 -> x5, Pallas kernels: none -> 131 us  [the longest x4 67.7 us: give_rows(): pl.pallas_call(functools.partial(give_rows_kernel, sizes, (cols, rows)),...]
    reduce_scatter x10 -> x0, waiting for transfers between devices: 53.7 us -> none  [the longest x5 52.3 us: rows_kept(): lax.psum_scatter(grad.astype(bf16), CORE, scatter_dimension=0, tiled=True)]
    all_to_all x3 -> x0, blocking collectives: 45 us -> none  [the longest x2 27.6 us: rows_back(): moved = lax.all_to_all(half, HG, split_axis=0, concat_axis=0, tiled=True)]
    reduce_scatter x3, waiting for transfers between devices: 74.7 us -> 45.1 us  [own_keys(): lax.psum_scatter(cut.reshape(cores * parts * groups * block, -1), (CORE,...]
    all_to_all x6 -> x0, waiting for transfers between devices: 23.9 us -> none  [the longest x3 13.2 us: rows_back(): moved = lax.all_to_all(half, HG, split_axis=0, concat_axis=0, tiled=True)]
    all_to_all x6 -> x0, starting transfers between devices: 21 us -> none  [the longest x3 10.6 us: columns(): moved = lax.all_to_all(packed, HG, split_axis=0, concat_axis=0, tiled=True)]
    all_gather x3, waiting for transfers between devices: 10.7 us -> 28.5 us  [all_keys(): every = lax.all_gather(kv, (CORE, SP), axis=0)]
    reduce_scatter x11, waiting for transfers between devices: 148 us -> 132 us  [collect(): lax.psum_scatter(partial.astype(bf16), HG, scatter_dimension=0, tiled=True)]
  transfers between devices with their start and end apart: 37 -> 18, of which waited for: 23 -> 14; matrix products, arithmetic and copies ran while one was open for 12% -> 11% of each run, Pallas kernels for 7% -> 13%
where the time goes in v2:
time: 908 us; the launch traced here: 897 us
  waiting for transfers between devices  321 us (35%)
  Pallas kernels  215 us (24%)
  blocking collectives  176 us (19%)
  local copies, waits for them, and re-layouts  64.6 us (7%)
  matrix products  54.1 us (6%)
  other arithmetic  48.3 us (5%)
  between operations  16.8 us (2%)
    reduce_scatter x11, waiting for transfers between devices, collect(): lax.psum_scatter(partial.astype(bf16), HG, scatter_dimension=0, tiled=True)  132 us
    psum x1, waiting for transfers between devices, summed_rows(): lax.psum(g, SP)  115 us
    all_gather x11, blocking collectives, spread(): return lax.all_gather(own, HG, axis=0, tiled=True)  106 us
    pallas_call x4, Pallas kernels, give_rows(): pl.pallas_call(functools.partial(give_rows_kernel, sizes, (cols, rows)),...  67.7 us
    pallas_call x1, Pallas kernels, recut(): pl.pallas_call(functools.partial(recut_kernel, sizes, (cols, rows)), out_...  63.8 us
    reduce_scatter x3, waiting for transfers between devices, own_keys(): lax.psum_scatter(cut.reshape(cores * parts * groups * block, -1), (CORE,...  45.1 us
    psum x1, blocking collectives, fast_device(): summed = lax.psum(packed, (HG, CORE, SP))  44.3 us
    pallas_call x3, Pallas kernels, mix_back(): pl.pallas_call(body, out_shape=tuple(shapes), in_specs=[pl.BlockSpec(memo...  41.4 us
  transfers between devices with their start and end apart: 18, of which 14 were waited for; matrix products, arithmetic and copies ran while one was open for 11% of the time, Pallas kernels for 13%

profile of v2, /device:TPU:0, one launch (start us, length us, event | category | flops | bytes accessed | tf_op | source)
XLA Modules:
  0.0 897.2 jit_solution(12378830769873146674)
XLA Ops:
  15.0 25.5 %all-reduce.4 = bf16[5376]{0:T(1024)(128)(2,1)S(1)} all-reduce(bf16[5376]{0:T(1024)(128)(2,1)S(1)} %dynamic-update-slice.12), channel_id=2, replica_groups=mesh['hg'=4,'core'=2,'sp'=4] {'hg','core'}, use_global_device_ids=true, to_apply=%add.4 | all-reduce | flops 5376 | bytes 21504
  60.2 63.8 %shard_map.544 = (bf16[4,2,96,576]{3,2,1,0:T(8,128)(2,1)}, bf16[4,2,96,576]{3,2,1,0:T(8,128)(2,1)}, bf16[4,2,96,1024]{3,2,1,0:T(8,128)(2,1)}, bf16[4,2,96,576]{3...) custom-call(bf16[4,96,576]{2,1,0:T(8,128)(2,1)} %get-tuple-element.2, ...), custom_call_target="tpu_custom_call" | custom-call | tf_op jit(solution)/shard_map/pallas_call | solution.py:976
  139.1 12.7 %all-gather.8.cloned.1.call-done = bf16[2048,384]{1,0:T(8,128)(2,1)} async-done(((bf16[256,384]{1,0:T(8,128)(2,1)}), bf16[2048,384]{1,0:T(8,128)(2,1)}) %all-gather.8.cloned.1.call-update) | async-done | bytes 1572880 | tf_op jit(solution)/shard_map/all_gather | solution.py:1148
  167.6 10.3 %all_gather.63 = bf16[256,768]{1,0:T(8,128)(2,1)S(1)} all-gather(bf16[64,768]{1,0:T(8,128)(2,1)S(1)} %fusion.65), channel_id=1, replica_groups=mesh['hg'=4,'core'=2,'sp'=4] {'hg'}, dimensions={0}, use_global_device_ids=true | all-gather | bytes 491520 | tf_op jit(solution)/shard_map/all_gather | solution.py:1142
  180.1 10.7 %reduce-scatter.15.cloned.1.call-done = bf16[64,768]{1,0:T(8,128)(2,1)} async-done(((bf16[256,768]{1,0:T(8,128)(2,1)}), bf16[64,768]{1,0:T(8,128)(2,1)}) %reduce-scatter.15.cloned.1.call-update) | async-done | bytes 98320 | tf_op jit(solution)/shard_map/reduce_scatter | solution.py:1145
  193.4 9.7 %all_gather.62 = bf16[256,768]{1,0:T(8,128)(2,1)S(1)} all-gather(bf16[64,768]{1,0:T(8,128)(2,1)S(1)} %multiply_convert_fusion.7), channel_id=1, replica_groups=mesh['hg'=4,'core'=2,'sp'=4] {'hg'}, dimensions={0}, use_global_device_ids=true | all-gather | bytes 491520 | tf_op jit(solution)/shard_map/all_gather | solution.py:1142
  221.4 9.5 %shard_map.548 = (bf16[256,192]{1,0:T(8,128)(2,1)}, f32[1,768]{1,0:T(1,128)}) custom-call(bf16[256,192]{1,0:T(8,128)(2,1)} %convolution_convert_fusion.26.q_ref.refs_1_, bf16[2048,192]{1,0:T(8,128)(2,1)} %get-tuple-element.205.k_ref.refs_2_, bf16[2048,192]{1,0:T(8,128)(2,1)} %get-tuple-element.204.v_ref.refs_3_, bf16[3,2304,256]{2,1,0:T(8,128)(2,1)} %shard_map.547.bm_ref.refs_6_), custom_call_target="tpu_custom_call" | custom-call | tf_op jit(solution)/shard_map/pallas_call | solution.py:753
  232.9 12.1 %reduce-scatter.17.cloned.1.call-done = bf16[64,768]{1,0:T(8,128)(2,1)} async-done(((bf16[256,768]{1,0:T(8,128)(2,1)}), bf16[64,768]{1,0:T(8,128)(2,1)}) %reduce-scatter.17.cloned.1.call-update) | async-done | bytes 98320 | tf_op jit(solution)/shard_map/reduce_scatter | solution.py:1145
  246.2 9.7 %all_gather.67 = bf16[256,768]{1,0:T(8,128)(2,1)S(1)} all-gather(bf16[64,768]{1,0:T(8,128)(2,1)S(1)} %multiply_convert_fusion.5), channel_id=1, replica_groups=mesh['hg'=4,'core'=2,'sp'=4] {'hg'}, dimensions={0}, use_global_device_ids=true | all-gather | bytes 491520 | tf_op jit(solution)/shard_map/all_gather | solution.py:1142
  261.2 11.5 %reduce-scatter.19.cloned.1.call-done = bf16[64,768]{1,0:T(8,128)(2,1)} async-done(((bf16[256,768]{1,0:T(8,128)(2,1)}), bf16[64,768]{1,0:T(8,128)(2,1)}) %reduce-scatter.19.cloned.1.call-update) | async-done | bytes 98320 | tf_op jit(solution)/shard_map/reduce_scatter | solution.py:1145
  275.2 10.1 %all_gather.66 = bf16[256,768]{1,0:T(8,128)(2,1)S(1)} all-gather(bf16[64,768]{1,0:T(8,128)(2,1)S(1)} %multiply_convert_fusion.6), channel_id=1, replica_groups=mesh['hg'=4,'core'=2,'sp'=4] {'hg'}, dimensions={0}, use_global_device_ids=true | all-gather | bytes 491520 | tf_op jit(solution)/shard_map/all_gather | solution.py:1142
  287.4 12.4 %all-gather.12.cloned.1.call-done = bf16[2048,384]{1,0:T(8,128)(2,1)} async-done(((bf16[256,384]{1,0:T(8,128)(2,1)}), bf16[2048,384]{1,0:T(8,128)(2,1)}) %all-gather.12.cloned.1.call-update) | async-done | bytes 1572880 | tf_op jit(solution)/shard_map/all_gather | solution.py:1148
  314.0 10.2 %all_gather.71 = bf16[256,768]{1,0:T(8,128)(2,1)S(1)} all-gather(bf16[64,768]{1,0:T(8,128)(2,1)S(1)} %copy-done.28), channel_id=1, replica_groups=mesh['hg'=4,'core'=2,'sp'=4] {'hg'}, dimensions={0}, use_global_device_ids=true | all-gather | bytes 491520 | tf_op jit(solution)/shard_map/all_gather | solution.py:1142
  324.2 13.8 %reduce-scatter.21.cloned.1.call-done = bf16[64,768]{1,0:T(8,128)(2,1)} async-done(((bf16[256,768]{1,0:T(8,128)(2,1)}), bf16[64,768]{1,0:T(8,128)(2,1)}) %reduce-scatter.21.cloned.1.call-update) | async-done | bytes 98320 | tf_op jit(solution)/shard_map/reduce_scatter | solution.py:1145
  340.1 9.6 %all_gather.70 = bf16[256,768]{1,0:T(8,128)(2,1)S(1)} all-gather(bf16[64,768]{1,0:T(8,128)(2,1)S(1)} %multiply_convert_fusion.4), channel_id=1, replica_groups=mesh['hg'=4,'core'=2,'sp'=4] {'hg'}, dimensions={0}, use_global_device_ids=true | all-gather | bytes 491520 | tf_op jit(solution)/shard_map/all_gather | solution.py:1142
  355.5 24.5 %reduce-scatter.25.cloned.1.call-done = bf16[64,768]{1,0:T(8,128)(2,1)} async-done(((bf16[256,768]{1,0:T(8,128)(2,1)}), bf16[64,768]{1,0:T(8,128)(2,1)}) %reduce-scatter.25.cloned.1.call-update) | async-done | bytes 98320 | tf_op jit(solution)/shard_map/reduce_scatter | solution.py:1145
  382.1 9.7 %all_gather.72 = bf16[256,768]{1,0:T(8,128)(2,1)S(1)} all-gather(bf16[64,768]{1,0:T(8,128)(2,1)S(1)} %fusion.95), channel_id=1, replica_groups=mesh['hg'=4,'core'=2,'sp'=4] {'hg'}, dimensions={0}, use_global_device_ids=true | all-gather | bytes 491520 | tf_op jit(solution)/shard_map/all_gather | solution.py:1142
  395.4 12.1 %shard_map.551 = (bf16[256,192]{1,0:T(8,128)(2,1)}, bf16[2048,192]{1,0:T(8,128)(2,1)}, bf16[2048,192]{1,0:T(8,128)(2,1)}) custom-call(s32[4]{0:T(128)} %copy-done.79, bf16[256,192]{1,0:T(8,128)(2,1)} %convolution_convert_fusion.25.q_ref.refs_1_, bf16[2048,192]{1,0:T(8,128)(2,1)} %get-tuple-element.203.k_ref.refs_2_, ...), custom_call_target="tpu_custom_call" | custom-call | tf_op jit(solution)/shard_map/pallas_call | solution.py:853
  413.3 37.3 %reduce-scatter.27.cloned.1.call-done = bf16[256,384]{1,0:T(8,128)(2,1)} async-done(((bf16[2048,384]{1,0:T(8,128)(2,1)}), bf16[256,384]{1,0:T(8,128)(2,1)}) %reduce-scatter.27.cloned.1.call-update) | async-done | bytes 196624 | tf_op jit(solution)/shard_map/reduce_scatter | solution.py:1154
  455.5 22.1 %reduce-scatter.37.cloned.1.call-done = bf16[64,768]{1,0:T(8,128)(2,1)} async-done(((bf16[256,768]{1,0:T(8,128)(2,1)}), bf16[64,768]{1,0:T(8,128)(2,1)}) %reduce-scatter.37.cloned.1.call-update) | async-done | bytes 98320 | tf_op jit(solution)/shard_map/reduce_scatter | solution.py:1145
  479.2 26.2 %reduce-scatter.29.cloned.1.call-done = bf16[64,768]{1,0:T(8,128)(2,1)} async-done(((bf16[256,768]{1,0:T(8,128)(2,1)}), bf16[64,768]{1,0:T(8,128)(2,1)}) %reduce-scatter.29.cloned.1.call-update) | async-done | bytes 98320 | tf_op jit(solution)/shard_map/reduce_scatter | solution.py:1145
  507.6 9.7 %all_gather.73 = bf16[256,768]{1,0:T(8,128)(2,1)S(1)} all-gather(bf16[64,768]{1,0:T(8,128)(2,1)S(1)} %fusion.96), channel_id=1, replica_groups=mesh['hg'=4,'core'=2,'sp'=4] {'hg'}, dimensions={0}, use_global_device_ids=true | all-gather | bytes 491520 | tf_op jit(solution)/shard_map/all_gather | solution.py:1142
  521.6 11.5 %reduce-scatter.23.cloned.1.call-done = bf16[64,768]{1,0:T(8,128)(2,1)} async-done(((bf16[256,768]{1,0:T(8,128)(2,1)}), bf16[64,768]{1,0:T(8,128)(2,1)}) %reduce-scatter.23.cloned.1.call-update) | async-done | bytes 98320 | tf_op jit(solution)/shard_map/reduce_scatter | solution.py:1145
  534.8 9.8 %all_gather.75 = bf16[256,768]{1,0:T(8,128)(2,1)S(1)} all-gather(bf16[64,768]{1,0:T(8,128)(2,1)S(1)} %get-tuple-element.188), channel_id=1, replica_groups=mesh['hg'=4,'core'=2,'sp'=4] {'hg'}, dimensions={0}, use_global_device_ids=true | all-gather | bytes 491520 | tf_op jit(solution)/shard_map/all_gather | solution.py:1142
  545.7 14.7 %shard_map.553 = (bf16[256,192]{1,0:T(8,128)(2,1)}, bf16[2048,192]{1,0:T(8,128)(2,1)}, bf16[2048,192]{1,0:T(8,128)(2,1)}, f32[3,320,64]{2,1,0:T(8,128)}, f32[6,256]{1,0:T(8,128)}) custom-call(s32[4]{0:T(128)} %copy-done.79, bf16[256,192]{1,0:T(8,128)(2,1)} %convolution_convert_fusion.26.q_ref.refs_1_, bf16[2048,192]{1,0:T(8,128)(2,1)} %get-tuple-element.205.k_ref.refs_2_, ...), custom_call_target="tpu_custom_call" | custom-call | tf_op jit(solution)/shard_map/pallas_call | solution.py:853
  576.7 14.6 %shard_map.552 = (bf16[256,192]{1,0:T(8,128)(2,1)}, bf16[2048,192]{1,0:T(8,128)(2,1)}, bf16[2048,192]{1,0:T(8,128)(2,1)}, f32[3,320,64]{2,1,0:T(8,128)}, f32[6,256]{1,0:T(8,128)}) custom-call(s32[4]{0:T(128)} %copy-done.79, bf16[256,192]{1,0:T(8,128)(2,1)} %convolution_convert_fusion.27.q_ref.refs_1_, bf16[2048,192]{1,0:T(8,128)(2,1)} %get-tuple-element.207.k_ref.refs_2_, ...), custom_call_target="tpu_custom_call" | custom-call | tf_op jit(solution)/shard_map/pallas_call | solution.py:853
  600.0 16.0 %shard_map.557 = (bf16[4,96,1024]{2,1,0:T(8,128)(2,1)}, bf16[256,768]{1,0:T(8,128)(2,1)}) custom-call(bf16[4,2,96,1024]{3,2,1,0:T(8,128)(2,1)} %bitcast.203, bf16[2,256,768]{2,1,0:T(8,128)(2,1)} %bitcast.210), custom_call_target="tpu_custom_call" | custom-call | tf_op jit(solution)/shard_map/pallas_call | solution.py:1054
  623.2 12.4 %shard_map.556 = (bf16[4,96,576]{2,1,0:T(8,128)(2,1)}, bf16[96,768]{1,0:T(8,128)(2,1)}) custom-call(bf16[4,2,96,576]{3,2,1,0:T(8,128)(2,1)} %pad_maximum_fusion.3.refs_0_, bf16[2,96,768]{2,1,0:T(8,128)(2,1)} %bitcast.231), custom_call_target="tpu_custom_call" | custom-call | tf_op jit(solution)/shard_map/pallas_call | solution.py:1054
  651.2 24.9 %shard_map.555 = (bf16[4,96,1024]{2,1,0:T(8,128)(2,1)}, bf16[4,96,576]{2,1,0:T(8,128)(2,1)}, bf16[96,768]{1,0:T(8,128)(2,1)}, bf16[256,768]{1,0:T(8,128)(2,1)}) custom-call(bf16[4,2,96,1024]{3,2,1,0:T(8,128)(2,1)} %bitcast.202, bf16[4,2,96,576]{3,2,1,0:T(8,128)(2,1)} %bitcast.207, bf16[2,96,768]{2,1,0:T(8,128)(2,1)} %bitcast.224, bf16[2,256,768]{2,1,0:T(8,128)(2,1)} %bitcast.209), custom_call_target="tpu_custom_call" | custom-call | tf_op jit(solution)/shard_map/pallas_call | solution.py:1054
  679.0 14.4 %shard_map.554 = (bf16[4,96,576]{2,1,0:T(8,128)(2,1)}, bf16[96,768]{1,0:T(8,128)(2,1)}) custom-call(bf16[4,2,96,576]{3,2,1,0:T(8,128)(2,1)} %bitcast.208, bf16[2,96,768]{2,1,0:T(8,128)(2,1)} %bitcast.232), custom_call_target="tpu_custom_call" | custom-call | tf_op jit(solution)/shard_map/pallas_call | solution.py:1054
  706.3 44.3 %psum.77 = f32[8,672]{1,0:T(8,128)S(1)} all-reduce(f32[8,672]{1,0:T(8,128)S(1)} %concatenate.82), channel_id=1, replica_groups=mesh['hg'=4,'core'=2,'sp'=4] {'hg','core','sp'}, use_global_device_ids=true, to_apply=%region_41.42 | all-reduce | flops 5376 | bytes 43008 | tf_op jit(solution)/shard_map/psum | solution.py:1287
  753.5 115.0 %all-reduce.8.cloned.1.call-done = (bf16[4,96,576]{2,1,0:T(8,128)(2,1)}, bf16[96,768]{1,0:T(8,128)(2,1)}, bf16[4,96,1024]{2,1,0:T(8,128)(2,1)}, bf16[256,768]{1,...) async-done(((bf16[4,96,576]{2,1,0:T(8,128)(2,1)}, ...) | async-done | bytes 4128784 | tf_op jit(solution)/shard_map/psum | solution.py:1249
  (476 shorter events, 229.5 us)
Async XLA Ops:
  7.2 46.3 %copy-start.66 = (bf16[96,768]{1,0:T(8,128)(2,1)S(1)}, bf16[96,768]{1,0:T(8,128)(2,1)}, u32[]{:S(2)}) copy-start(bf16[96,768]{1,0:T(8,128)(2,1)} %param.50) | copy-start | bytes 442372
  7.2 46.5 %copy-start.67 = (bf16[96,768]{1,0:T(8,128)(2,1)S(1)}, bf16[96,768]{1,0:T(8,128)(2,1)}, u32[]{:S(2)}) copy-start(bf16[96,768]{1,0:T(8,128)(2,1)} %param.49) | copy-start | bytes 442372
  7.2 46.8 %copy-start.68 = (bf16[96,768]{1,0:T(8,128)(2,1)S(1)}, bf16[96,768]{1,0:T(8,128)(2,1)}, u32[]{:S(2)}) copy-start(bf16[96,768]{1,0:T(8,128)(2,1)} %param.62) | copy-start | bytes 442372
  7.2 144.6 %all-gather.8.cloned.1.call-start = ((), (), s32[]{:S(2)}) async-start(), calls=%async_computation.28 | async-start | bytes 1769472 | tf_op jit(solution)/shard_map/all_gather | solution.py:1148
  52.2 85.1 %copy-start.11 = (bf16[256,768]{1,0:T(8,128)(2,1)}, bf16[256,768]{1,0:T(8,128)(2,1)S(1)}, u32[]{:S(2)}) copy-start(bf16[256,768]{1,0:T(8,128)(2,1)S(1)} %all_gather.59) | copy-start | bytes 1179652
  126.3 64.5 %reduce-scatter.15.cloned.1.call-start = ((), (), s32[]{:S(2)}) async-start(), calls=%async_computation.14 | async-start | bytes 491520 | tf_op jit(solution)/shard_map/reduce_scatter | solution.py:1145
  166.7 51.4 %all-gather.10.cloned.1.call-start = ((), (), s32[]{:S(2)}) async-start(), calls=%async_computation.29 | async-start | bytes 1769472 | tf_op jit(solution)/shard_map/all_gather | solution.py:1148
  179.1 65.9 %reduce-scatter.17.cloned.1.call-start = ((), (), s32[]{:S(2)}) async-start(), calls=%async_computation.15 | async-start | bytes 491520 | tf_op jit(solution)/shard_map/reduce_scatter | solution.py:1145
  205.3 67.3 %reduce-scatter.19.cloned.1.call-start = ((), (), s32[]{:S(2)}) async-start(), calls=%async_computation.16 | async-start | bytes 491520 | tf_op jit(solution)/shard_map/reduce_scatter | solution.py:1145
  232.9 66.9 %all-gather.12.cloned.1.call-start = ((), (), s32[]{:S(2)}) async-start(), calls=%async_computation.30 | async-start | bytes 1769472 | tf_op jit(solution)/shard_map/all_gather | solution.py:1148
  246.0 319.2 %copy-start.3 = (f32[64,768]{1,0:T(8,128)}, f32[64,768]{1,0:T(8,128)S(1)}, u32[]{:S(2)}) copy-start(f32[64,768]{1,0:T(8,128)S(1)} %get-tuple-element.193) | copy-start | bytes 589828
  258.3 79.7 %reduce-scatter.21.cloned.1.call-start = ((), (), s32[]{:S(2)}) async-start(), calls=%async_computation.17 | async-start | bytes 491520 | tf_op jit(solution)/shard_map/reduce_scatter | solution.py:1145
  311.9 26.1 %copy-start.2 = (bf16[64,768]{1,0:T(8,128)(2,1)S(1)}, bf16[64,768]{1,0:T(8,128)(2,1)}, u32[]{:S(2)}) copy-start(bf16[64,768]{1,0:T(8,128)(2,1)} %reduce-scatter.19.cloned.1.call-done) | copy-start | bytes 294916
  313.9 66.1 %reduce-scatter.25.cloned.1.call-start = ((), (), s32[]{:S(2)}) async-start(), calls=%async_computation.19 | async-start | bytes 491520 | tf_op jit(solution)/shard_map/reduce_scatter | solution.py:1145
  324.2 27.6 %copy-start.17 = (bf16[256,768]{1,0:T(8,128)(2,1)}, bf16[256,768]{1,0:T(8,128)(2,1)S(1)}, u32[]{:S(2)}) copy-start(bf16[256,768]{1,0:T(8,128)(2,1)S(1)} %all_gather.71) | copy-start | bytes 1179652
  354.0 26.0 %copy-start.5 = (bf16[64,768]{1,0:T(8,128)(2,1)S(1)}, bf16[64,768]{1,0:T(8,128)(2,1)}, u32[]{:S(2)}) copy-start(bf16[64,768]{1,0:T(8,128)(2,1)} %reduce-scatter.21.cloned.1.call-done) | copy-start | bytes 294916
  354.0 27.1 %copy-start.29 = (bf16[64,768]{1,0:T(8,128)(2,1)S(1)}, bf16[64,768]{1,0:T(8,128)(2,1)}, u32[]{:S(2)}) copy-start(bf16[64,768]{1,0:T(8,128)(2,1)} %param.44) | copy-start | bytes 294916
  355.4 95.1 %reduce-scatter.27.cloned.1.call-start = ((), (), s32[]{:S(2)}) async-start(), calls=%async_computation.20 | async-start | bytes 1769472 | tf_op jit(solution)/shard_map/reduce_scatter | solution.py:1154
  381.1 26.4 %copy-start.83 = (f32[64]{0:T(128)}, f32[64]{0:T(128)S(1)}, u32[]{:S(2)}) copy-start(f32[64]{0:T(128)S(1)} %broadcast_multiply_fusion.5) | copy-start | bytes 772
  411.0 66.6 %reduce-scatter.37.cloned.1.call-start = ((), (), s32[]{:S(2)}) async-start(), calls=%async_computation.25 | async-start | bytes 491520 | tf_op jit(solution)/shard_map/reduce_scatter | solution.py:1145
  413.2 92.2 %reduce-scatter.29.cloned.1.call-start = ((), (), s32[]{:S(2)}) async-start(), calls=%async_computation.21 | async-start | bytes 491520 | tf_op jit(solution)/shard_map/reduce_scatter | solution.py:1145
  453.1 80.0 %reduce-scatter.23.cloned.1.call-start = ((), (), s32[]{:S(2)}) async-start(), calls=%async_computation.18 | async-start | bytes 491520 | tf_op jit(solution)/shard_map/reduce_scatter | solution.py:1145
  455.5 108.6 %reduce-scatter.31.cloned.1.call-start = ((), (), s32[]{:S(2)}) async-start(), calls=%async_computation.22 | async-start | bytes 491520 | tf_op jit(solution)/shard_map/reduce_scatter | solution.py:1145
  521.5 96.9 %reduce-scatter.39.cloned.1.call-start = ((), (), s32[]{:S(2)}) async-start(), calls=%async_computation.26 | async-start | bytes 1769472 | tf_op jit(solution)/shard_map/reduce_scatter | solution.py:1154
  564.0 80.7 %reduce-scatter.33.cloned.1.call-start = ((), (), s32[]{:S(2)}) async-start(), calls=%async_computation.23 | async-start | bytes 1769472 | tf_op jit(solution)/shard_map/reduce_scatter | solution.py:1154
  594.8 103.9 %reduce-scatter.41.cloned.1.call-start = ((), (), s32[]{:S(2)}) async-start(), calls=%async_computation.27 | async-start | bytes 491520 | tf_op jit(solution)/shard_map/reduce_scatter | solution.py:1145
  621.1 83.9 %reduce-scatter.35.cloned.1.call-start = ((), (), s32[]{:S(2)}) async-start(), calls=%async_computation.24 | async-start | bytes 491520 | tf_op jit(solution)/shard_map/reduce_scatter | solution.py:1145
  647.3 221.1 %all-reduce.8.cloned.1.call-start = ((), (), s32[]{:S(2)}) async-start(), calls=%async_computation.31 | async-start | bytes 8552448 | tf_op jit(solution)/shard_map/psum | solution.py:1249
  651.2 25.9 %copy-start.12 = (bf16[256,768]{1,0:T(8,128)(2,1)S(1)}, bf16[256,768]{1,0:T(8,128)(2,1)}, u32[]{:S(2)}) copy-start(bf16[256,768]{1,0:T(8,128)(2,1)} %copy-done.11) | copy-start | bytes 1179652
  651.2 25.9 %copy-start.62 = (bf16[256,384]{1,0:T(8,128)(2,1)S(1)}, bf16[256,384]{1,0:T(8,128)(2,1)}, u32[]{:S(2)}) copy-start(bf16[256,384]{1,0:T(8,128)(2,1)} %reduce-scatter.33.cloned.1.call-done) | copy-start | bytes 589828
  701.5 50.3 %copy-start.36 = (f32[64,768]{1,0:T(8,128)S(1)}, f32[64,768]{1,0:T(8,128)}, u32[]{:S(2)}) copy-start(f32[64,768]{1,0:T(8,128)} %get-tuple-element.191) | copy-start | bytes 589828
  701.5 50.3 %copy-start.88 = (f32[64]{0:T(128)S(1)}, f32[64]{0:T(128)}, u32[]{:S(2)}) copy-start(f32[64]{0:T(128)} %get-tuple-element.239) | copy-start | bytes 772
  (77 other events, 502.0 us)
Sparse Core Ops, SparseCore 0:
  126.5 25.3 all-gather.7
  166.8 23.9 reduce-scatter.14
  193.0 25.0 all-gather.9
  221.3 23.6 reduce-scatter.16
  248.2 24.3 reduce-scatter.18
  274.7 25.0 all-gather.11
  314.0 23.9 reduce-scatter.20
  355.5 24.4 reduce-scatter.24
  411.1 39.3 reduce-scatter.26
  453.8 23.7 reduce-scatter.36
  481.0 24.3 reduce-scatter.28
  508.6 24.4 reduce-scatter.22
  536.4 24.4 reduce-scatter.30
  564.1 39.4 reduce-scatter.38
  605.8 38.8 reduce-scatter.32
  647.9 27.0 reduce-scatter.40
  678.3 24.9 reduce-scatter.34
  706.3 162.1 all-reduce.7

commit v3 on v2

--- a/solution.py
+++ b/solution.py
@@ -710,160 +710,6 @@
 
 
 VMEM_BYTES = 56 << 20
-ROWS = 512
-
-
-def head_scores(k_ref, masked_q, bm_ref, head, at):
-    bias_head = head if bm_ref.shape[0] > 1 else 0
-    bias = bm_ref[bias_head, pl.ds(pl.multiple_of(BLOCK_PAD + at, 128), ROWS), :].astype(jnp.float32)
-    return nt(k_ref[pl.ds(at, ROWS), :], masked_q) + bias
-
-
-def mix_kernel(q_ref, k_ref, v_ref, bm_ref, o_ref, lse_ref, s_ref, p_ref, ot_ref):
-    key_len, width = k_ref.shape
-    lanes = q_ref.shape[0]
-    vt = nt(identity(width), v_ref[...]).astype(jnp.bfloat16)
-    for head in range(width // HD):
-        masked_q = only_head(q_ref[...], head)
-
-        def first(number, top):
-            at = pl.multiple_of(number * ROWS, ROWS)
-            scores = head_scores(k_ref, masked_q, bm_ref, head, at)
-            s_ref[pl.ds(at, ROWS), :] = scores
-            return jnp.maximum(top, jnp.max(scores, axis=0, keepdims=True))
-
-        top = lax.fori_loop(0, key_len // ROWS, first, jnp.full((1, lanes), NEGATIVE, jnp.float32))
-
-        def second(number, total):
-            at = pl.multiple_of(number * ROWS, ROWS)
-            weights = jnp.exp(s_ref[pl.ds(at, ROWS), :] - top)
-            p_ref[pl.ds(at, ROWS), :] = weights.astype(jnp.bfloat16)
-            return total + jnp.sum(weights, axis=0, keepdims=True)
-
-        total = lax.fori_loop(0, key_len // ROWS, second, jnp.zeros((1, lanes), jnp.float32))
-        lse_ref[:, head * lanes : (head + 1) * lanes] = top + jnp.log(total)
-        mixed = nn(vt[head * HD : (head + 1) * HD], p_ref[...])
-        ot_ref[head * HD : (head + 1) * HD, :] = (mixed / total).astype(jnp.bfloat16)
-    o_ref[...] = nt(identity(lanes), ot_ref[...]).astype(jnp.bfloat16)
-
-
-def mix(q, k, v, bm):
-    lanes, width = q.shape
-    heads = width // HD
-    return pl.pallas_call(
-        mix_kernel,
-        out_shape=(
-            jax.ShapeDtypeStruct((lanes, width), jnp.bfloat16),
-            jax.ShapeDtypeStruct((1, heads * lanes), jnp.float32),
-        ),
-        in_specs=[pl.BlockSpec(memory_space=pltpu.VMEM)] * 4,
-        out_specs=(pl.BlockSpec(memory_space=pltpu.VMEM),) * 2,
-        scratch_shapes=[
-            pltpu.VMEM((k.shape[0], lanes), jnp.float32),
-            pltpu.VMEM((k.shape[0], lanes), jnp.bfloat16),
-            pltpu.VMEM((width, lanes), jnp.bfloat16),
-        ],
-        compiler_params=pltpu.CompilerParams(vmem_limit_bytes=VMEM_BYTES),
-    )(q, k, v, bm)
-
-
-def mix_back_kernel(block, starts_ref, q_ref, k_ref, v_ref, do_ref, lse_ref, bm_ref, qstart_ref, dq_ref, dk_ref, dv_ref, strip_ref, edge_ref, p_ref, dp_ref, ds_ref, pb_ref, ot_ref):
-    key_len, width = k_ref.shape
-    lanes = q_ref.shape[0]
-    heads = width // HD
-    biased = strip_ref is not None
-    strip = block + 2 * BLOCK_PAD
-    kt = nt(identity(width), k_ref[...]).astype(jnp.bfloat16)
-    if biased:
-        none = jnp.zeros((BLOCK_PAD, heads * lanes), jnp.bfloat16)
-        ds_ref[0:BLOCK_PAD, :] = none
-        ds_ref[BLOCK_PAD + key_len :, :] = none
-    for head in range(heads):
-        masked_q = only_head(q_ref[...], head)
-        masked_do = only_head(do_ref[...], head)
-        across = slice(head * lanes, (head + 1) * lanes)
-
-        def first(number, inner):
-            at = pl.multiple_of(number * ROWS, ROWS)
-            p = jnp.exp(head_scores(k_ref, masked_q, bm_ref, head, at) - lse_ref[:, across])
-            dp = nt(v_ref[pl.ds(at, ROWS), :], masked_do)
-            p_ref[pl.ds(at, ROWS), :] = p
-            dp_ref[pl.ds(at, ROWS), :] = dp
-            pb_ref[pl.ds(at, ROWS), across] = p.astype(jnp.bfloat16)
-            return inner + jnp.sum(p * dp, axis=0, keepdims=True)
-
-        inner = lax.fori_loop(0, key_len // ROWS, first, jnp.zeros((1, lanes), jnp.float32))
-
-        def second(number, sums):
-            at = pl.multiple_of(number * ROWS, ROWS)
-            ds = (p_ref[pl.ds(at, ROWS), :] * (dp_ref[pl.ds(at, ROWS), :] - inner)).astype(jnp.bfloat16)
-            ds_ref[pl.ds(BLOCK_PAD + at, ROWS), across] = ds
-            if not biased:
-                return sums
-            wide = ds.astype(jnp.float32)
-            places = lax.broadcasted_iota(jnp.int32, wide.shape, 0) + (at + BLOCK_PAD)
-            left = jnp.sum(jnp.where(places < qstart_ref[...], wide, 0.0), axis=0, keepdims=True)
-            right = jnp.sum(jnp.where(places >= qstart_ref[...] + strip, wide, 0.0), axis=0, keepdims=True)
-            return (sums[0] + left, sums[1] + right)
-
-        nothing = jnp.zeros((1, lanes), jnp.float32)
-        left, right = lax.fori_loop(0, key_len // ROWS, second, (nothing, nothing))
-        if biased:
-            edge_ref[2 * head : 2 * head + 1, :] = left
-            edge_ref[2 * head + 1 : 2 * head + 2, :] = right
-            total = jnp.zeros((strip, block), jnp.float32)
-            for number in range(lanes // block):
-                low = head * lanes + number * block
-                rows = pl.ds(pl.multiple_of(starts_ref[number], block), strip)
-                total = total + ds_ref[rows, low : low + block].astype(jnp.float32)
-            strip_ref[head] = total
-        back = nn(kt[head * HD : (head + 1) * HD], ds_ref[BLOCK_PAD : BLOCK_PAD + key_len, across])
-        ot_ref[head * HD : (head + 1) * HD, :] = back.astype(jnp.bfloat16)
-    dq_ref[...] = nt(identity(lanes), ot_ref[...]).astype(jnp.bfloat16)
-    stacked_q = jnp.concatenate([only_head(q_ref[...], head) for head in range(heads)], axis=0)
-    stacked_do = jnp.concatenate([only_head(do_ref[...], head) for head in range(heads)], axis=0)
-
-    @pl.loop(0, key_len // ROWS)
-    def _(number):
-        at = pl.multiple_of(number * ROWS, ROWS)
-        dk_ref[pl.ds(at, ROWS), :] = nn(ds_ref[pl.ds(BLOCK_PAD + at, ROWS), :], stacked_q).astype(dk_ref.dtype)
-        dv_ref[pl.ds(at, ROWS), :] = nn(pb_ref[pl.ds(at, ROWS), :], stacked_do).astype(dv_ref.dtype)
-
-
-def mix_back(starts, q, k, v, do, lse, bm, block, biased):
-    lanes, width = q.shape
-    key_len = k.shape[0]
-    heads = width // HD
-    qstart = jnp.repeat(starts, block)[None, :]
-    shapes = [
-        jax.ShapeDtypeStruct((lanes, width), jnp.bfloat16),
-        jax.ShapeDtypeStruct((key_len, width), jnp.bfloat16),
-        jax.ShapeDtypeStruct((key_len, width), jnp.bfloat16),
-    ]
-    if biased:
-        shapes.append(jax.ShapeDtypeStruct((heads, block + 2 * BLOCK_PAD, block), jnp.float32))
-        shapes.append(jax.ShapeDtypeStruct((2 * heads, lanes), jnp.float32))
-
-    def body(*refs):
-        refs = list(refs)
-        if not biased:
-            refs[11:11] = [None, None]
-        mix_back_kernel(block, *refs)
-
-    return pl.pallas_call(
-        body,
-        out_shape=tuple(shapes),
-        in_specs=[pl.BlockSpec(memory_space=pltpu.SMEM)] + [pl.BlockSpec(memory_space=pltpu.VMEM)] * 7,
-        out_specs=(pl.BlockSpec(memory_space=pltpu.VMEM),) * len(shapes),
-        scratch_shapes=[
-            pltpu.VMEM((key_len, lanes), jnp.float32),
-            pltpu.VMEM((key_len, lanes), jnp.float32),
-            pltpu.VMEM((key_len + 2 * BLOCK_PAD, heads * lanes), jnp.bfloat16),
-            pltpu.VMEM((key_len, heads * lanes), jnp.bfloat16),
-            pltpu.VMEM((width, lanes), jnp.bfloat16),
-        ],
-        compiler_params=pltpu.CompilerParams(vmem_limit_bytes=VMEM_BYTES),
-    )(starts, q, k, v, do, lse, bm, qstart)
 
 
 def send(src, dst, send_sem, recv_sem, to):
@@ -1064,48 +910,531 @@
     return got[:cols], got[cols:]
 
 
+def spread_start(place, buf, sent, got):
+    mine = buf.at[place.group]
+    return [
+        send(mine, mine, sent.at[step], got.at[step], place.chip(place.ahead(step))) for step in range(1, place.groups)
+    ]
+
+
+def spread_wait(place, buf, sent, got):
+    for step in range(1, place.groups):
+        source = place.behind(step)
+        arrived(buf.at[source], sent.at[step], got.at[step], place.chip(source))
+
+
+def collect_start(place, partial, out_buf, in_buf, sent, got):
+    out_buf[...] = partial.astype(jnp.bfloat16).reshape(out_buf.shape)
+    pending = []
+    for step in range(1, place.groups):
+        to = place.ahead(step)
+        pending.append(send(out_buf.at[to], in_buf.at[place.group], sent.at[step], got.at[step], place.chip(to)))
+    return pending
+
+
+def collect_wait(place, out_buf, in_buf, sent, got):
+    total = out_buf[place.group].astype(jnp.float32)
+    for step in range(1, place.groups):
+        source = place.behind(step)
+        arrived(in_buf.at[source], sent.at[step], got.at[step], place.chip(source))
+        total = total + in_buf[source].astype(jnp.float32)
+    return total
+
+
+def whole(buf):
+    return buf[...].reshape(buf.shape[0] * buf.shape[1], buf.shape[2])
+
+
+def gelu_and_slope(v):
+    scale, cubic = math.sqrt(2.0 / math.pi), 0.044715
+    t = jnp.tanh(scale * (v + cubic * v * v * v))
+    return 0.5 * v * (1.0 + t), 0.5 * (1.0 + t) + 0.5 * v * (1.0 - t * t) * scale * (1.0 + 3.0 * cubic * v * v)
+
+
+def norm_back(x, g, dn):
+    r = lax.rsqrt(jnp.mean(x * x, axis=-1, keepdims=True) + EPSILON)
+    w = dn * g
+    dx = r * w - x * (r * r * r) * jnp.mean(w * x, axis=-1, keepdims=True)
+    return dx, jnp.sum(dn * x * r, axis=0, keepdims=True)
+
+
+def low(value):
+    return value.astype(jnp.bfloat16)
+
+
+def feed_forward_kernel(sizes, x_ref, gain_ref, final_ref, gu_ref, down_ref, y_ref, last_ref, n_ref, n_buf, p_buf, r_buf, sent, got):
+    place = Place(*sizes)
+    place.greet(sibling=False)
+    x = x_ref[...]
+    n_buf[place.group] = low(rms_norm(x, gain_ref[...]))
+    pending = spread_start(place, n_buf, sent.at[0], got.at[0])
+    spread_wait(place, n_buf, sent.at[0], got.at[0])
+    n = whole(n_buf)
+    hidden = down_ref.shape[0]
+    gu = nn(n, gu_ref[...])
+    h = low(gelu_and_slope(gu[:, :hidden])[0] * gu[:, hidden:])
+    pending += collect_start(place, nn(h, down_ref[...]), p_buf, r_buf, sent.at[1], got.at[1])
+    n_ref[...] = n
+    y = x + collect_wait(place, p_buf, r_buf, sent.at[1], got.at[1])
+    y_ref[...] = y
+    last_ref[...] = low(rms_norm(y, final_ref[...]))
+    for copy in pending:
+        copy.wait_send()
+
+
+def feed_back_part(n, dyb, gu_ref, down_ref):
+    hidden = down_ref.shape[0]
+    gu = nn(n, gu_ref[...])
+    g, u = gu[:, :hidden], gu[:, hidden:]
+    act, slope = gelu_and_slope(g)
+    h = low(act * u)
+    dh = nt(dyb, down_ref[...])
+    dgu = jnp.concatenate([low(dh * u * slope), low(dh * act)], axis=1)
+    return h, dgu
+
+
+def feed_both_kernel(
+    sizes, x_ref, cot_ref, gain_ref, gu_ref, down_ref,
+    y_ref, dx_ref, dgain_ref, dgu_ref, ddown_ref,
+    n_buf, d_buf, py_buf, ry_buf, pn_buf, rn_buf, sent, got,
+):
+    place = Place(*sizes)
+    place.greet(sibling=False)
+    x = x_ref[...]
+    n_buf[place.group] = low(rms_norm(x, gain_ref[...]))
+    d_buf[place.group] = cot_ref[...]
+    pending = spread_start(place, n_buf, sent.at[0], got.at[0]) + spread_start(place, d_buf, sent.at[1], got.at[1])
+    spread_wait(place, n_buf, sent.at[0], got.at[0])
+    spread_wait(place, d_buf, sent.at[1], got.at[1])
+    n, dyb = whole(n_buf), whole(d_buf)
+    h, dgu = feed_back_part(n, dyb, gu_ref, down_ref)
+    pending += collect_start(place, nt(dgu, gu_ref[...]), pn_buf, rn_buf, sent.at[2], got.at[2])
+    pending += collect_start(place, nn(h, down_ref[...]), py_buf, ry_buf, sent.at[3], got.at[3])
+    dgu_ref[...] = low(tn(n, dgu))
+    ddown_ref[...] = low(tn(h, dyb))
+    dn = collect_wait(place, pn_buf, rn_buf, sent.at[2], got.at[2])
+    back, dgain = norm_back(x, gain_ref[...], dn)
+    dx_ref[...] = cot_ref[...].astype(jnp.float32) + back
+    dgain_ref[...] = dgain
+    y_ref[...] = x + collect_wait(place, py_buf, ry_buf, sent.at[3], got.at[3])
+    for copy in pending:
+        copy.wait_send()
+
+
+def feed_back_kernel(
+    sizes, x_ref, y_ref, cot_ref, dlast_ref, gain_ref, final_ref, n_ref, gu_ref, down_ref,
+    dx_ref, dgain_ref, dfinal_ref, dgu_ref, ddown_ref,
+    d_buf, pn_buf, rn_buf, sent, got,
+):
+    place = Place(*sizes)
+    place.greet(sibling=False)
+    back, dfinal = norm_back(y_ref[...], final_ref[...], dlast_ref[...])
+    dfinal_ref[...] = dfinal
+    dy = cot_ref[...].astype(jnp.float32) + back
+    d_buf[place.group] = low(dy)
+    pending = spread_start(place, d_buf, sent.at[0], got.at[0])
+    spread_wait(place, d_buf, sent.at[0], got.at[0])
+    n, dyb = n_ref[...], whole(d_buf)
+    h, dgu = feed_back_part(n, dyb, gu_ref, down_ref)
+    pending += collect_start(place, nt(dgu, gu_ref[...]), pn_buf, rn_buf, sent.at[1], got.at[1])
+    dgu_ref[...] = low(tn(n, dgu))
+    ddown_ref[...] = low(tn(h, dyb))
+    dn = collect_wait(place, pn_buf, rn_buf, sent.at[1], got.at[1])
+    back, dgain = norm_back(x_ref[...], gain_ref[...], dn)
+    dx_ref[...] = dy + back
+    dgain_ref[...] = dgain
+    for copy in pending:
+        copy.wait_send()
+
+
+def stage(sizes, collective_id, kernel, operands, outs, scratch, copies):
+    vmem = pl.BlockSpec(memory_space=pltpu.VMEM)
+    dma = pltpu.SemaphoreType.DMA
+    return pl.pallas_call(
+        functools.partial(kernel, sizes),
+        out_shape=tuple(jax.ShapeDtypeStruct(shape, dtype) for shape, dtype in outs),
+        in_specs=[vmem] * len(operands),
+        out_specs=(vmem,) * len(outs),
+        scratch_shapes=[pltpu.VMEM(s, jnp.bfloat16) if isinstance(s, tuple) else s for s in scratch] + [dma(copies), dma(copies)],
+        compiler_params=pltpu.CompilerParams(collective_id=collective_id, has_side_effects=True, vmem_limit_bytes=VMEM_BYTES),
+    )(*operands)
+
+
+def head_scores(kv_ref, masked_q, bm_ref, head, chunk):
+    rows = kv_ref.shape[1] * kv_ref.shape[2] * kv_ref.shape[3]
+    width = masked_q.shape[1]
+    bias_head = head if bm_ref.shape[0] > 1 else 0
+    at = pl.multiple_of(BLOCK_PAD + chunk * rows, 128)
+    keys = kv_ref[chunk].reshape(rows, 2 * width)[:, :width]
+    return nt(keys, masked_q) + bm_ref[bias_head, pl.ds(at, rows), :].astype(jnp.float32)
+
+
+def value_side(kv_ref, chunk):
+    rows = kv_ref.shape[1] * kv_ref.shape[2] * kv_ref.shape[3]
+    lanes = kv_ref.shape[4]
+    first = lanes // 2 // 128 * 128
+    return kv_ref[chunk].reshape(rows, lanes)[:, first:]
+
+
+def mix_part(q, kv_ref, bm_ref, o_ref, lse_ref, s_ref, p_ref, ot_ref):
+    chunks = kv_ref.shape[0]
+    rows = kv_ref.shape[1] * kv_ref.shape[2] * kv_ref.shape[3]
+    queries, width = q.shape
+    for head in range(width // HD):
+        masked_q = only_head(q, head)
+
+        def first(chunk, top):
+            scores = head_scores(kv_ref, masked_q, bm_ref, head, chunk)
+            s_ref[pl.ds(pl.multiple_of(chunk * rows, rows), rows), :] = scores
+            return jnp.maximum(top, jnp.max(scores, axis=0, keepdims=True))
+
+        top = lax.fori_loop(0, chunks, first, jnp.full((1, queries), NEGATIVE, jnp.float32))
+
+        def second(chunk, carried):
+            total, mixed = carried
+            weights = jnp.exp(s_ref[pl.ds(pl.multiple_of(chunk * rows, rows), rows), :] - top)
+            values = value_side(kv_ref, chunk)
+            values_t = low(nt(identity(values.shape[1]), values))
+            low_at = values.shape[1] - width + head * HD
+            mixed = mixed + nn(values_t[low_at : low_at + HD], low(weights))
+            return total + jnp.sum(weights, axis=0, keepdims=True), mixed
+
+        start = (jnp.zeros((1, queries), jnp.float32), jnp.zeros((HD, queries), jnp.float32))
+        total, mixed = lax.fori_loop(0, chunks, second, start)
+        lse_ref[:, head * queries : (head + 1) * queries] = top + jnp.log(total)
+        ot_ref[head * HD : (head + 1) * HD, :] = low(mixed / total)
+    o_ref[...] = low(nt(identity(queries), ot_ref[...]))
+
+
+def keys_send(place, kv_ref, base, sent, got):
+    mine = kv_ref.at[:, place.core, place.part]
+    pending = [
+        send(mine, mine, sent.at[base, step], got.at[base, step], place.at_plane(place.plane(step)))
+        for step in range(1, place.parts)
+    ]
+    pending.append(send(mine, mine, sent.at[base + 1, 0], got.at[base + 1, 0], place.sibling()))
+    return pending
+
+
+def keys_relay(place, kv_ref, base, sent, got):
+    pending = []
+    for step in range(1, place.parts):
+        source = place.plane_behind(step)
+        slot = kv_ref.at[:, place.core, source]
+        arrived(slot, sent.at[base, step], got.at[base, step], place.at_plane(source))
+        pending.append(send(slot, slot, sent.at[base + 1, step], got.at[base + 1, step], place.sibling()))
+    return pending
+
+
+def keys_wait(place, kv_ref, base, sent, got):
+    for step in range(place.parts):
+        slot = kv_ref.at[:, 1 - place.core, place.plane_behind(step)]
+        arrived(slot, sent.at[base + 1, step], got.at[base + 1, step], place.sibling())
+
+
+def attend_kernel(sizes, crosses, *refs):
+    place = Place(*sizes)
+    refs = list(refs)
+
+    def take(count):
+        taken, refs[:] = refs[:count], refs[count:]
+        return taken
+
+    count = len(crosses)
+    ins = [take(6 if cross else 5) for cross in crosses]
+    outs = [take(7 if cross else 6) for cross in crosses]
+    s_ref, p_ref, ot_ref = take(3)
+    bufs = [take(4 if cross else 3) for cross in crosses]
+    sent, got = take(2)
+    place.greet(planes=True)
+    pending = []
+    for index, cross in enumerate(crosses):
+        x_ref, gain_ref = ins[index][0], ins[index][1]
+        if cross:
+            bufs[index][3][place.group] = ins[index][5][...]
+            pending += spread_start(place, bufs[index][3], sent.at[5 * index + 4], got.at[5 * index + 4])
+        bufs[index][0][place.group] = low(rms_norm(x_ref[...].astype(jnp.float32), gain_ref[...]))
+        pending += spread_start(place, bufs[index][0], sent.at[5 * index], got.at[5 * index])
+    queries = []
+    for index, cross in enumerate(crosses):
+        w_ref, kv_ref = ins[index][2], outs[index][3]
+        kv_width = kv_ref.shape[4]
+        n_buf = bufs[index][0]
+        if cross:
+            source = bufs[index][3]
+            spread_wait(place, source, sent.at[5 * index + 4], got.at[5 * index + 4])
+            kv = low(nn(whole(source), w_ref[:, :kv_width]))
+            outs[index][6][...] = whole(source)
+        else:
+            spread_wait(place, n_buf, sent.at[5 * index], got.at[5 * index])
+            both = low(nn(whole(n_buf), w_ref[...]))
+            kv, q = both[:, :kv_width], both[:, kv_width:]
+        kv_ref[:, place.core, place.part] = kv.reshape(kv_ref.shape[0], kv_ref.shape[3], kv_width)
+        pending += keys_send(place, kv_ref, 5 * index + 1, sent, got)
+        if cross:
+            spread_wait(place, n_buf, sent.at[5 * index], got.at[5 * index])
+            q = low(nn(whole(n_buf), w_ref[:, kv_width:]))
+        outs[index][1][...] = whole(n_buf)
+        outs[index][2][...] = q
+        queries.append(q)
+    for index in range(count):
+        pending += keys_relay(place, outs[index][3], 5 * index + 1, sent, got)
+    for index in range(count):
+        x_ref, wo_ref, bm_ref = ins[index][0], ins[index][3], ins[index][4]
+        kv_ref, o_ref, lse_ref = outs[index][3], outs[index][4], outs[index][5]
+        keys_wait(place, kv_ref, 5 * index + 1, sent, got)
+        mix_part(outs[index][2][...], kv_ref, bm_ref, o_ref, lse_ref, s_ref, p_ref, ot_ref)
+        share = nn(o_ref[...], wo_ref[...])
+        pending += collect_start(place, share, bufs[index][1], bufs[index][2], sent.at[5 * index + 3], got.at[5 * index + 3])
+    for index in range(count):
+        total = collect_wait(place, bufs[index][1], bufs[index][2], sent.at[5 * index + 3], got.at[5 * index + 3])
+        outs[index][0][...] = ins[index][0][...].astype(jnp.float32) + total
+    for copy in pending:
+        copy.wait_send()
+
+
+def attend(sizes, collective_id, layers):
+    groups, cores, parts = sizes
+    operands, outs, scratch, crosses = [], [], [], []
+    f32, bf16 = jnp.float32, jnp.bfloat16
+    for x, gain, w, wo, bm, memory in layers:
+        block, model = x.shape
+        width = wo.shape[0]
+        tokens = groups * block
+        operands += [x, gain, w, wo, bm] + ([] if memory is None else [memory])
+        outs += [
+            ((block, model), f32), ((tokens, model), bf16), ((tokens, width), bf16),
+            ((groups, cores, parts, block, 2 * width), bf16), ((tokens, width), bf16), ((1, width // HD * tokens), f32),
+        ]
+        if memory is not None:
+            outs.append(((tokens, model), bf16))
+        scratch += [(groups, block, model)] * (3 if memory is None else 4)
+        crosses.append(memory is not None)
+    keys = cores * parts * tokens
+    first = [pltpu.VMEM((keys, tokens), f32), (keys, tokens), (width, tokens)]
+    copies = (5 * len(layers), max(groups, parts))
+    got = stage(sizes, collective_id, lambda s, *refs: attend_kernel(s, crosses, *refs), operands, outs, first + scratch, copies)
+    results, at = [], 0
+    for cross in crosses:
+        size = 7 if cross else 6
+        results.append(tuple(got[at : at + size]) + (() if cross else (None,)))
+        at += size
+    return results
+
+
+def mix_back_part(starts, q, do, kv_ref, lse_ref, bm_ref, strip_ref, edge_ref, dkv_ref, p_ref, dp_ref, ds_ref, pb_ref, ot_ref):
+    chunks, _, _, block, lanes = kv_ref.shape
+    rows = kv_ref.shape[1] * kv_ref.shape[2] * block
+    queries, width = q.shape
+    heads = width // HD
+    biased = strip_ref is not None
+    strip = block + 2 * BLOCK_PAD
+    first_value = width // 128 * 128
+    lead = width - first_value
+    do_wide = jnp.concatenate([jnp.zeros((queries, lead), do.dtype), do], axis=1) if lead else do
+
+    def only_value_head(head):
+        at = lax.broadcasted_iota(jnp.int32, do_wide.shape, 1)
+        keep = (at >= lead + head * HD) & (at < lead + (head + 1) * HD)
+        return jnp.where(keep, do_wide, jnp.zeros_like(do_wide))
+
+    if biased:
+        none = jnp.zeros((BLOCK_PAD, heads * queries), jnp.bfloat16)
+        ds_ref[0:BLOCK_PAD, :] = none
+        ds_ref[BLOCK_PAD + chunks * rows :, :] = none
+        cores = kv_ref.shape[1]
+        parts = kv_ref.shape[2]
+        of_lane = lax.broadcasted_iota(jnp.int32, (1, queries), 1) // block
+        lane_start = ((cores * of_lane + starts.core) * parts + starts.part) * block
+    for head in range(heads):
+        masked_q, masked_do = only_head(q, head), only_value_head(head)
+        across = slice(head * queries, (head + 1) * queries)
+
+        def first(chunk, inner):
+            inside = pl.ds(pl.multiple_of(chunk * rows, rows), rows)
+            p = jnp.exp(head_scores(kv_ref, masked_q, bm_ref, head, chunk) - lse_ref[:, across])
+            dp = nt(value_side(kv_ref, chunk), masked_do)
+            p_ref[inside, :] = p
+            dp_ref[inside, :] = dp
+            pb_ref[inside, across] = low(p)
+            return inner + jnp.sum(p * dp, axis=0, keepdims=True)
+
+        inner = lax.fori_loop(0, chunks, first, jnp.zeros((1, queries), jnp.float32))
+
+        def second(chunk, carried):
+            left, right, back = carried
+            at = pl.multiple_of(chunk * rows, rows)
+            ds = low(p_ref[pl.ds(at, rows), :] * (dp_ref[pl.ds(at, rows), :] - inner))
+            ds_ref[pl.ds(BLOCK_PAD + at, rows), across] = ds
+            keys = kv_ref[chunk].reshape(rows, lanes)[:, :width]
+            keys_t = low(nt(identity(width), keys))
+            back = back + nn(keys_t[head * HD : (head + 1) * HD], ds)
+            if biased:
+                wide = ds.astype(jnp.float32)
+                places = lax.broadcasted_iota(jnp.int32, wide.shape, 0) + (at + BLOCK_PAD)
+                left = left + jnp.sum(jnp.where(places < lane_start, wide, 0.0), axis=0, keepdims=True)
+                right = right + jnp.sum(jnp.where(places >= lane_start + strip, wide, 0.0), axis=0, keepdims=True)
+            return left, right, back
+
+        nothing = jnp.zeros((1, queries), jnp.float32)
+        left, right, back = lax.fori_loop(0, chunks, second, (nothing, nothing, jnp.zeros((HD, queries), jnp.float32)))
+        ot_ref[head * HD : (head + 1) * HD, :] = low(back)
+        if biased:
+            edge_ref[2 * head : 2 * head + 1, :] = left
+            edge_ref[2 * head + 1 : 2 * head + 2, :] = right
+            total = jnp.zeros((strip, block), jnp.float32)
+            for number in range(queries // block):
+                at = pl.multiple_of(((cores * number + starts.core) * parts + starts.part) * block, block)
+                low_at = head * queries + number * block
+                total = total + ds_ref[pl.ds(at, strip), low_at : low_at + block].astype(jnp.float32)
+            strip_ref[head] = total
+    stacked_q = jnp.concatenate([only_head(q, head) for head in range(heads)], axis=0)
+    if lead:
+        stacked_q = jnp.concatenate([stacked_q, jnp.zeros((stacked_q.shape[0], lead), stacked_q.dtype)], axis=1)
+    stacked_do = jnp.concatenate([only_value_head(head) for head in range(heads)], axis=0)
+
+    def third(chunk, carried):
+        at = pl.multiple_of(chunk * rows, rows)
+        dk = nn(ds_ref[pl.ds(BLOCK_PAD + at, rows), :], stacked_q)
+        dv = nn(pb_ref[pl.ds(at, rows), :], stacked_do)
+        if lead:
+            shared = dk[:, first_value:] + dv[:, : 2 * lead]
+            both = jnp.concatenate([dk[:, :first_value], shared, dv[:, 2 * lead :]], axis=1)
+        else:
+            both = jnp.concatenate([dk, dv], axis=1)
+        dkv_ref[chunk] = low(both).reshape(dkv_ref.shape[1:])
+        return carried
+
+    lax.fori_loop(0, chunks, third, 0)
+    return low(nt(identity(queries), ot_ref[...]))
+
+
+def attend_back_kernel(sizes, cross, *refs):
+    refs = list(refs)
+
+    def take(count):
+        taken, refs[:] = refs[:count], refs[count:]
+        return taken
+
+    place = Place(*sizes)
+    x_ref, gain_ref, dy_ref, n_ref, q_ref, kv_ref, o_ref, lse_ref, w_ref, wo_ref, bm_ref = take(11)
+    memory_ref = take(1)[0] if cross else None
+    dx_ref, dgain_ref, dw_ref, dwo_ref = take(4)
+    strip_ref, edge_ref = (None, None) if cross else take(2)
+    dmem_ref = take(1)[0] if cross else None
+    p_ref, dp_ref, ds_ref, pb_ref, ot_ref, dkv_ref, sib_ref, zout_ref, zin_ref, d_buf, pn_buf, rn_buf = take(12)
+    pm_buf, rm_buf = take(2) if cross else (None, None)
+    sent, got = take(2)
+    place.greet(planes=True)
+    dy = dy_ref[...]
+    d_buf[place.group] = low(dy)
+    pending = spread_start(place, d_buf, sent.at[0], got.at[0])
+    spread_wait(place, d_buf, sent.at[0], got.at[0])
+    dyb = whole(d_buf)
+    do = low(nt(dyb, wo_ref[...]))
+    dq = mix_back_part(place, q_ref[...], do, kv_ref, lse_ref, bm_ref, strip_ref, edge_ref, dkv_ref, p_ref, dp_ref, ds_ref, pb_ref, ot_ref)
+    mine = place.core
+    pending.append(send(dkv_ref.at[:, 1 - mine], sib_ref, sent.at[1, 0], got.at[1, 0], place.sibling()))
+    kv_width = kv_ref.shape[4]
+    width = kv_width // 2
+    dwo_ref[...] = low(tn(o_ref[...], dyb))
+    dn_share = nt(dq, w_ref[:, kv_width:])
+    dw_ref[:, kv_width:] = low(tn(n_ref[...], dq))
+    if cross:
+        pending += collect_start(place, dn_share, pn_buf, rn_buf, sent.at[3], got.at[3])
+    arrived(sib_ref, sent.at[1, 0], got.at[1, 0], place.sibling())
+    for step in list(range(1, place.parts)) + [0]:
+        to = place.plane(step)
+        zout_ref[to] = low(dkv_ref[:, mine, to].astype(jnp.float32) + sib_ref[:, to].astype(jnp.float32))
+        if step:
+            pending.append(send(zout_ref.at[to], zin_ref.at[place.part], sent.at[2, step], got.at[2, step], place.at_plane(to)))
+    total = zout_ref[place.part].astype(jnp.float32)
+    for step in range(1, place.parts):
+        source = place.plane_behind(step)
+        arrived(zin_ref.at[source], sent.at[2, step], got.at[2, step], place.at_plane(source))
+        total = total + zin_ref[source].astype(jnp.float32)
+    dkv = low(total).reshape(q_ref.shape[0], kv_width)
+    if cross:
+        pending += collect_start(place, nt(dkv, w_ref[:, :kv_width]), pm_buf, rm_buf, sent.at[4], got.at[4])
+        dw_ref[:, :kv_width] = low(tn(memory_ref[...], dkv))
+        dmem_ref[...] = collect_wait(place, pm_buf, rm_buf, sent.at[4], got.at[4])
+    else:
+        share = dn_share + nt(dkv, w_ref[:, :kv_width])
+        pending += collect_start(place, share, pn_buf, rn_buf, sent.at[3], got.at[3])
+        dw_ref[:, :kv_width] = low(tn(n_ref[...], dkv))
+    dn = collect_wait(place, pn_buf, rn_buf, sent.at[3], got.at[3])
+    back, dgain = norm_back(x_ref[...].astype(jnp.float32), gain_ref[...], dn)
+    dx_ref[...] = dy + back
+    dgain_ref[...] = dgain
+    for copy in pending:
+        copy.wait_send()
+
+
+def attend_back(sizes, collective_id, x, gain, dy, kept, w, wo, bm, cross):
+    groups, cores, parts = sizes
+    _, n, q, kv, o, lse, memory = kept
+    block, model = x.shape
+    tokens, width = q.shape
+    heads = width // HD
+    keys = cores * parts * tokens
+    f32 = jnp.float32
+    operands = [x, gain, dy, n, q, kv, o, lse, w, wo, bm] + ([memory] if cross else [])
+    bf16 = jnp.bfloat16
+    outs = [((block, model), f32), ((1, model), f32), (w.shape, bf16), (wo.shape, bf16)]
+    if cross:
+        outs.append(((block, model), f32))
+    else:
+        outs += [((heads, block + 2 * BLOCK_PAD, block), f32), ((2 * heads, tokens), f32)]
+    half = (groups, parts, block, 2 * width)
+    turned = (parts, groups, block, 2 * width)
+    scratch = [
+        pltpu.VMEM((keys, tokens), f32), pltpu.VMEM((keys, tokens), f32),
+        (keys + 2 * BLOCK_PAD, heads * tokens), (keys, heads * tokens), (width, tokens),
+        kv.shape, half, turned, turned,
+    ] + [(groups, block, model)] * (5 if cross else 3)
+    copies = (5, max(groups, parts))
+    return stage(sizes, collective_id, lambda s, *refs: attend_back_kernel(s, cross, *refs), operands, outs, scratch, copies)
+
+
 def fast_device(
     enc_in, dec_in, enc_cot, dec_cot, enc_segments, dec_segments, buckets,
     enc_norm1, enc_query, enc_key, enc_value, enc_proj, enc_rel, enc_norm2, enc_gate, enc_up, enc_down, enc_final,
     dec_norm1, dec_query, dec_key, dec_value, dec_proj, dec_rel, dec_norm2, cross_query, cross_key, cross_value, cross_proj,
     dec_norm3, dec_gate, dec_up, dec_down,
 ):
-    groups, cores, parts = lax.axis_size(HG), lax.axis_size(CORE), lax.axis_size(SP)
+    groups, cores, parts = sizes = lax.axis_size(HG), lax.axis_size(CORE), lax.axis_size(SP)
     my_group, my_core, my_part = lax.axis_index(HG), lax.axis_index(CORE), lax.axis_index(SP)
     block, model = enc_in.shape
     share = model // (groups * cores)
-    width = HEADS // groups * HD
     heads = HEADS // groups
     reach = (buckets.shape[1] - 1) // 2
     bf16, f32 = jnp.bfloat16, jnp.float32
 
-    sizes = (groups, cores, parts)
-
     def packed(*weights):
         cut = [w.reshape(w.shape[0], groups, w.shape[1] // groups) for w in weights]
         return jnp.concatenate(cut, axis=2).transpose(1, 0, 2)
 
+    small = jnp.concatenate([enc_norm1, enc_norm2, enc_final, dec_norm1, dec_norm2, dec_norm3, enc_rel, dec_rel])
+    small = jnp.broadcast_to(small, (groups, 16, small.shape[0]))
     cols, rows = recut(
         sizes,
         1,
         [
-            packed(enc_query, enc_key, enc_value),
-            packed(dec_query, dec_key, dec_value),
+            small,
+            packed(enc_key, enc_value, enc_query),
+            packed(dec_key, dec_value, dec_query),
             packed(enc_gate, enc_up),
-            packed(cross_query, cross_key, cross_value),
+            packed(cross_key, cross_value, cross_query),
             packed(dec_gate, dec_up),
         ],
         [enc_proj, dec_proj, cross_proj, enc_down, dec_down],
     )
-    enc_qkv, dec_qkv, enc_gu, cross_qkv, dec_gu = cols
+    small, enc_kvq, dec_kvq, enc_gu, cross_kvq, dec_gu = cols
     enc_wo, dec_wo, cross_wo, enc_wd, dec_wd = rows
-    cross_q, cross_kv = cross_qkv[:, :width], cross_qkv[:, width:]
-    small = jnp.concatenate([enc_norm1, enc_norm2, enc_final, dec_norm1, dec_norm2, dec_norm3, enc_rel, dec_rel])
-    small = lax.all_gather(small, (HG, CORE), axis=0)
-    gains = [small[:, i * share : (i + 1) * share].reshape(1, model).astype(f32) for i in range(6)]
-    g_e1, g_e2, g_ef, g_d1, g_d2, g_d3 = gains
+    small = small.reshape(groups * cores, 16, -1)[:, 0].astype(f32)
+    g_e1, g_e2, g_ef, g_d1, g_d2, g_d3 = [small[:, i * share : (i + 1) * share].reshape(1, model) for i in range(6)]
     rel_len = enc_rel.shape[0]
-    rels = [small[:, 6 * share + i * rel_len : 6 * share + (i + 1) * rel_len].reshape(-1, HEADS).astype(f32) for i in range(2)]
+    rels = [small[:, 6 * share + i * rel_len : 6 * share + (i + 1) * rel_len].reshape(-1, HEADS) for i in range(2)]
 
     def table_of(relative, row):
         onehot = (row[:, None] == jnp.arange(relative.shape[0], dtype=jnp.int32)[None, :]).astype(f32)
@@ -1138,130 +1467,49 @@
     dec_bm = bias_mask(firsts, turned(dec_table), dec_k_ids, dec_q_ids, qpos, block, True)
     cross_bm = bias_mask(firsts, None, enc_k_ids, dec_q_ids, qpos, block, False)
 
-    def spread(own):
-        return lax.all_gather(own, HG, axis=0, tiled=True)
-
-    def collect(partial):
-        return lax.psum_scatter(partial.astype(bf16), HG, scatter_dimension=0, tiled=True).astype(f32)
-
-    def all_keys(kv):
-        every = lax.all_gather(kv, (CORE, SP), axis=0)
-        every = every.reshape(cores, parts, groups, block, -1).transpose(2, 0, 1, 3, 4)
-        return every.reshape(cores * parts * groups * block, -1)
-
-    def own_keys(dkv):
-        cut = dkv.reshape(groups, cores, parts, block, -1).transpose(1, 2, 0, 3, 4)
-        return lax.psum_scatter(cut.reshape(cores * parts * groups * block, -1), (CORE, SP), scatter_dimension=0, tiled=True)
-
-    def attend(n_query, w_query, kv, bm):
-        q = nn(n_query, w_query).astype(bf16)
-        every = all_keys(kv)
-        k, v = every[:, :width], every[:, width:]
-        o, lse = mix(q, k, v, bm)
-        return o, (q, k, v, o, lse)
-
-    def attend_back(dyb, kept, bm, w_proj, biased):
-        q, k, v, o, lse = kept
-        do = nt(dyb, w_proj).astype(bf16)
-        d_proj = tn(o, dyb)
-        got = mix_back(firsts, q, k, v, do, lse, bm, block, biased)
-        dq, dk, dv = got[:3]
-        dkv = own_keys(jnp.concatenate([dk, dv], axis=1)).astype(bf16)
-        return d_proj, dq, dkv, got[3:]
-
-    def normed(x, g):
-        return rms_norm(x, g).astype(bf16)
-
-    def norm_back(x, g, dn):
-        r = lax.rsqrt(jnp.mean(x * x, axis=-1, keepdims=True) + EPSILON)
-        w = dn * g
-        dx = r * w - x * (r * r * r) * jnp.mean(w * x, axis=-1, keepdims=True)
-        return dx, jnp.sum(dn * x * r, axis=0)
-
-    enc_x, dec_x = enc_in.astype(f32), dec_in.astype(f32)
-    en1, dn1 = spread(normed(enc_x, g_e1)), spread(normed(dec_x, g_d1))
-    enc_o, enc_kept = attend(en1, enc_qkv[:, :width], nn(en1, enc_qkv[:, width:]).astype(bf16), enc_bm)
-    dec_o, dec_kept = attend(dn1, dec_qkv[:, :width], nn(dn1, dec_qkv[:, width:]).astype(bf16), dec_bm)
-    ex = enc_x + collect(nn(enc_o, enc_wo))
-    dx = dec_x + collect(nn(dec_o, dec_wo))
-    hidden = enc_wd.shape[0]
-
-    def feed(n, w_gu, w_d):
-        gu = nn(n, w_gu)
-        g, u = gu[:, :hidden], gu[:, hidden:]
-        h = gated(g, u).astype(bf16)
-        return g, u, h, collect(nn(h, w_d))
-
-    def feed_back(n, g, u, h, dyb, w_gu, w_d):
-        dh = nt(dyb, w_d)
-        d_down = tn(h, dyb)
-        _, pullback = jax.vjp(gated, g, u)
-        dg, du = pullback(dh)
-        dgu = jnp.concatenate([dg, du], axis=1).astype(bf16)
-        return tn(n, dgu), d_down, collect(nt(dgu, w_gu))
-
-    en2 = spread(normed(ex, g_e2))
-    e_g, e_u, e_h, y = feed(en2, enc_gu, enc_wd)
-    enc_out = ex + y
-    memory = spread(normed(enc_out, g_ef))
-    dn2 = spread(normed(dx, g_d2))
-    cross_o, cross_kept = attend(dn2, cross_q, nn(memory, cross_kv).astype(bf16), cross_bm)
-    cx = dx + collect(nn(cross_o, cross_wo))
-    dn3 = spread(normed(cx, g_d3))
-    d_g, d_u, d_h, y = feed(dn3, dec_gu, dec_wd)
-    dec_out = cx + y
-
-    d_cot, e_cot = dec_cot.astype(f32), enc_cot.astype(f32)
-    dyb = spread(dec_cot)
-    dw_dgu, dw_ddown, dn = feed_back(dn3, d_g, d_u, d_h, dyb, dec_gu, dec_wd)
-    back, dg_d3 = norm_back(cx, g_d3, dn)
-    grad_dec = d_cot + back
-    dyb = spread(grad_dec.astype(bf16))
-    dw_cproj, dq, dkv, _ = attend_back(dyb, cross_kept, cross_bm, cross_wo, False)
-    dw_cq = tn(dn2, dq)
-    dw_ckv = tn(memory, dkv)
-    dn, dmem = collect(nt(dq, cross_q)), collect(nt(dkv, cross_kv))
-    back, dg_d2 = norm_back(dx, g_d2, dn)
-    grad_dec = grad_dec + back
-    dyb = spread(grad_dec.astype(bf16))
-    dw_dproj, dq, dkv, dec_tab = attend_back(dyb, dec_kept, dec_bm, dec_wo, True)
-    dqkv = jnp.concatenate([dq, dkv], axis=1)
-    dw_dqkv = tn(dn1, dqkv)
-    back, dg_d1 = norm_back(dec_x, g_d1, collect(nt(dqkv, dec_qkv)))
-    dec_in_grad = grad_dec + back
-    back, dg_ef = norm_back(enc_out, g_ef, dmem)
-    grad_enc = e_cot + back
-    dyb = spread(grad_enc.astype(bf16))
-    dw_egu, dw_edown, dn = feed_back(en2, e_g, e_u, e_h, dyb, enc_gu, enc_wd)
-    back, dg_e2 = norm_back(ex, g_e2, dn)
-    grad_enc = grad_enc + back
-    dyb = spread(grad_enc.astype(bf16))
-    dw_eproj, dq, dkv, enc_tab = attend_back(dyb, enc_kept, enc_bm, enc_wo, True)
-    dqkv = jnp.concatenate([dq, dkv], axis=1)
-    dw_eqkv = tn(en1, dqkv)
-    back, dg_e1 = norm_back(enc_x, g_e1, collect(nt(dqkv, enc_qkv)))
-    enc_in_grad = grad_enc + back
+    enc_kept, dec_kept = attend(
+        sizes,
+        2,
+        [(enc_in, g_e1, enc_kvq, enc_wo, enc_bm, None), (dec_in, g_d1, dec_kvq, dec_wo, dec_bm, None)],
+    )
+    ex, dx = enc_kept[0], dec_kept[0]
+    tokens, hidden = groups * block, enc_wd.shape[0]
+    token_f32, token_bf16, gain_f32 = ((block, model), f32), ((block, model), bf16), ((1, model), f32)
+    gu_grad, down_grad = ((model, 2 * hidden), bf16), ((hidden, model), bf16)
+    buffer = (groups, block, model)
+    enc_out, memory, en2 = stage(
+        sizes, 3, feed_forward_kernel, [ex, g_e2, g_ef, enc_gu, enc_wd],
+        [token_f32, token_bf16, ((tokens, model), bf16)], [buffer] * 3, (2, groups),
+    )
+    (cross_kept,) = attend(sizes, 4, [(dx, g_d2, cross_kvq, cross_wo, cross_bm, memory)])
+    cx, memory_all = cross_kept[0], cross_kept[6]
+    dec_out, grad_cx, dg_d3, dw_dgu, dw_ddown = stage(
+        sizes, 5, feed_both_kernel, [cx, dec_cot, g_d3, dec_gu, dec_wd],
+        [token_f32, token_f32, gain_f32, gu_grad, down_grad], [buffer] * 6, (4, groups),
+    )
+
+    grad_dx, dg_d2, dw_ckvq, dw_co, dmem = attend_back(
+        sizes, 6, dx, g_d2, grad_cx, cross_kept, cross_kvq, cross_wo, cross_bm, True
+    )
+    dec_in_grad, dg_d1, dw_dkvq, dw_do, *dec_tab = attend_back(
+        sizes, 7, dec_in, g_d1, grad_dx, dec_kept, dec_kvq, dec_wo, dec_bm, False
+    )
+    grad_ex, dg_e2, dg_ef, dw_egu, dw_edown = stage(
+        sizes, 8, feed_back_kernel, [ex, enc_out, enc_cot, dmem, g_e2, g_ef, en2, enc_gu, enc_wd],
+        [token_f32, gain_f32, gain_f32, gu_grad, down_grad], [buffer] * 3, (2, groups),
+    )
+    enc_in_grad, dg_e1, dw_ekvq, dw_eo, *enc_tab = attend_back(
+        sizes, 9, enc_in, g_e1, grad_ex, enc_kept, enc_kvq, enc_wo, enc_bm, False
+    )
 
     def summed_rows(collective_id, col_grads, row_grads):
-        mine_cols, mine_rows = give_rows(
-            sizes, collective_id, [g.astype(bf16) for g in col_grads], [g.astype(bf16) for g in row_grads]
-        )
+        mine_cols, mine_rows = give_rows(sizes, collective_id, col_grads, row_grads)
         return [lax.psum(g, SP) for g in mine_cols], [lax.psum(g, SP).astype(f32) for g in mine_rows]
 
     def unpacked(whole, pieces):
         each = whole.shape[2] // pieces
         whole = whole.astype(f32)
         return [whole[:, :, i * each : (i + 1) * each].transpose(1, 0, 2).reshape(share, groups * each) for i in range(pieces)]
-
-    (dgu_rows,), (d_wd,) = summed_rows(2, [dw_dgu], [dw_ddown])
-    (cross_rows,), (c_wo,) = summed_rows(3, [jnp.concatenate([dw_cq, dw_ckv], axis=1)], [dw_cproj])
-    (egu_rows, dqkv_rows), (d_wo, e_wd) = summed_rows(4, [dw_egu, dw_dqkv], [dw_dproj, dw_edown])
-    (eqkv_rows,), (e_wo,) = summed_rows(5, [dw_eqkv], [dw_eproj])
-    e_wq, e_wk, e_wv = unpacked(eqkv_rows, 3)
-    e_wg, e_wu = unpacked(egu_rows, 2)
-    d_wq, d_wk, d_wv = unpacked(dqkv_rows, 3)
-    c_wq, c_wk, c_wv = unpacked(cross_rows, 3)
-    d_wg, d_wu = unpacked(dgu_rows, 2)
 
     def fold(tab, onehot):
         strips, edges = tab
@@ -1283,9 +1531,20 @@
         return jnp.dot(onehot.T, full.T, precision=HIGHEST).reshape(-1)
 
     small_grads = [dg_e1, dg_e2, dg_ef, dg_d1, dg_d2, dg_d3, fold(enc_tab, enc_onehot), fold(dec_tab, dec_onehot)]
-    packed = jnp.concatenate([v.reshape(groups * cores, -1) for v in small_grads], axis=1)
-    summed = lax.psum(packed, (HG, CORE, SP))
-    own = lax.dynamic_index_in_dim(summed, my_group * cores + my_core, 0, False)
+    packed_small = jnp.concatenate([v.reshape(groups * cores, 1, -1) for v in small_grads], axis=2)
+    packed_small = jnp.broadcast_to(packed_small, (groups * cores, 16, packed_small.shape[2]))
+    packed_small = packed_small.reshape(groups * cores * 16, -1).astype(bf16)
+
+    (dgu_rows,), (d_wd,) = summed_rows(10, [dw_dgu], [dw_ddown])
+    (cross_rows,), (c_wo,) = summed_rows(11, [dw_ckvq], [dw_co])
+    (dkvq_rows, egu_rows), (d_wo, e_wd) = summed_rows(12, [dw_dkvq, dw_egu], [dw_do, dw_edown])
+    (ekvq_rows, small_rows), (e_wo,) = summed_rows(13, [dw_ekvq, packed_small], [dw_eo])
+    e_wk, e_wv, e_wq = unpacked(ekvq_rows, 3)
+    e_wg, e_wu = unpacked(egu_rows, 2)
+    d_wk, d_wv, d_wq = unpacked(dkvq_rows, 3)
+    c_wk, c_wv, c_wq = unpacked(cross_rows, 3)
+    d_wg, d_wu = unpacked(dgu_rows, 2)
+    own = jnp.sum(small_rows[:, 0].astype(f32), axis=0)
     s = [own[i * share : (i + 1) * share] for i in range(6)]
     e_rel, d_rel = own[6 * share : 6 * share + rel_len], own[6 * share + rel_len :]
     return (

time: 908 us -> 731 us (0.81)
  Pallas kernels: 215 us -> 475 us
  blocking collectives: 176 us -> 0 us
  waiting for transfers between devices: 321 us -> 169 us
  matrix products: 54.1 us -> 0.92 us
  other arithmetic: 48.3 us -> 15 us
  local copies, waits for them, and re-layouts: 64.6 us -> 50.9 us
    pallas_call x6 -> x8, Pallas kernels: 69.1 us -> 327 us  [stage(): pl.pallas_call(functools.partial(kernel, sizes), out_shape=tuple((jax.Sha...]
    reduce_scatter x14 -> x0, waiting for transfers between devices: 177 us -> none  [the longest x11 132 us: collect(): lax.psum_scatter(partial.astype(bf16), HG, scatter_dimension=0, tiled=True)]
    all_gather x11 -> x0, blocking collectives: 106 us -> none  [spread(): return lax.all_gather(own, HG, axis=0, tiled=True)]
    psum x1, waiting for transfers between devices: 115 us -> 169 us  [summed_rows(): lax.psum(g, SP)]
    dot_general x35 -> x0, matrix products: 53.1 us -> none  [the longest x13 22.7 us: nn(): return jnp.dot(left, right, preferred_element_type=jnp.float32)]
    psum x1 -> x0, blocking collectives: 44.3 us -> none  [fast_device(): summed = lax.psum(packed, (HG, CORE, SP))]
    all_gather x3 -> x0, waiting for transfers between devices: 28.5 us -> none  [all_keys(): every = lax.all_gather(kv, (CORE, SP), axis=0)]
    unnamed x1 -> x0, blocking collectives: 25.5 us -> none
  transfers between devices with their start and end apart: 18 -> 1, of which waited for: 14 -> 1; matrix products, arithmetic and copies ran while one was open for 11% -> 0% of each run, Pallas kernels for 13% -> 0%
where the time goes in v3:
time: 731 us; the launch traced here: 727 us
  Pallas kernels  475 us (65%)
  waiting for transfers between devices  169 us (23%)
  local copies, waits for them, and re-layouts  50.9 us (7%)
  between operations  15.4 us (2%)
  other arithmetic  15 us (2%)
    pallas_call x8, Pallas kernels, stage(): pl.pallas_call(functools.partial(kernel, sizes), out_shape=tuple((jax.Sha...  327 us
    psum x1, waiting for transfers between devices, summed_rows(): lax.psum(g, SP)  169 us
    pallas_call x1, Pallas kernels, recut(): pl.pallas_call(functools.partial(recut_kernel, sizes, (cols, rows)), out_...  67.2 us
    pallas_call x4, Pallas kernels, give_rows(): pl.pallas_call(functools.partial(give_rows_kernel, sizes, (cols, rows)),...  66.9 us
  transfers between devices with their start and end apart: 1, of which 1 were waited for; matrix products, arithmetic and copies ran while one was open for 0% of the time, Pallas kernels for 0%

profile of v3, /device:TPU:0, one launch (start us, length us, event | category | flops | bytes accessed | tf_op | source)
XLA Modules:
  0.0 726.6 jit_solution(16987595834945311790)
XLA Ops:
  7.3 1.2 reshape.421
  8.6 1.1 reshape.422
  11.8 1.0 maximum_bitcast_fusion.refs_3_
  13.0 1.0 maximum_bitcast_fusion.1.refs_5_
  15.0 1.3 maximum_bitcast_fusion.2
  17.0 67.2 %shard_map.544 = (bf16[4,2,16,672]{3,2,1,0:T(8,128)(2,1)}, bf16[4,2,96,576]{3,2,1,0:T(8,128)(2,1)}, bf16[4,2,96,576]{3,2,1,0:T(8,128)(2,1)}, bf16[4,2,96,1024]{3...) custom-call(bf16[4,16,672]{2,1,0:T(8,128)(2,1)} %broadcast_in_dim.24, ...), custom_call_target="tpu_custom_call" | custom-call | tf_op jit(solution)/shard_map/pallas_call | solution.py:822
  86.3 1.1 compare_reduce_fusion
  89.1 1.3 copy.121.refs_2_
  91.6 1.4 copy.120.refs_2_.refs_1_
  98.1 2.6 shard_map.549.refs_4_.refs_10_
  100.7 6.0 shard_map.546.refs_9_.refs_10_
  107.3 5.6 shard_map.545.refs_4_.refs_10_
  112.9 70.2 %shard_map.547 = (f32[64,768]{1,0:T(8,128)}, bf16[256,768]{1,0:T(8,128)(2,1)}, bf16[256,192]{1,0:T(8,128)(2,1)}, bf16[4,2,4,64,384]{4,3,2,1,0:T(8,128)(2,1)}, bf...) custom-call(bf16[64,768]{1,0:T(8,128)(2,1)} %refs_0_.4, ...), custom_call_target="tpu_custom_call" | custom-call | tf_op jit(solution)/shard_map/pallas_call | solution.py:1053
  183.1 17.2 %shard_map.548 = (f32[64,768]{1,0:T(8,128)}, bf16[64,768]{1,0:T(8,128)(2,1)}, bf16[256,768]{1,0:T(8,128)(2,1)}) custom-call(f32[64,768]{1,0:T(8,128)} %get-tuple-element.154.x_ref, f32[1,768]{1,0:T(1,128)} %reshape.446.gain_ref, f32[1,768]{1,0:T(1,128)} %reshape.447.final_ref, bf16[768,1024]{1,0:T(8,128)(2,1)} %bitcast.102, bf16[512,768]{1,0:T(8,128)(2,1)} %bitcast.110), custom_call_target="tpu_custom_call" | custom-call | tf_op jit(solution)/shard_map/pallas_call | solution.py:1053
  200.3 42.9 %shard_map.550 = (f32[64,768]{1,0:T(8,128)}, bf16[256,768]{1,0:T(8,128)(2,1)}, bf16[256,192]{1,0:T(8,128)(2,1)}, bf16[4,2,4,64,384]{4,3,2,1,0:T(8,128)(2,1)}, bf...) custom-call(f32[64,768]{1,0:T(8,128)} %get-tuple-element.158.refs_0_, ...), custom_call_target="tpu_custom_call" | custom-call | tf_op jit(solution)/shard_map/pallas_call | solution.py:1053
  243.2 28.0 %shard_map.551 = (f32[64,768]{1,0:T(8,128)}, f32[64,768]{1,0:T(8,128)}, f32[1,768]{1,0:T(1,128)}, bf16[768,1024]{1,0:T(8,128)(2,1)}, bf16[512,768]{1,0:T(8,128)(2,1)}) custom-call(f32[64,768]{1,0:T(8,128)} %get-tuple-element.162.x_ref, bf16[64,768]{1,0:T(8,128)(2,1)} %cot_ref.2, f32[1,768]{1,0:T(1,128)} %reshape.453.gain_ref, bf16[768,1024]{1,0:T(8,128)(2,1)} %bitcast.116, ...), custom_call_target="tpu_custom_call" | custom-call | tf_op jit(solution)/shard_map/pallas_call | solution.py:1053
  271.2 47.8 %shard_map.552 = (f32[64,768]{1,0:T(8,128)}, f32[1,768]{1,0:T(1,128)}, bf16[768,576]{1,0:T(8,128)(2,1)}, bf16[192,768]{1,0:T(8,128)(2,1)}, f32[64,768]{1,0:T(8,128)}) custom-call(f32[64,768]{1,0:T(8,128)} %get-tuple-element.158.refs_0_, f32[1,768]{1,0:T(1,128)} %reshape.450.refs_1_, f32[64,768]{1,0:T(8,128)} %get-tuple-element.166.refs_2_, ...), custom_call_target="tpu_custom_call" | custom-call | tf_op jit(solution)/shard_map/pallas_call | solution.py:1053
  318.9 52.6 %shard_map.555 = (f32[64,768]{1,0:T(8,128)}, f32[1,768]{1,0:T(1,128)}, bf16[768,576]{1,0:T(8,128)(2,1)}, bf16[192,768]{1,0:T(8,128)(2,1)}, f32[3,320,64]{2,1,0:T(8,128)}, /*index=5*/f32[6,256]{1,0:T(8,128)}) custom-call(bf16[64,768]{1,0:T(8,128)(2,1)} %refs_0_.5, f32[1,768]{1,0:T(1,128)} %reshape.440.refs_6_.refs_1_, f32[64,768]{1,0:T(8,128)} %get-tuple-element.182.refs_2_, ...), custom_call_target="tpu_custom_call" | custom-call | tf_op jit(solution)/shard_map/pallas_call | solution.py:1053
  371.5 4.6 rev.15
  377.3 18.9 %shard_map.553 = (f32[64,768]{1,0:T(8,128)}, f32[1,768]{1,0:T(1,128)}, f32[1,768]{1,0:T(1,128)}, bf16[768,1024]{1,0:T(8,128)(2,1)}, bf16[512,768]{1,0:T(8,128)(2,1)}) custom-call(f32[64,768]{1,0:T(8,128)} %get-tuple-element.154.x_ref, f32[64,768]{1,0:T(8,128)} %get-tuple-element.308.y_ref, bf16[64,768]{1,0:T(8,128)(2,1)} %cot_ref.3, ...), custom_call_target="tpu_custom_call" | custom-call | tf_op jit(solution)/shard_map/pallas_call | solution.py:1053
  396.2 49.4 %shard_map.554 = (f32[64,768]{1,0:T(8,128)}, f32[1,768]{1,0:T(1,128)}, bf16[768,576]{1,0:T(8,128)(2,1)}, bf16[192,768]{1,0:T(8,128)(2,1)}, f32[3,320,64]{2,1,0:T(8,128)}, /*index=5*/f32[6,256]{1,0:T(8,128)}) custom-call(bf16[64,768]{1,0:T(8,128)(2,1)} %refs_0_.4, f32[1,768]{1,0:T(1,128)} %reshape.434.refs_1_, f32[64,768]{1,0:T(8,128)} %get-tuple-element.175.refs_2_, ...), custom_call_target="tpu_custom_call" | custom-call | tf_op jit(solution)/shard_map/pallas_call | solution.py:1053
  445.6 4.9 rev.14
  456.0 17.9 %shard_map.559 = (bf16[4,96,1024]{2,1,0:T(8,128)(2,1)}, bf16[256,768]{1,0:T(8,128)(2,1)}) custom-call(bf16[4,2,96,1024]{3,2,1,0:T(8,128)(2,1)} %bitcast.115, bf16[2,256,768]{2,1,0:T(8,128)(2,1)} %bitcast.134), custom_call_target="tpu_custom_call" | custom-call | tf_op jit(solution)/shard_map/pallas_call | solution.py:900
  474.0 12.1 %shard_map.558 = (bf16[4,96,576]{2,1,0:T(8,128)(2,1)}, bf16[96,768]{1,0:T(8,128)(2,1)}) custom-call(bf16[4,2,96,576]{3,2,1,0:T(8,128)(2,1)} %bitcast.126, bf16[2,96,768]{2,1,0:T(8,128)(2,1)} %bitcast.140), custom_call_target="tpu_custom_call" | custom-call | tf_op jit(solution)/shard_map/pallas_call | solution.py:900
  486.9 14.2 %shard_map.556 = (bf16[4,96,576]{2,1,0:T(8,128)(2,1)}, bf16[4,16,672]{2,1,0:T(8,128)(2,1)}, bf16[96,768]{1,0:T(8,128)(2,1)}) custom-call(bf16[4,2,96,576]{3,2,1,0:T(8,128)(2,1)} %bitcast.127, bf16[4,2,16,672]{3,2,1,0:T(8,128)(2,1)} %broadcast_in_dim.60.refs_1_, bf16[2,96,768]{2,1,0:T(8,128)(2,1)} %bitcast.141), custom_call_target="tpu_custom_call" | custom-call | tf_op jit(solution)/shard_map/pallas_call | solution.py:900
  501.1 22.7 %shard_map.557 = (bf16[4,96,576]{2,1,0:T(8,128)(2,1)}, bf16[4,96,1024]{2,1,0:T(8,128)(2,1)}, bf16[96,768]{1,0:T(8,128)(2,1)}, bf16[256,768]{1,0:T(8,128)(2,1)}) custom-call(bf16[4,2,96,576]{3,2,1,0:T(8,128)(2,1)} %bitcast.125, bf16[4,2,96,1024]{3,2,1,0:T(8,128)(2,1)} %bitcast.114, bf16[2,96,768]{2,1,0:T(8,128)(2,1)} %bitcast.139, bf16[2,256,768]{2,1,0:T(8,128)(2,1)} %bitcast.128), custom_call_target="tpu_custom_call" | custom-call | tf_op jit(solution)/shard_map/pallas_call | solution.py:900
  523.8 169.2 %all-reduce.7.cloned.1.call-done = (bf16[4,16,672]{2,1,0:T(8,128)(2,1)}, bf16[4,96,576]{2,1,0:T(8,128)(2,1)}, bf16[96,768]{1,0:T(8,128)(2,1)}, bf16[4,96,1024]{2...) async-done(((bf16[4,16,672]{2,1,0:T(8,128)(2,1)}, ...) | async-done | bytes 4214800 | tf_op jit(solution)/shard_map/psum | solution.py:1507
  695.0 1.3 convert_element_type.52
  703.6 1.0 reshape.466
  705.1 1.0 reshape.473
  706.3 1.0 reshape.474
  707.5 1.0 reshape.475
  (246 shorter events, 42.8 us)
Async XLA Ops:
  7.2 2.5 copy-start.17
  7.2 2.8 copy-start.18
  7.2 3.0 copy-start.19
  7.2 685.8 %all-reduce.7.cloned.1.call-start = ((), (), s32[]{:S(2)}) async-start(), calls=%async_computation | async-start | bytes 8749056 | tf_op jit(solution)/shard_map/psum | solution.py:1507
  7.3 81.5 %copy-start.29 = (s32[4]{0:T(128)}, s32[4]{0:T(128)S(1)}, u32[]{:S(2)}) copy-start(s32[4]{0:T(128)S(1)} %add_multiply_fusion.refs_0_) | copy-start | bytes 52
  14.0 2.3 copy-start.40
  14.0 2.3 copy-start.41
  14.0 2.3 copy-start.42
  14.0 2.3 copy-start.43
  14.0 2.3 copy-start.44
  17.0 68.3 %copy-start.30 = (s32[2,257]{1,0:T(2,128)S(1)}, s32[2,257]{1,0:T(2,128)}, u32[]{:S(2)}) copy-start(s32[2,257]{1,0:T(2,128)} %param.47) | copy-start | bytes 6172
  17.0 71.0 %copy-start.25 = (s32[2048]{0:T(1024)S(1)}, s32[2048]{0:T(1024)}, u32[]{:S(2)}) copy-start(s32[2048]{0:T(1024)} %param.45) | copy-start | bytes 24580
  17.0 71.0 %copy-start.24 = (s32[2048]{0:T(1024)S(1)}, s32[2048]{0:T(1024)}, u32[]{:S(2)}) copy-start(s32[2048]{0:T(1024)} %param.46) | copy-start | bytes 24580
  89.0 9.1 %copy-start.26 = (s32[1,256]{1,0:T(1,128)}, s32[1,256]{1,0:T(1,128)S(1)}, u32[]{:S(2)}) copy-start(s32[1,256]{1,0:T(1,128)S(1)} %add.150.refs_5_.refs_4_) | copy-start | bytes 3076
  450.4 3.1 copy-start.28
  450.4 4.9 copy-start.33
  450.5 5.0 copy-start.36
  450.5 5.1 copy-start.35
  450.5 5.2 copy-start.34
  450.5 5.3 copy-start.32
  450.5 5.4 copy-start.31
  702.1 2.5 copy-start.3
  706.0 2.5 copy-start.2
  710.0 2.5 copy-start.10
  710.2 3.2 copy-start.9
  711.5 2.9 copy-start.16
  712.4 2.6 copy-start.15
  712.5 3.4 copy-start.14
  712.5 4.1 copy-start
  713.4 3.8 copy-start.11
  713.4 4.5 copy-start.13
  713.4 5.2 copy-start.12
  (14 other events, 21.5 us)
Sparse Core Ops, SparseCore 0:
  523.9 169.0 all-reduce.6

commit v4 on v0

--- a/solution.py
+++ b/solution.py
@@ -1,8 +1,13 @@
+import functools
 import math
 
 import jax
 import jax.numpy as jnp
+import numpy as np
 from jax import lax
+from jax.experimental import pallas as pl
+from jax.experimental.pallas import tpu as pltpu
+from jax.sharding import Mesh
 from jax.sharding import PartitionSpec as P
 
 HEADS = 12
@@ -627,7 +632,1094 @@
     return (enc_result, dec_result, grad_enc, grad_dec) + tuple(reduced)
 
 
-def solution(mesh):
+HG, CORE, SP = "hg", "core", "sp"
+BLOCK_PAD = 128
+VMEM_BYTES = 60 << 20
+
+
+def nt(left, right):
+    return lax.dot_general(left, right, (((1,), (1,)), ((), ())), preferred_element_type=jnp.float32)
+
+
+def tn(left, right):
+    return lax.dot_general(left, right, (((0,), (0,)), ((), ())), preferred_element_type=jnp.float32)
+
+
+def nn(left, right):
+    return jnp.dot(left, right, preferred_element_type=jnp.float32)
+
+
+def low(value):
+    return value.astype(jnp.bfloat16)
+
+
+def identity(size):
+    rows = lax.broadcasted_iota(jnp.int32, (size, size), 0)
+    cols = lax.broadcasted_iota(jnp.int32, (size, size), 1)
+    return low(jnp.where(rows == cols, 1.0, 0.0))
+
+
+def only_lanes(array, first, count):
+    lanes = lax.broadcasted_iota(jnp.int32, array.shape, 1)
+    return jnp.where((lanes >= first) & (lanes < first + count), array, jnp.zeros_like(array))
+
+
+def gelu_and_slope(v):
+    scale, cubic = math.sqrt(2.0 / math.pi), 0.044715
+    t = jnp.tanh(scale * (v + cubic * v * v * v))
+    return 0.5 * v * (1.0 + t), 0.5 * (1.0 + t) + 0.5 * v * (1.0 - t * t) * scale * (1.0 + 3.0 * cubic * v * v)
+
+
+def norm_back(x, g, dn):
+    r = lax.rsqrt(jnp.mean(x * x, axis=-1, keepdims=True) + EPSILON)
+    w = dn * g
+    dx = r * w - x * (r * r * r) * jnp.mean(w * x, axis=-1, keepdims=True)
+    return dx, jnp.sum(dn * x * r, axis=0, keepdims=True)
+
+
+def send(src, dst, send_sem, recv_sem, to):
+    copy = pltpu.make_async_remote_copy(
+        src_ref=src, dst_ref=dst, send_sem=send_sem, recv_sem=recv_sem, device_id=to, device_id_type=pl.DeviceIdType.MESH
+    )
+    copy.start()
+    return copy
+
+
+def arrived(dst, send_sem, recv_sem, to):
+    pltpu.make_async_remote_copy(
+        src_ref=dst, dst_ref=dst, send_sem=send_sem, recv_sem=recv_sem, device_id=to, device_id_type=pl.DeviceIdType.MESH
+    ).wait_recv()
+
+
+class Place:
+    def __init__(self, groups, cores, parts):
+        self.groups, self.cores, self.parts = groups, cores, parts
+        self.group, self.core, self.part = lax.axis_index(HG), lax.axis_index(CORE), lax.axis_index(SP)
+
+    def ahead(self, step):
+        return lax.rem(self.group + step, self.groups)
+
+    def behind(self, step):
+        return lax.rem(self.group + self.groups - step, self.groups)
+
+    def chip(self, group):
+        return (group, self.core, self.part)
+
+    def sibling(self):
+        return (self.group, 1 - self.core, self.part)
+
+    def plane(self, step):
+        return lax.rem(self.part + step, self.parts)
+
+    def plane_behind(self, step):
+        return lax.rem(self.part + self.parts - step, self.parts)
+
+    def at_plane(self, part):
+        return (self.group, self.core, part)
+
+    def first_token(self, number, block):
+        return pl.multiple_of(((self.cores * number + self.core) * self.parts + self.part) * block, block)
+
+    def greet(self, planes=False):
+        barrier = pltpu.get_barrier_semaphore()
+        partners = [self.chip(self.ahead(step)) for step in range(1, self.groups)] + [self.sibling()]
+        if planes:
+            partners += [self.at_plane(self.plane(step)) for step in range(1, self.parts)]
+        for partner in partners:
+            pl.semaphore_signal(barrier, inc=1, device_id=partner, device_id_type=pl.DeviceIdType.MESH)
+        pl.semaphore_wait(barrier, len(partners))
+
+
+def spread_start(place, buf, sent, got):
+    mine = buf.at[place.group]
+    return [
+        send(mine, mine, sent.at[step], got.at[step], place.chip(place.ahead(step))) for step in range(1, place.groups)
+    ]
+
+
+def spread_wait(place, buf, sent, got):
+    for step in range(1, place.groups):
+        source = place.behind(step)
+        arrived(buf.at[source], sent.at[step], got.at[step], place.chip(source))
+
+
+def collect_start(place, partial, out_buf, in_buf, sent, got):
+    out_buf[...] = low(partial).reshape(out_buf.shape)
+    pending = []
+    for step in range(1, place.groups):
+        to = place.ahead(step)
+        pending.append(send(out_buf.at[to], in_buf.at[place.group], sent.at[step], got.at[step], place.chip(to)))
+    return pending
+
+
+def collect_wait(place, out_buf, in_buf, sent, got):
+    total = out_buf[place.group].astype(jnp.float32)
+    for step in range(1, place.groups):
+        source = place.behind(step)
+        arrived(in_buf.at[source], sent.at[step], got.at[step], place.chip(source))
+        total = total + in_buf[source].astype(jnp.float32)
+    return total
+
+
+def all_rows(buf):
+    return buf[...].reshape(buf.shape[0] * buf.shape[1], buf.shape[2])
+
+
+DMA = pltpu.SemaphoreType.DMA
+IN_VMEM = pl.BlockSpec(memory_space=pltpu.VMEM)
+ANYWHERE = pl.BlockSpec(memory_space=pl.ANY)
+
+
+class Recut:
+    def __init__(self, sizes, col_packs, row_packs):
+        groups, cores, _ = sizes
+        self.cols, self.rows = len(col_packs), len(row_packs)
+        self.operands = list(col_packs) + list(row_packs)
+        self.in_specs = [ANYWHERE] * len(self.operands)
+        self.outs = [((groups, cores) + w.shape[1:], w.dtype) for w in col_packs]
+        self.outs += [((cores,) + w.shape, w.dtype) for w in row_packs]
+        self.out_specs = [ANYWHERE] * len(self.outs)
+        cols = (self.cols, groups)
+        self.scratch = [DMA(cols)] * 4 + [DMA((self.rows,))] * 2 + [DMA((self.cols + self.rows,))]
+
+    def bind(self, ins, outs, scratch):
+        self.col_refs, self.row_refs = ins[: self.cols], ins[self.cols :]
+        self.col_outs, self.row_outs = outs[: self.cols], outs[self.cols :]
+        self.sems = scratch
+        self.pending, self.copies = [], []
+
+    def begin(self, place):
+        sent, got, relay_sent, relay_got, pair_sent, pair_got, local = self.sems
+        group, core = place.group, place.core
+        for index, (ref, out) in enumerate(zip(self.col_refs, self.col_outs)):
+            slot = out.at[group, core]
+            for step in range(1, place.groups):
+                to = place.ahead(step)
+                self.pending.append(send(ref.at[to], slot, sent.at[index, step], got.at[index, step], place.chip(to)))
+            self.pending.append(send(ref.at[group], slot, relay_sent.at[index, 0], relay_got.at[index, 0], place.sibling()))
+            self.copies.append(pltpu.make_async_copy(ref.at[group], slot, local.at[index]))
+        for index, (ref, out) in enumerate(zip(self.row_refs, self.row_outs)):
+            slot = out.at[core]
+            self.pending.append(send(ref, slot, pair_sent.at[index], pair_got.at[index], place.sibling()))
+            self.copies.append(pltpu.make_async_copy(ref, slot, local.at[self.cols + index]))
+        for copy in self.copies:
+            copy.start()
+
+    def middle(self, place):
+        sent, got, relay_sent, relay_got = self.sems[:4]
+        for index, out in enumerate(self.col_outs):
+            for step in range(1, place.groups):
+                source = place.behind(step)
+                slot = out.at[source, place.core]
+                arrived(slot, sent.at[index, step], got.at[index, step], place.chip(source))
+                self.pending.append(
+                    send(slot, slot, relay_sent.at[index, step], relay_got.at[index, step], place.sibling())
+                )
+
+    def end(self, place):
+        _, _, relay_sent, relay_got, pair_sent, pair_got, _ = self.sems
+        for index, out in enumerate(self.col_outs):
+            for step in range(place.groups):
+                slot = out.at[place.behind(step), 1 - place.core]
+                arrived(slot, relay_sent.at[index, step], relay_got.at[index, step], place.sibling())
+        for index, out in enumerate(self.row_outs):
+            arrived(out.at[1 - place.core], pair_sent.at[index], pair_got.at[index], place.sibling())
+        for copy in self.copies:
+            copy.wait()
+        for copy in self.pending:
+            copy.wait_send()
+
+    def result(self, got):
+        cols = [w.reshape(w.shape[0] * w.shape[1] * w.shape[2], w.shape[3]) for w in got[: self.cols]]
+        return cols, [w.reshape(w.shape[0] * w.shape[1], w.shape[2]) for w in got[self.cols :]]
+
+
+class GiveRows:
+    def __init__(self, sizes, col_grads, row_grads):
+        groups, cores, _ = sizes
+        self.cols, self.rows = len(col_grads), len(row_grads)
+        col_in = [w.reshape(groups, cores, w.shape[0] // (groups * cores), w.shape[1]) for w in col_grads]
+        row_in = [w.reshape(cores, w.shape[0] // cores, w.shape[1]) for w in row_grads]
+        self.operands = col_in + row_in
+        self.in_specs = [IN_VMEM] * len(self.operands)
+        own = [(groups,) + w.shape[2:] for w in col_in] + [(1,) + w.shape[1:] for w in row_in]
+        self.outs = [(shape, jnp.bfloat16) for shape in own]
+        self.out_specs = [IN_VMEM] * len(self.outs)
+        self.scratch = [pltpu.VMEM(shape, jnp.bfloat16) for shape in own + own[: self.cols]]
+        self.scratch += [DMA((self.cols, groups))] * 4 + [DMA((self.rows,))] * 2
+
+    def bind(self, ins, outs, scratch):
+        self.col_refs, self.row_refs = ins[: self.cols], ins[self.cols :]
+        self.col_outs, self.row_outs = outs[: self.cols], outs[self.cols :]
+        self.col_sibs, scratch = scratch[: self.cols], scratch[self.cols :]
+        self.row_sibs, scratch = scratch[: self.rows], scratch[self.rows :]
+        self.col_sums, self.sems = scratch[: self.cols], scratch[self.cols :]
+        self.pending = []
+
+    def begin(self, place):
+        _, _, pair_sent, pair_got, row_sent, row_got = self.sems
+        other = 1 - place.core
+        for index, (ref, sib) in enumerate(zip(self.col_refs, self.col_sibs)):
+            for step in range(place.groups):
+                to = place.ahead(step)
+                self.pending.append(
+                    send(
+                        ref.at[to, other], sib.at[to],
+                        pair_sent.at[index, step], pair_got.at[index, step], place.sibling(),
+                    )
+                )
+        for index, (ref, sib) in enumerate(zip(self.row_refs, self.row_sibs)):
+            self.pending.append(send(ref.at[other], sib.at[0], row_sent.at[index], row_got.at[index], place.sibling()))
+
+    def middle(self, place):
+        sent, got, pair_sent, pair_got, row_sent, row_got = self.sems
+        core = place.core
+        for index, (ref, sib) in enumerate(zip(self.col_refs, self.col_sibs)):
+            out, sums = self.col_outs[index], self.col_sums[index]
+            for step in list(range(1, place.groups)) + [0]:
+                to = place.ahead(step)
+                arrived(sib.at[to], pair_sent.at[index, step], pair_got.at[index, step], place.sibling())
+                both = low(ref[to, core].astype(jnp.float32) + sib[to].astype(jnp.float32))
+                if step:
+                    sums[to] = both
+                    self.pending.append(
+                        send(sums.at[to], out.at[place.group], sent.at[index, step], got.at[index, step], place.chip(to))
+                    )
+                else:
+                    out[place.group] = both
+        for index, (ref, sib) in enumerate(zip(self.row_refs, self.row_sibs)):
+            arrived(sib.at[0], row_sent.at[index], row_got.at[index], place.sibling())
+            self.row_outs[index][0] = low(ref[core].astype(jnp.float32) + sib[0].astype(jnp.float32))
+
+    def end(self, place):
+        sent, got = self.sems[:2]
+        for index, out in enumerate(self.col_outs):
+            for step in range(1, place.groups):
+                source = place.behind(step)
+                arrived(out.at[source], sent.at[index, step], got.at[index, step], place.chip(source))
+        for copy in self.pending:
+            copy.wait_send()
+
+    def result(self, got):
+        return list(got)
+
+
+class FoldPlanes:
+    def __init__(self, arrays):
+        self.operands = list(arrays)
+        self.in_specs = [IN_VMEM] * len(arrays)
+        self.outs = [(w.shape, jnp.bfloat16) for w in arrays]
+        self.out_specs = [IN_VMEM] * len(arrays)
+        self.pieces = [(index, piece) for index, w in enumerate(arrays) for piece in range(w.shape[0])]
+        self.scratch = [pltpu.VMEM(w.shape, jnp.bfloat16) for _ in range(3) for w in arrays] + [DMA((len(self.pieces),))] * 6
+
+    def bind(self, ins, outs, scratch):
+        count = len(self.outs)
+        self.ins, self.totals = ins, outs
+        self.inner, self.sums, self.across = (scratch[i * count : (i + 1) * count] for i in range(3))
+        self.sems = scratch[3 * count :]
+
+    def copy(self, hop, number, src, dst, to):
+        return pltpu.make_async_remote_copy(
+            src_ref=src, dst_ref=dst, send_sem=self.sems[2 * hop].at[number], recv_sem=self.sems[2 * hop + 1].at[number],
+            device_id=to, device_id_type=pl.DeviceIdType.MESH,
+        )
+
+    def hops(self, place, number):
+        index, piece = self.pieces[number]
+        part = place.part
+        inward, across, outward = (place.at_plane(p) for p in (1 + part // 3, 3 - part, 3 * (part - 1)))
+        ref, inner, sums = self.ins[index].at[piece], self.inner[index].at[piece], self.sums[index].at[piece]
+        other, total = self.across[index].at[piece], self.totals[index].at[piece]
+        return (ref, inner, inward), (sums, other, across), (total, total, outward)
+
+    def roles(self, place):
+        middle = (place.part == 1) | (place.part == 2)
+        return pl.when(middle), pl.when(jnp.logical_not(middle))
+
+    def start(self, place, numbers):
+        @self.roles(place)[1]
+        def _():
+            for number in numbers:
+                self.copy(0, number, *self.hops(place, number)[0]).start()
+
+    def add_inner(self, place, number):
+        inward, across, _ = self.hops(place, number)
+        self.copy(0, number, *inward).wait_recv()
+        across[0][...] = low(inward[0][...].astype(jnp.float32) + inward[1][...].astype(jnp.float32))
+        self.copy(1, number, *across).start()
+
+    def add_across(self, place, number):
+        _, across, outward = self.hops(place, number)
+        self.copy(1, number, *across).wait_recv()
+        outward[0][...] = low(across[0][...].astype(jnp.float32) + across[1][...].astype(jnp.float32))
+        self.copy(2, number, *outward).start()
+
+    def serve(self, place, inner, across):
+        @self.roles(place)[0]
+        def _():
+            inners, others = list(inner), list(across)
+            while inners or others:
+                if inners:
+                    self.add_inner(place, inners.pop(0))
+                if others and (not inners or len(inners) < len(others) + 2):
+                    self.add_across(place, others.pop(0))
+
+    def end(self, place):
+        in_middle, at_end = self.roles(place)
+
+        @at_end
+        def _():
+            for number in range(len(self.pieces)):
+                inward, _, outward = self.hops(place, number)
+                self.copy(0, number, *inward).wait_send()
+                self.copy(2, number, *outward).wait_recv()
+
+        @in_middle
+        def _():
+            for number in range(len(self.pieces)):
+                _, across, outward = self.hops(place, number)
+                self.copy(1, number, *across).wait_send()
+                self.copy(2, number, *outward).wait_send()
+
+    def result(self, got):
+        return list(got)
+
+
+def finish_kernel(sizes, give, fold, before, *refs):
+    refs = list(refs)
+
+    def take(count):
+        taken, refs[:] = refs[:count], refs[count:]
+        return taken
+
+    give_ins, ready = take(len(give.operands)), take(before)
+    totals = take(len(fold.outs))
+    given = take(len(give.outs))
+    give.bind(give_ins, given, take(len(give.scratch)))
+    fold.bind(ready + given, totals, take(len(fold.scratch)))
+    place = Place(*sizes)
+    place.greet(planes=True)
+    early = [n for n, (index, _) in enumerate(fold.pieces) if index < before]
+    last = [n for n, (index, _) in enumerate(fold.pieces) if index >= before]
+    first = early[: len(early) // 2]
+    give.begin(place)
+    fold.start(place, early)
+    give.middle(place)
+    fold.serve(place, first, [])
+    give.end(place)
+    fold.start(place, last)
+    fold.serve(place, early[len(first) :] + last, early + last)
+    fold.end(place)
+
+
+def finish(sizes, collective_id, give, arrays):
+    fold = FoldPlanes(list(arrays) + [jax.ShapeDtypeStruct(shape, dtype) for shape, dtype in give.outs])
+    count = len(arrays)
+    got = pl.pallas_call(
+        functools.partial(finish_kernel, sizes, give, fold, count),
+        out_shape=tuple(jax.ShapeDtypeStruct(shape, dtype) for shape, dtype in fold.outs),
+        in_specs=[IN_VMEM] * (len(give.operands) + count),
+        out_specs=(IN_VMEM,) * len(fold.outs),
+        scratch_shapes=[pltpu.VMEM(shape, dtype) for shape, dtype in give.outs] + give.scratch + fold.scratch,
+        compiler_params=pltpu.CompilerParams(collective_id=collective_id, has_side_effects=True, vmem_limit_bytes=VMEM_BYTES),
+        cost_estimate=pl.CostEstimate(flops=20_000_000_000, bytes_accessed=10_000_000, transcendentals=0),
+    )(*give.operands, *arrays)
+    return list(got[count:]), list(got[:count])
+
+
+def stage(sizes, collective_id, kernel, operands, outs, scratch, copies, job=None):
+    jobs = [] if job is None else [job]
+    allocated = [pltpu.VMEM(s, jnp.bfloat16) if isinstance(s, tuple) else s for s in scratch]
+    if copies is not None:
+        allocated += [DMA(copies), DMA(copies)]
+    counts = (len(operands), len(outs), len(allocated))
+    job_ins, job_outs = [len(j.operands) for j in jobs], [len(j.outs) for j in jobs]
+
+    def body(*refs):
+        refs = list(refs)
+
+        def take(count):
+            taken, refs[:] = refs[:count], refs[count:]
+            return taken
+
+        own_ins, their_ins = take(counts[0]), [take(n) for n in job_ins]
+        own_outs, their_outs = take(counts[1]), [take(n) for n in job_outs]
+        own_scratch, their_scratch = take(counts[2]), [take(len(j.scratch)) for j in jobs]
+        for j, i, o, s in zip(jobs, their_ins, their_outs, their_scratch):
+            j.bind(i, o, s)
+        place = Place(*sizes)
+
+        def run(step):
+            for j in jobs:
+                getattr(j, step)(place)
+
+        kernel(place, run, *own_ins, *own_outs, *own_scratch)
+
+    all_outs = list(outs) + [o for j in jobs for o in j.outs]
+    got = pl.pallas_call(
+        body,
+        out_shape=tuple(jax.ShapeDtypeStruct(shape, dtype) for shape, dtype in all_outs),
+        in_specs=[IN_VMEM] * counts[0] + [s for j in jobs for s in j.in_specs],
+        out_specs=tuple([IN_VMEM] * counts[1] + [s for j in jobs for s in j.out_specs]),
+        scratch_shapes=allocated + [s for j in jobs for s in j.scratch],
+        compiler_params=pltpu.CompilerParams(collective_id=collective_id, has_side_effects=True, vmem_limit_bytes=VMEM_BYTES),
+        cost_estimate=pl.CostEstimate(flops=20_000_000_000, bytes_accessed=10_000_000, transcendentals=0),
+    )(*operands, *[w for j in jobs for w in j.operands])
+    return got[: counts[1]], (None if job is None else job.result(got[counts[1] :]))
+
+
+def job_alone_kernel(place, run):
+    place.greet()
+    run("begin")
+    run("middle")
+    run("end")
+
+
+def job_alone(sizes, collective_id, job):
+    return stage(sizes, collective_id, job_alone_kernel, [], [], [], None, job)[1]
+
+
+def feed_forward_kernel(gain_at, final_at, place, run, x_ref, gains_ref, gu_ref, down_ref, y_ref, last_ref, n_ref, n_buf, p_buf, r_buf, sent, got):
+    place.greet()
+    x = x_ref[...]
+    n_buf[place.group] = low(rms_norm(x, gains_ref[gain_at]))
+    pending = spread_start(place, n_buf, sent.at[0], got.at[0])
+    run("begin")
+    spread_wait(place, n_buf, sent.at[0], got.at[0])
+    n = all_rows(n_buf)
+    hidden = down_ref.shape[0]
+    gu = nn(n, gu_ref[...])
+    h = low(gelu_and_slope(gu[:, :hidden])[0] * gu[:, hidden:])
+    pending += collect_start(place, nn(h, down_ref[...]), p_buf, r_buf, sent.at[1], got.at[1])
+    n_ref[...] = n
+    run("middle")
+    y = x + collect_wait(place, p_buf, r_buf, sent.at[1], got.at[1])
+    y_ref[...] = y
+    last_ref[...] = low(rms_norm(y, gains_ref[final_at]))
+    run("end")
+    for copy in pending:
+        copy.wait_send()
+
+
+def feed_back_part(n, dyb, gu_ref, down_ref):
+    hidden = down_ref.shape[0]
+    gu = nn(n, gu_ref[...])
+    g, u = gu[:, :hidden], gu[:, hidden:]
+    act, slope = gelu_and_slope(g)
+    dh = nt(dyb, down_ref[...])
+    return low(act * u), jnp.concatenate([low(dh * u * slope), low(dh * act)], axis=1)
+
+
+def feed_both_kernel(
+    gain_at, place, run, x_ref, cot_ref, gains_ref, gu_ref, down_ref,
+    y_ref, dx_ref, dgain_ref, dgu_ref, ddown_ref,
+    n_buf, d_buf, py_buf, ry_buf, pn_buf, rn_buf, sent, got,
+):
+    place.greet()
+    x = x_ref[...]
+    d_buf[place.group] = cot_ref[...]
+    pending = spread_start(place, d_buf, sent.at[1], got.at[1])
+    n_buf[place.group] = low(rms_norm(x, gains_ref[gain_at]))
+    pending += spread_start(place, n_buf, sent.at[0], got.at[0])
+    run("begin")
+    spread_wait(place, n_buf, sent.at[0], got.at[0])
+    spread_wait(place, d_buf, sent.at[1], got.at[1])
+    n, dyb = all_rows(n_buf), all_rows(d_buf)
+    h, dgu = feed_back_part(n, dyb, gu_ref, down_ref)
+    pending += collect_start(place, nt(dgu, gu_ref[...]), pn_buf, rn_buf, sent.at[2], got.at[2])
+    pending += collect_start(place, nn(h, down_ref[...]), py_buf, ry_buf, sent.at[3], got.at[3])
+    dgu_ref[...] = low(tn(n, dgu))
+    ddown_ref[...] = low(tn(h, dyb))
+    run("middle")
+    dn = collect_wait(place, pn_buf, rn_buf, sent.at[2], got.at[2])
+    back, dgain = norm_back(x, gains_ref[gain_at], dn)
+    dx_ref[...] = cot_ref[...].astype(jnp.float32) + back
+    dgain_ref[...] = dgain
+    y_ref[...] = x + collect_wait(place, py_buf, ry_buf, sent.at[3], got.at[3])
+    run("end")
+    for copy in pending:
+        copy.wait_send()
+
+
+def feed_back_kernel(
+    gain_at, final_at, place, run, x_ref, y_ref, cot_ref, dlast_ref, gains_ref, n_ref, gu_ref, down_ref,
+    dx_ref, dgain_ref, dfinal_ref, dgu_ref, ddown_ref,
+    d_buf, pn_buf, rn_buf, sent, got,
+):
+    place.greet()
+    back, dfinal = norm_back(y_ref[...], gains_ref[final_at], dlast_ref[...])
+    dfinal_ref[...] = dfinal
+    dy = cot_ref[...].astype(jnp.float32) + back
+    d_buf[place.group] = low(dy)
+    pending = spread_start(place, d_buf, sent.at[0], got.at[0])
+    run("begin")
+    spread_wait(place, d_buf, sent.at[0], got.at[0])
+    n, dyb = n_ref[...], all_rows(d_buf)
+    h, dgu = feed_back_part(n, dyb, gu_ref, down_ref)
+    pending += collect_start(place, nt(dgu, gu_ref[...]), pn_buf, rn_buf, sent.at[1], got.at[1])
+    dgu_ref[...] = low(tn(n, dgu))
+    ddown_ref[...] = low(tn(h, dyb))
+    run("middle")
+    dn = collect_wait(place, pn_buf, rn_buf, sent.at[1], got.at[1])
+    back, dgain = norm_back(x_ref[...], gains_ref[gain_at], dn)
+    dx_ref[...] = dy + back
+    dgain_ref[...] = dgain
+    run("end")
+    for copy in pending:
+        copy.wait_send()
+
+
+def bias_mask(place, block, causal, rel_ref, turn_ref, kdoc_ref, qdoc_ref, out_ref):
+    heads, rows_total, lanes = out_ref.shape
+    key_len = kdoc_ref.shape[0]
+    strip = block + 2 * BLOCK_PAD
+    query = lax.broadcasted_iota(jnp.int32, (1, lanes), 1)
+    start = ((place.cores * (query // block) + place.core) * place.parts + place.part) * block
+    allowed = kdoc_ref[...] == qdoc_ref[...]
+    if causal:
+        places = lax.broadcasted_iota(jnp.int32, (key_len, lanes), 0)
+        allowed = allowed & (places <= start + query % block)
+    inside = pl.ds(BLOCK_PAD, key_len)
+    if rel_ref is None:
+        out_ref[0, inside, :] = low(jnp.where(allowed, 0.0, NEGATIVE))
+        return
+    by_head = tn(rel_ref[...], turn_ref[...])
+    width = by_head.shape[1]
+    pick_rows = lax.broadcasted_iota(jnp.int32, (8, by_head.shape[0]), 0)
+    pick_cols = lax.broadcasted_iota(jnp.int32, (8, by_head.shape[0]), 1)
+    picked = nn(low(jnp.where(pick_cols == pick_rows + place.group * heads, 1.0, 0.0)), low(by_head))
+    places = lax.broadcasted_iota(jnp.int32, (rows_total, lanes), 0)
+    for head in range(heads):
+        row = picked[head : head + 1, :]
+        left, right = row[:, width - 2 : width - 1], row[:, 0:1]
+        out_ref[head] = low(jnp.where(places < start, left, right))
+        wide = jnp.broadcast_to(row, (strip, width))
+        for number in range(lanes // block):
+            at = (number * block) % 128
+            turned = pltpu.roll(wide, (width - (strip - 1) + at) % width, 1, stride=1, stride_axis=0)
+            rows = pl.ds(place.first_token(number, block), strip)
+            out_ref[head, rows, number * block : (number + 1) * block] = low(turned[:, at : at + block])
+        out_ref[head, inside, :] = low(jnp.where(allowed, out_ref[head, inside, :].astype(jnp.float32), NEGATIVE))
+
+
+def chunk_rows(kv_ref):
+    return kv_ref.shape[1] * kv_ref.shape[2] * kv_ref.shape[3]
+
+
+def key_side(kv_ref, chunk):
+    return kv_ref[chunk].reshape(chunk_rows(kv_ref), kv_ref.shape[4])[:, : kv_ref.shape[4] // 2]
+
+
+def value_side(kv_ref, chunk):
+    lanes = kv_ref.shape[4]
+    return kv_ref[chunk].reshape(chunk_rows(kv_ref), lanes)[:, lanes // 2 // 128 * 128 :]
+
+
+def bias_rows(bm_ref, head, chunk, rows):
+    at = pl.multiple_of(BLOCK_PAD + chunk * rows, 128)
+    return bm_ref[head if bm_ref.shape[0] > 1 else 0, pl.ds(at, rows), :].astype(jnp.float32)
+
+
+def mix_part(q, kv_ref, bm_ref, o_ref, lse_ref, s_ref, ot_ref):
+    chunks, rows = kv_ref.shape[0], chunk_rows(kv_ref)
+    queries, width = q.shape
+    heads = width // HD
+    across = [slice(head * queries, (head + 1) * queries) for head in range(heads)]
+    masked_q = [only_lanes(q, head * HD, HD) for head in range(heads)]
+
+    def first(chunk, tops):
+        keys = key_side(kv_ref, chunk)
+        inside = pl.ds(pl.multiple_of(chunk * rows, rows), rows)
+        new = []
+        for head in range(heads):
+            scores = nt(keys, masked_q[head]) + bias_rows(bm_ref, head, chunk, rows)
+            s_ref[inside, across[head]] = scores
+            new.append(jnp.maximum(tops[head], jnp.max(scores, axis=0, keepdims=True)))
+        return tuple(new)
+
+    tops = lax.fori_loop(0, chunks, first, (jnp.full((1, queries), NEGATIVE, jnp.float32),) * heads)
+
+    def second(chunk, carried):
+        values = value_side(kv_ref, chunk)
+        inside = pl.ds(pl.multiple_of(chunk * rows, rows), rows)
+        lead = values.shape[1] - width
+        values_t = low(nt(identity(values.shape[1]), values))
+        new = []
+        for head in range(heads):
+            total, mixed = carried[head]
+            weights = jnp.exp(s_ref[inside, across[head]] - tops[head])
+            mixed = mixed + nn(values_t[lead + head * HD : lead + (head + 1) * HD], low(weights))
+            new.append((total + jnp.sum(weights, axis=0, keepdims=True), mixed))
+        return tuple(new)
+
+    start = (jnp.zeros((1, queries), jnp.float32), jnp.zeros((HD, queries), jnp.float32))
+    done = lax.fori_loop(0, chunks, second, (start,) * heads)
+    for head in range(heads):
+        total, mixed = done[head]
+        lse_ref[:, across[head]] = tops[head] + jnp.log(total)
+        ot_ref[head * HD : (head + 1) * HD, :] = low(mixed / total)
+    o_ref[...] = low(nt(identity(queries), ot_ref[...]))
+
+
+def keys_send(place, kv_ref, base, sent, got):
+    mine = kv_ref.at[:, place.core, place.part]
+    pending = [
+        send(mine, mine, sent.at[base, step], got.at[base, step], place.at_plane(place.plane(step)))
+        for step in range(1, place.parts)
+    ]
+    pending.append(send(mine, mine, sent.at[base + 1, 0], got.at[base + 1, 0], place.sibling()))
+    return pending
+
+
+def keys_relay(place, kv_ref, base, sent, got):
+    pending = []
+    for step in range(1, place.parts):
+        source = place.plane_behind(step)
+        slot = kv_ref.at[:, place.core, source]
+        arrived(slot, sent.at[base, step], got.at[base, step], place.at_plane(source))
+        pending.append(send(slot, slot, sent.at[base + 1, step], got.at[base + 1, step], place.sibling()))
+    return pending
+
+
+def keys_wait(place, kv_ref, base, sent, got):
+    for step in range(place.parts):
+        slot = kv_ref.at[:, 1 - place.core, place.plane_behind(step)]
+        arrived(slot, sent.at[base + 1, step], got.at[base + 1, step], place.sibling())
+
+
+def attend_kernel(crosses, gain_at, place, run, *refs):
+    refs = list(refs)
+
+    def take(count):
+        taken, refs[:] = refs[:count], refs[count:]
+        return taken
+
+    count = len(crosses)
+    ins = [take(7 if cross else 8) for cross in crosses]
+    outs = [take(8 if cross else 7) for cross in crosses]
+    s_ref, ot_ref = take(2)
+    bufs = [take(4 if cross else 3) for cross in crosses]
+    sent, got = take(2)
+    place.greet(planes=True)
+    pending = []
+    for index, cross in enumerate(crosses):
+        x_ref, gain_ref = ins[index][0], ins[index][1]
+        if cross:
+            bufs[index][3][place.group] = ins[index][6][...]
+            pending += spread_start(place, bufs[index][3], sent.at[5 * index + 4], got.at[5 * index + 4])
+        bufs[index][0][place.group] = low(rms_norm(x_ref[...].astype(jnp.float32), gain_ref[gain_at[index]]))
+        pending += spread_start(place, bufs[index][0], sent.at[5 * index], got.at[5 * index])
+    for index, cross in enumerate(crosses):
+        w_ref, kv_ref = ins[index][2], outs[index][3]
+        kv_width = kv_ref.shape[4]
+        n_buf = bufs[index][0]
+        if cross:
+            source = bufs[index][3]
+            spread_wait(place, source, sent.at[5 * index + 4], got.at[5 * index + 4])
+            kv = low(nn(all_rows(source), w_ref[:, :kv_width]))
+            outs[index][7][...] = all_rows(source)
+        else:
+            spread_wait(place, n_buf, sent.at[5 * index], got.at[5 * index])
+            both = low(nn(all_rows(n_buf), w_ref[...]))
+            kv, q = both[:, :kv_width], both[:, kv_width:]
+        kv_ref[:, place.core, place.part] = kv.reshape(kv_ref.shape[0], kv_ref.shape[3], kv_width)
+        pending += keys_send(place, kv_ref, 5 * index + 1, sent, got)
+        if cross:
+            spread_wait(place, n_buf, sent.at[5 * index], got.at[5 * index])
+            q = low(nn(all_rows(n_buf), w_ref[:, kv_width:]))
+        outs[index][1][...] = all_rows(n_buf)
+        outs[index][2][...] = q
+    run("begin")
+    for index, cross in enumerate(crosses):
+        block = ins[index][0].shape[0]
+        kdoc_ref, qdoc_ref = ins[index][4:6]
+        rel_ref, turn_ref = (None, None) if cross else [r.at[index] for r in ins[index][6:8]]
+        bias_mask(place, block, index == count - 1 and not cross, rel_ref, turn_ref, kdoc_ref, qdoc_ref, outs[index][6])
+    for index in range(count):
+        wo_ref = ins[index][3]
+        kv_ref, o_ref, lse_ref, bm_ref = outs[index][3:7]
+        pending += keys_relay(place, kv_ref, 5 * index + 1, sent, got)
+        keys_wait(place, kv_ref, 5 * index + 1, sent, got)
+        mix_part(outs[index][2][...], kv_ref, bm_ref, o_ref, lse_ref, s_ref, ot_ref)
+        share = nn(o_ref[...], wo_ref[...])
+        pending += collect_start(place, share, bufs[index][1], bufs[index][2], sent.at[5 * index + 3], got.at[5 * index + 3])
+        if index == 0:
+            run("middle")
+    for index in range(count):
+        total = collect_wait(place, bufs[index][1], bufs[index][2], sent.at[5 * index + 3], got.at[5 * index + 3])
+        outs[index][0][...] = ins[index][0][...].astype(jnp.float32) + total
+    run("end")
+    for copy in pending:
+        copy.wait_send()
+
+
+def attend(sizes, collective_id, gain_at, layers, job=None):
+    groups, cores, parts = sizes
+    operands, outs, scratch, crosses = [], [], [], []
+    f32, bf16 = jnp.float32, jnp.bfloat16
+    for layer in layers:
+        x, wo = layer[0], layer[3]
+        cross = len(layer) == 7
+        block, model = x.shape
+        width = wo.shape[0]
+        tokens = groups * block
+        keys = cores * parts * tokens
+        operands += layer
+        outs += [
+            ((block, model), f32), ((tokens, model), bf16), ((tokens, width), bf16),
+            ((groups, cores, parts, block, 2 * width), bf16), ((tokens, width), bf16), ((1, width // HD * tokens), f32),
+            ((1 if cross else width // HD, keys + 2 * BLOCK_PAD, tokens), bf16),
+        ]
+        if cross:
+            outs.append(((tokens, model), bf16))
+        scratch += [(groups, block, model)] * (4 if cross else 3)
+        crosses.append(cross)
+    first = [pltpu.VMEM((keys, width // HD * tokens), f32), (width, tokens)]
+    copies = (5 * len(layers), max(groups, parts))
+    got, given = stage(
+        sizes, collective_id, functools.partial(attend_kernel, crosses, gain_at), operands, outs, first + scratch, copies, job
+    )
+    results, at = [], 0
+    for cross in crosses:
+        size = 8 if cross else 7
+        results.append(tuple(got[at : at + size]) + (() if cross else (None,)))
+        at += size
+    return results, given
+
+
+def mix_back_part(place, q, do, kv_ref, lse_ref, bm_ref, biased, dkv_ref, p_ref, dp_ref, ds_ref, pb_ref, ot_ref):
+    chunks, cores, parts, block, lanes = kv_ref.shape
+    rows = chunk_rows(kv_ref)
+    queries, width = q.shape
+    heads = width // HD
+    strip = block + 2 * BLOCK_PAD
+    first_value = width // 128 * 128
+    lead = width - first_value
+    do_wide = jnp.concatenate([jnp.zeros((queries, lead), do.dtype), do], axis=1) if lead else do
+    across = [slice(head * queries, (head + 1) * queries) for head in range(heads)]
+    masked_q = [only_lanes(q, head * HD, HD) for head in range(heads)]
+    masked_do = [only_lanes(do_wide, lead + head * HD, HD) for head in range(heads)]
+    nothing = jnp.zeros((1, queries), jnp.float32)
+    if biased:
+        none = jnp.zeros((BLOCK_PAD, heads * queries), jnp.bfloat16)
+        ds_ref[0:BLOCK_PAD, :] = none
+        ds_ref[BLOCK_PAD + chunks * rows :, :] = none
+        of_lane = lax.broadcasted_iota(jnp.int32, (1, queries), 1) // block
+        lane_start = ((cores * of_lane + place.core) * parts + place.part) * block
+
+    def first(chunk, inners):
+        keys, values = key_side(kv_ref, chunk), value_side(kv_ref, chunk)
+        inside = pl.ds(pl.multiple_of(chunk * rows, rows), rows)
+        new = []
+        for head in range(heads):
+            scores = nt(keys, masked_q[head]) + bias_rows(bm_ref, head, chunk, rows)
+            p = jnp.exp(scores - lse_ref[:, across[head]])
+            dp = nt(values, masked_do[head])
+            p_ref[inside, across[head]] = p
+            dp_ref[inside, across[head]] = dp
+            pb_ref[inside, across[head]] = low(p)
+            new.append(inners[head] + jnp.sum(p * dp, axis=0, keepdims=True))
+        return tuple(new)
+
+    inners = lax.fori_loop(0, chunks, first, (nothing,) * heads)
+    stacked_q = jnp.concatenate(masked_q, axis=0)
+    if lead:
+        stacked_q = jnp.concatenate([stacked_q, jnp.zeros((stacked_q.shape[0], lead), stacked_q.dtype)], axis=1)
+    stacked_do = jnp.concatenate(masked_do, axis=0)
+
+    def second(chunk, carried):
+        at = pl.multiple_of(chunk * rows, rows)
+        inside, padded = pl.ds(at, rows), pl.ds(pl.multiple_of(BLOCK_PAD + at, 128), rows)
+        keys_t = low(nt(identity(width), key_side(kv_ref, chunk)))
+        new = []
+        for head in range(heads):
+            left, right, back = carried[head]
+            ds = low(p_ref[inside, across[head]] * (dp_ref[inside, across[head]] - inners[head]))
+            ds_ref[padded, across[head]] = ds
+            back = back + nn(keys_t[head * HD : (head + 1) * HD], ds)
+            if biased:
+                wide = ds.astype(jnp.float32)
+                places = lax.broadcasted_iota(jnp.int32, wide.shape, 0) + (at + BLOCK_PAD)
+                left = left + jnp.sum(jnp.where(places < lane_start, wide, 0.0), axis=0, keepdims=True)
+                right = right + jnp.sum(jnp.where(places >= lane_start + strip, wide, 0.0), axis=0, keepdims=True)
+            new.append((left, right, back))
+        dk = nn(ds_ref[padded, :], stacked_q)
+        dv = nn(pb_ref[inside, :], stacked_do)
+        if lead:
+            shared = dk[:, first_value:] + dv[:, : 2 * lead]
+            both = jnp.concatenate([dk[:, :first_value], shared, dv[:, 2 * lead :]], axis=1)
+        else:
+            both = jnp.concatenate([dk, dv], axis=1)
+        dkv_ref[chunk] = low(both).reshape(dkv_ref.shape[1:])
+        return tuple(new)
+
+    start = (nothing, nothing, jnp.zeros((HD, queries), jnp.float32))
+    done = lax.fori_loop(0, chunks, second, (start,) * heads)
+    for head in range(heads):
+        ot_ref[head * HD : (head + 1) * HD, :] = low(done[head][2])
+    return low(nt(identity(queries), ot_ref[...])), done
+
+
+def table_grads(place, block, done, ds_ref, ahead_ref, rel_ref):
+    queries = done[0][0].shape[1]
+    width = ahead_ref.shape[1]
+    strip = block + 2 * BLOCK_PAD
+    rows = lax.broadcasted_iota(jnp.int32, (block, block), 0)
+    cols = lax.broadcasted_iota(jnp.int32, (block, block), 1)
+    backwards = jnp.where(rows + cols == block - 1, 1.0, 0.0)
+    at = lax.broadcasted_iota(jnp.int32, (1, width), 1)
+    sums = []
+    for head, (left, right, _) in enumerate(done):
+        total = jnp.zeros((strip, block), jnp.float32)
+        for number in range(queries // block):
+            low_at = head * queries + number * block
+            near = pl.ds(place.first_token(number, block), strip)
+            total = total + ds_ref[near, low_at : low_at + block].astype(jnp.float32)
+        turned = lax.dot_general(
+            backwards, total, (((1,), (1,)), ((), ())), precision=HIGHEST, preferred_element_type=jnp.float32
+        )
+        turned = jnp.concatenate([turned, jnp.zeros((block, width - strip), jnp.float32)], axis=1)
+        by_distance = jnp.sum(pltpu.roll(turned, 0, 1, stride=1, stride_axis=0), axis=0, keepdims=True)
+        left, right = (jnp.sum(side, axis=1, keepdims=True) for side in (left, right))
+        sums.append(by_distance + jnp.where(at == 0, left, 0.0) + jnp.where(at == width - 2, right, 0.0))
+    sums = jnp.concatenate(sums + [jnp.zeros((8 - len(sums), width), jnp.float32)], axis=0)
+    rel_ref[...] = lax.dot_general(
+        sums, ahead_ref[...], (((1,), (1,)), ((), ())), precision=HIGHEST, preferred_element_type=jnp.float32
+    )
+
+
+def attend_back_kernel(cross, gain_at, which, place, run, *refs):
+    refs = list(refs)
+
+    def take(count):
+        taken, refs[:] = refs[:count], refs[count:]
+        return taken
+
+    x_ref, gain_ref, dy_ref, n_ref, q_ref, kv_ref, o_ref, lse_ref, w_ref, wo_ref, bm_ref = take(11)
+    memory_ref, ahead_ref = (take(1)[0], None) if cross else (None, take(1)[0])
+    dx_ref, dgain_ref, dw_ref, dwo_ref = take(4)
+    dmem_ref, rel_ref = (take(1)[0], None) if cross else (None, take(1)[0])
+    p_ref, dp_ref, ds_ref, pb_ref, ot_ref, dkv_ref, sib_ref, zout_ref, zin_ref, d_buf, pn_buf, rn_buf = take(12)
+    pm_buf, rm_buf = take(2) if cross else (None, None)
+    sent, got = take(2)
+    place.greet(planes=True)
+    dy = dy_ref[...]
+    d_buf[place.group] = low(dy)
+    pending = spread_start(place, d_buf, sent.at[0], got.at[0])
+    run("begin")
+    spread_wait(place, d_buf, sent.at[0], got.at[0])
+    dyb = all_rows(d_buf)
+    do = low(nt(dyb, wo_ref[...]))
+    dq, done = mix_back_part(
+        place, q_ref[...], do, kv_ref, lse_ref, bm_ref, not cross, dkv_ref, p_ref, dp_ref, ds_ref, pb_ref, ot_ref
+    )
+    mine = place.core
+    pending.append(send(dkv_ref.at[:, 1 - mine], sib_ref, sent.at[1, 0], got.at[1, 0], place.sibling()))
+    kv_width = kv_ref.shape[4]
+    dn_share = nt(dq, w_ref[:, kv_width:])
+    if cross:
+        pending += collect_start(place, dn_share, pn_buf, rn_buf, sent.at[3], got.at[3])
+    arrived(sib_ref, sent.at[1, 0], got.at[1, 0], place.sibling())
+    for step in list(range(1, place.parts)) + [0]:
+        to = place.plane(step)
+        zout_ref[to] = low(dkv_ref[:, mine, to].astype(jnp.float32) + sib_ref[:, to].astype(jnp.float32))
+        if step:
+            pending.append(send(zout_ref.at[to], zin_ref.at[place.part], sent.at[2, step], got.at[2, step], place.at_plane(to)))
+    run("middle")
+    dwo_ref[...] = low(tn(o_ref[...], dyb))
+    dw_ref[:, kv_width:] = low(tn(n_ref[...], dq))
+    if not cross:
+        table_grads(place, dy_ref.shape[0], done, ds_ref, ahead_ref.at[which], rel_ref)
+    total = zout_ref[place.part].astype(jnp.float32)
+    for step in range(1, place.parts):
+        source = place.plane_behind(step)
+        arrived(zin_ref.at[source], sent.at[2, step], got.at[2, step], place.at_plane(source))
+        total = total + zin_ref[source].astype(jnp.float32)
+    dkv = low(total).reshape(q_ref.shape[0], kv_width)
+    if cross:
+        pending += collect_start(place, nt(dkv, w_ref[:, :kv_width]), pm_buf, rm_buf, sent.at[4], got.at[4])
+        dw_ref[:, :kv_width] = low(tn(memory_ref[...], dkv))
+        dmem_ref[...] = collect_wait(place, pm_buf, rm_buf, sent.at[4], got.at[4])
+    else:
+        share = dn_share + nt(dkv, w_ref[:, :kv_width])
+        pending += collect_start(place, share, pn_buf, rn_buf, sent.at[3], got.at[3])
+        dw_ref[:, :kv_width] = low(tn(n_ref[...], dkv))
+    dn = collect_wait(place, pn_buf, rn_buf, sent.at[3], got.at[3])
+    back, dgain = norm_back(x_ref[...].astype(jnp.float32), gain_ref[gain_at], dn)
+    dx_ref[...] = dy + back
+    dgain_ref[...] = dgain
+    run("end")
+    for copy in pending:
+        copy.wait_send()
+
+
+def attend_back(sizes, collective_id, x, gains, gain_at, dy, kept, w, wo, ahead, which, job=None):
+    cross = ahead is None
+    groups, cores, parts = sizes
+    _, n, q, kv, o, lse, bm, memory = kept
+    block, model = x.shape
+    tokens, width = q.shape
+    heads = width // HD
+    keys = cores * parts * tokens
+    f32, bf16 = jnp.float32, jnp.bfloat16
+    operands = [x, gains, dy, n, q, kv, o, lse, w, wo, bm] + [memory if cross else ahead]
+    outs = [((block, model), f32), ((1, model), f32), (w.shape, bf16), (wo.shape, bf16)]
+    outs.append(((block, model) if cross else (8, ahead.shape[1]), f32))
+    turned = (parts, groups, block, 2 * width)
+    scratch = [
+        pltpu.VMEM((keys, heads * tokens), f32), pltpu.VMEM((keys, heads * tokens), f32),
+        (keys + 2 * BLOCK_PAD, heads * tokens), (keys, heads * tokens), (width, tokens),
+        kv.shape, (groups, parts, block, 2 * width), turned, turned,
+    ] + [(groups, block, model)] * (5 if cross else 3)
+    copies = (5, max(groups, parts))
+    return stage(sizes, collective_id, functools.partial(attend_back_kernel, cross, gain_at, which), operands, outs, scratch, copies, job)
+
+
+def fast_device(
+    enc_in, dec_in, enc_cot, dec_cot, enc_segments, dec_segments, buckets,
+    enc_norm1, enc_query, enc_key, enc_value, enc_proj, enc_rel, enc_norm2, enc_gate, enc_up, enc_down, enc_final,
+    dec_norm1, dec_query, dec_key, dec_value, dec_proj, dec_rel, dec_norm2, cross_query, cross_key, cross_value, cross_proj,
+    dec_norm3, dec_gate, dec_up, dec_down,
+):
+    groups, cores, parts = sizes = lax.axis_size(HG), lax.axis_size(CORE), lax.axis_size(SP)
+    my_group, my_core, my_part = lax.axis_index(HG), lax.axis_index(CORE), lax.axis_index(SP)
+    block, model = enc_in.shape
+    devices = groups * cores
+    share = model // devices
+    heads = HEADS // groups
+    reach = (buckets.shape[1] - 1) // 2
+    bf16, f32 = jnp.bfloat16, jnp.float32
+
+    def packed(*weights):
+        cut = [w.reshape(w.shape[0], groups, w.shape[1] // groups) for w in weights]
+        return jnp.concatenate(cut, axis=2).transpose(1, 0, 2)
+
+    small = jnp.concatenate([enc_norm1, enc_norm2, enc_final, dec_norm1, dec_norm2, dec_norm3, enc_rel, dec_rel])
+    small = jnp.broadcast_to(small, (groups, 16, small.shape[0]))
+    (small, enc_kvq, dec_kvq), (enc_wo, dec_wo) = job_alone(
+        sizes,
+        1,
+        Recut(
+            sizes,
+            [small, packed(enc_key, enc_value, enc_query), packed(dec_key, dec_value, dec_query)],
+            [enc_proj, dec_proj],
+        ),
+    )
+    later = Recut(
+        sizes,
+        [packed(enc_gate, enc_up), packed(cross_key, cross_value, cross_query), packed(dec_gate, dec_up)],
+        [enc_down, cross_proj, dec_down],
+    )
+    small = small.reshape(devices, 16, -1)[:, 0]
+    gains = small[:, : 6 * share].reshape(devices, 6, share).transpose(1, 0, 2).reshape(6, 1, model).astype(f32)
+    rel_len = enc_rel.shape[0]
+    rels = small[:, 6 * share :].reshape(devices, 2, rel_len).transpose(1, 0, 2).reshape(2, -1, HEADS)
+    rels = jnp.pad(rels, ((0, 0), (0, 0), (0, 128 - HEADS)))
+
+    bucket_count = devices * rel_len // HEADS
+    numbers = jnp.arange(bucket_count, dtype=jnp.int32)[None, :, None]
+    long = jnp.pad(buckets, ((0, 0), (block - 1, block)), mode="edge")[:, None, :]
+    ahead = (long == numbers).astype(f32)
+    back_way = jnp.pad(buckets[:, ::-1], ((0, 0), (block - 1, block)), mode="edge")[:, None, :]
+    turn = (back_way == numbers).astype(bf16)
+
+    def mine(ids):
+        return lax.dynamic_index_in_dim(
+            lax.dynamic_index_in_dim(ids.reshape(groups, cores, parts, block), my_core, 1, False), my_part, 1, False
+        ).reshape(1, -1)
+
+    enc_q_ids, dec_q_ids = mine(enc_segments), mine(dec_segments)
+    enc_k_ids, dec_k_ids = enc_segments[:, None], dec_segments[:, None]
+
+    (enc_kept, dec_kept), ((enc_gu, cross_kvq, dec_gu), (enc_wd, cross_wo, dec_wd)) = attend(
+        sizes,
+        2,
+        (0, 3),
+        [
+            (enc_in, gains, enc_kvq, enc_wo, enc_k_ids, enc_q_ids, rels, turn),
+            (dec_in, gains, dec_kvq, dec_wo, dec_k_ids, dec_q_ids, rels, turn),
+        ],
+        later,
+    )
+    ex, dx = enc_kept[0], dec_kept[0]
+    tokens, hidden = groups * block, enc_wd.shape[0]
+    token_f32, token_bf16, gain_f32 = ((block, model), f32), ((block, model), bf16), ((1, model), f32)
+    gu_grad, down_grad = ((model, 2 * hidden), bf16), ((hidden, model), bf16)
+    buffer = (groups, block, model)
+    (enc_out, memory, en2), _ = stage(
+        sizes, 3, functools.partial(feed_forward_kernel, 1, 2), [ex, gains, enc_gu, enc_wd],
+        [token_f32, token_bf16, ((tokens, model), bf16)], [buffer] * 3, (2, groups),
+    )
+    (cross_kept,), _ = attend(sizes, 4, (4,), [(dx, gains, cross_kvq, cross_wo, enc_k_ids, dec_q_ids, memory)])
+    cx = cross_kept[0]
+    (dec_out, grad_cx, dg_d3, dw_dgu, dw_ddown), _ = stage(
+        sizes, 5, functools.partial(feed_both_kernel, 5), [cx, dec_cot, gains, dec_gu, dec_wd],
+        [token_f32, token_f32, gain_f32, gu_grad, down_grad], [buffer] * 6, (4, groups),
+    )
+
+    tie = lax.optimization_barrier
+
+    def summed(grads, before):
+        grads, _ = tie((grads, before))
+        return [lax.psum(g, SP) for g in grads]
+
+    (grad_dx, dg_d2, dw_ckvq, dw_co, dmem), rows_a = attend_back(
+        sizes, 6, dx, gains, 4, grad_cx, cross_kept, cross_kvq, cross_wo, None, None, GiveRows(sizes, [dw_dgu], [dw_ddown])
+    )
+    (grad_ex, dg_e2, dg_ef, dw_egu, dw_edown), rows_b = stage(
+        sizes, 7, functools.partial(feed_back_kernel, 1, 2), [ex, enc_out, enc_cot, dmem, gains, en2, enc_gu, enc_wd],
+        [token_f32, gain_f32, gain_f32, gu_grad, down_grad], [buffer] * 3, (2, groups),
+        GiveRows(sizes, [dw_ckvq], [dw_co]),
+    )
+    sum_ab = summed(rows_a + rows_b, [small])
+    grad_dx, grad_ex = tie((grad_dx, grad_ex))
+    (dec_in_grad, dg_d1, dw_dkvq, dw_do, dec_tab), rows_c = attend_back(
+        sizes, 8, dec_in, gains, 3, grad_dx, dec_kept, dec_kvq, dec_wo, ahead, 1, GiveRows(sizes, [dw_egu], [dw_edown])
+    )
+    grad_ex, sum_ab = tie((grad_ex, sum_ab))
+    sum_c = summed(rows_c, sum_ab)
+    (enc_in_grad, dg_e1, dw_ekvq, dw_eo, enc_tab), rows_d = attend_back(
+        sizes, 9, enc_in, gains, 0, grad_ex, enc_kept, enc_kvq, enc_wo, ahead, 0, GiveRows(sizes, [dw_dkvq], [dw_do])
+    )
+
+    def rel_grad(mine):
+        full = lax.dynamic_update_slice_in_dim(jnp.zeros((HEADS, bucket_count), f32), mine[:heads], my_group * heads, 0)
+        return full.T.reshape(-1)
+
+    small_grads = [dg_e1, dg_e2, dg_ef, dg_d1, dg_d2, dg_d3, rel_grad(enc_tab), rel_grad(dec_tab)]
+    packed_small = jnp.concatenate([v.reshape(devices, 1, -1) for v in small_grads], axis=2)
+    packed_small = jnp.broadcast_to(packed_small, (devices, 16, packed_small.shape[2]))
+    packed_small = packed_small.reshape(devices * 16, -1).astype(bf16)
+    dw_ekvq, sum_c = tie((dw_ekvq, sum_c))
+    sum_e, sum_d = finish(sizes, 10, GiveRows(sizes, [dw_ekvq, packed_small], [dw_eo]), rows_d)
+
+    def unpacked(whole, pieces):
+        each = whole.shape[2] // pieces
+        whole = whole.astype(f32)
+        return [whole[:, :, i * each : (i + 1) * each].transpose(1, 0, 2).reshape(share, groups * each) for i in range(pieces)]
+
+    dgu_rows, d_wd, cross_rows, c_wo = sum_ab
+    egu_rows, e_wd = sum_c
+    dkvq_rows, d_wo = sum_d
+    ekvq_rows, small_rows, e_wo = sum_e
+    d_wd, c_wo, e_wd, d_wo, e_wo = [g[0].astype(f32) for g in (d_wd, c_wo, e_wd, d_wo, e_wo)]
+    e_wk, e_wv, e_wq = unpacked(ekvq_rows, 3)
+    e_wg, e_wu = unpacked(egu_rows, 2)
+    d_wk, d_wv, d_wq = unpacked(dkvq_rows, 3)
+    c_wk, c_wv, c_wq = unpacked(cross_rows, 3)
+    d_wg, d_wu = unpacked(dgu_rows, 2)
+    own = jnp.sum(small_rows[:, 0].astype(f32), axis=0)
+    s = [own[i * share : (i + 1) * share] for i in range(6)]
+    e_rel, d_rel = own[6 * share : 6 * share + rel_len], own[6 * share + rel_len :]
+    return (
+        enc_out, dec_out, enc_in_grad, dec_in_grad,
+        s[0], e_wq, e_wk, e_wv, e_wo, e_rel, s[1], e_wg, e_wu, e_wd, s[2],
+        s[3], d_wq, d_wk, d_wv, d_wo, d_rel, s[4], c_wq, c_wk, c_wv, c_wo, s[5], d_wg, d_wu, d_wd,
+    )
+
+
+def general_plan(mesh):
     placed = (
         P(("ctx", "sp"), None),
         P(("ctx", "sp"), None),
@@ -701,3 +1793,25 @@
         ),
         check_vma=False,
     )
+
+
+def split_plan(mesh, groups):
+    cut = Mesh(np.asarray(mesh.devices).reshape(groups, 2, mesh.shape["sp"]), (HG, CORE, SP))
+    tokens, rows, gain, same = P((HG, CORE, SP), None), P((HG, CORE), None), P((HG, CORE)), P()
+    attention = (gain, rows, rows, rows, rows, gain)
+    feed = (gain, rows, rows, rows)
+    weights = attention + feed + (gain,) + attention + (gain, rows, rows, rows, rows) + feed
+    return jax.shard_map(
+        fast_device,
+        mesh=cut,
+        in_specs=(tokens,) * 4 + (same,) * 3 + weights,
+        out_specs=(tokens,) * 4 + weights,
+        check_vma=False,
+    )
+
+
+def solution(mesh):
+    groups, odd = divmod(mesh.shape["ctx"], 2)
+    if odd or HEADS % groups or mesh.shape["sp"] != 4:
+        return general_plan(mesh)
+    return split_plan(mesh, groups)

time: 2070 us -> 508 us (0.25)
  waiting for transfers between devices: 831 us -> 41 us
  local copies, waits for them, and re-layouts: 542 us -> 36.7 us
  Pallas kernels: 0 us -> 398 us
  matrix products: 211 us -> 0 us
  blocking collectives: 196 us -> 0 us
  other arithmetic: 135 us -> 12.9 us
  starting transfers between devices: 79.3 us -> 0.08 us
  loops' own time: 45.9 us -> 0 us
    reduce_scatter x21 -> x0, waiting for transfers between devices: 533 us -> none  [the longest x1 63.9 us: per_device(): lax.psum_scatter(d_wg, 'ctx', scatter_dimension=0, tiled=True)]
    pallas_call x0 -> x10, Pallas kernels: none -> 398 us  [the longest x9 350 us: stage(): pl.pallas_call(body, out_shape=tuple((jax.ShapeDtypeStruct(shape, dtype)...]
    reshape x38 -> x43, local copies, waits for them, and re-layouts: 267 us -> 18.5 us  [the longest x13 12.5 us: unpacked(): whole[:, :, i * each:(i + 1) * each].transpose(1, 0, 2)]
    dot_general x98 -> x0, matrix products: 211 us -> none  [the longest x18 47.1 us: weight_grad(): jnp.einsum('td,te->de', left, right, preferred_element_type=jnp.float32)]
    all_gather x18 -> x0, waiting for transfers between devices: 143 us -> none  [the longest x1 30.7 us: per_device(): lax.all_gather(dec_up, 'ctx', axis=0, tiled=True)]
    slice x32 -> x9, local copies, waits for them, and re-layouts: 97.6 us -> 3.93 us  [the longest x4 1.57 us: rel_grad(): mine[:heads]]
    all_to_all x17 -> x0, starting transfers between devices: 77.6 us -> none  [the longest x3 15.7 us: attention_forward(): lax.all_to_all(mixed_low, 'sp', split_axis=0, concat_axis=1, tiled=True)]
    all_gather x6 -> x0, blocking collectives: 71.3 us -> none  [the longest x3 36 us: attention_forward(): value_block = lax.all_gather(value_local, 'ctx', axis=0, tiled=True)]
  transfers between devices with their start and end apart: 57 -> 2, of which waited for: 27 -> 2; matrix products, arithmetic and copies ran while one was open for 39% -> 2% of each run, Pallas kernels for 0% -> 22%
where the time goes in v4:
time: 508 us; the launch traced here: 504 us
  Pallas kernels  398 us (78%)
  waiting for transfers between devices  41 us (8%)
  local copies, waits for them, and re-layouts  36.7 us (7%)
  between operations  14.9 us (3%)
  other arithmetic  12.9 us (3%)
    pallas_call x9, Pallas kernels, stage(): pl.pallas_call(body, out_shape=tuple((jax.ShapeDtypeStruct(shape, dtype)...  350 us
    pallas_call x1, Pallas kernels, finish(): pl.pallas_call(functools.partial(finish_kernel, sizes, give, fold, count)...  47.8 us
    psum x2, waiting for transfers between devices, summed(): return [lax.psum(g, SP) for g in grads]  41 us
    reshape x13, local copies, waits for them, and re-layouts, unpacked(): whole[:, :, i * each:(i + 1) * each].transpose(1, 0, 2)  12.5 us
  transfers between devices with their start and end apart: 2, of which 2 were waited for; matrix products, arithmetic and copies ran while one was open for 2% of the time, Pallas kernels for 22%

profile of v4, /device:TPU:0, one launch (start us, length us, event | category | flops | bytes accessed | tf_op | source)
XLA Modules:
  0.0 503.9 jit_solution(1996199691009820501)
XLA Ops:
  7.3 1.2 reshape.306
  8.6 1.1 reshape.307
  10.8 1.3 maximum_bitcast_fusion.2
  12.9 22.7 %shard_map.544 = (bf16[4,2,16,672]{3,2,1,0:T(8,128)(2,1)}, bf16[4,2,96,576]{3,2,1,0:T(8,128)(2,1)}, bf16[4,2,96,576]{3,2,1,0:T(8,128)(2,1)}, bf16[2,96,768]{2,1,0:T(8,128)(2,1)}, bf16[2,96,768]{2,1,0:T(8,128)(2,1)}) custom-call(bf16[4,16,672]{2,1,0:T(8,128)(2,1)} %broadcast_in_dim.23.refs_0_, bf16[4,96,576]{2,1,0:T(8,128)(2,1)} %get-tuple-element.239.refs_1_, ...), custom_call_target="tpu_custom_call" | custom-call | flops 20000000000 | bytes 10000000 | tf_op jit(solution)/shard_map/pallas_call | solution.py:1060
  35.6 1.0 slice.128
  40.6 1.4 copy.81.refs_4_
  42.8 1.3 copy.82.refs_12_
  44.8 1.0 maximum_bitcast_fusion.refs_16_
  45.9 1.0 maximum_bitcast_fusion.1.refs_18_
  47.9 66.6 %shard_map.545 = (f32[64,768]{1,0:T(8,128)}, bf16[256,768]{1,0:T(8,128)(2,1)}, bf16[256,192]{1,0:T(8,128)(2,1)}, bf16[4,2,4,64,384]{4,3,2,1,0:T(8,128)(2,1)}, bf...) custom-call(bf16[64,768]{1,0:T(8,128)(2,1)} %refs_0_.5, ...), custom_call_target="tpu_custom_call" | custom-call | flops 20000000000 | bytes 10000000 | tf_op jit(solution)/shard_map/pallas_call | solution.py:1060
  114.5 16.1 %shard_map.546 = (f32[64,768]{1,0:T(8,128)}, bf16[64,768]{1,0:T(8,128)(2,1)}, bf16[256,768]{1,0:T(8,128)(2,1)}) custom-call(f32[64,768]{1,0:T(8,128)} %get-tuple-element.125.refs_0_, f32[6,1,768]{2,1,0:T(1,128)} %reshape.362.refs_1_.refs_9_.refs_2_.refs_4_, bf16[768,1024]{1,0:T(8,128)(2,1)} %bitcast.124, bf16[512,768]{1,0:T(8,128)(2,1)} %bitcast.138), custom_call_target="tpu_custom_call" | custom-call | flops 20000000000 | bytes 10000000 | tf_op jit(solution)/shard_map/pallas_call | solution.py:1060
  130.6 35.8 %shard_map.547 = (f32[64,768]{1,0:T(8,128)}, bf16[256,768]{1,0:T(8,128)(2,1)}, bf16[256,192]{1,0:T(8,128)(2,1)}, bf16[4,2,4,64,384]{4,3,2,1,0:T(8,128)(2,1)}, bf...) custom-call(f32[64,768]{1,0:T(8,128)} %get-tuple-element.129.refs_0_, ...), custom_call_target="tpu_custom_call" | custom-call | flops 20000000000 | bytes 10000000 | tf_op jit(solution)/shard_map/pallas_call | solution.py:1060
  166.4 28.6 %shard_map.548 = (f32[64,768]{1,0:T(8,128)}, f32[64,768]{1,0:T(8,128)}, f32[1,768]{1,0:T(1,128)}, bf16[768,1024]{1,0:T(8,128)(2,1)}, bf16[512,768]{1,0:T(8,128)(2,1)}) custom-call(f32[64,768]{1,0:T(8,128)} %get-tuple-element.133.refs_0_, bf16[64,768]{1,0:T(8,128)(2,1)} %refs_1_.1, f32[6,1,768]{2,1,0:T(1,128)} %reshape.362.refs_1_.refs_9_.refs_2_.refs_4_, ...), custom_call_target="tpu_custom_call" | custom-call | flops 20000000000 | bytes 10000000 | tf_op jit(solution)/shard_map/pallas_call | solution.py:1060
  195.0 44.8 %shard_map.549 = (f32[64,768]{1,0:T(8,128)}, f32[1,768]{1,0:T(1,128)}, bf16[768,576]{1,0:T(8,128)(2,1)}, bf16[192,768]{1,0:T(8,128)(2,1)}, f32[64,768]{1,0:T(8,1...) custom-call(f32[64,768]{1,0:T(8,128)} %get-tuple-element.129.refs_0_, ...), custom_call_target="tpu_custom_call" | custom-call | flops 20000000000 | bytes 10000000 | tf_op jit(solution)/shard_map/pallas_call | solution.py:1060
  239.8 26.7 %shard_map.550 = (f32[64,768]{1,0:T(8,128)}, f32[1,768]{1,0:T(1,128)}, f32[1,768]{1,0:T(1,128)}, bf16[768,1024]{1,0:T(8,128)(2,1)}, bf16[512,768]{1,0:T(8,128)(2...) custom-call(f32[64,768]{1,0:T(8,128)} %get-tuple-element.125.refs_0_, ...), custom_call_target="tpu_custom_call" | custom-call | flops 20000000000 | bytes 10000000 | tf_op jit(solution)/shard_map/pallas_call | solution.py:1060
  267.5 58.3 %shard_map.551 = (f32[64,768]{1,0:T(8,128)}, f32[1,768]{1,0:T(1,128)}, bf16[768,576]{1,0:T(8,128)(2,1)}, bf16[192,768]{1,0:T(8,128)(2,1)}, f32[8,32]{1,0:T(8,128...) custom-call(bf16[64,768]{1,0:T(8,128)(2,1)} %refs_0_.4, ...), custom_call_target="tpu_custom_call" | custom-call | flops 20000000000 | bytes 10000000 | tf_op jit(solution)/shard_map/pallas_call | solution.py:1060
  328.0 33.9 %all-reduce.8.cloned.1.call-done = (bf16[4,96,1024]{2,1,0:T(8,128)(2,1)}, bf16[1,256,768]{2,1,0:T(8,128)(2,1)}, bf16[4,96,576]{2,1,0:T(8,128)(2,1)}, bf16[1,96,768]{2,1,0:T(8,128)(2,1)}) async-done(((bf16[4,96,1024]{2,1,0:T(8,128)(2,1)}, bf16[1,256,768]{2,1,0:T(8,128)(2,1)}, bf16[4,96,576]{2,1,0:T(8,128)(2,1)}, bf16[1,96,768]{2,1,0:T(8,128)(2,1)}), (bf16[4,96,1024]{2,1,0:T(8,128)(2,1)}, ...) | async-done | bytes 1769488 | tf_op jit(solution)/shard_map/psum | solution.py:1665
  362.0 50.8 %shard_map.552 = (f32[64,768]{1,0:T(8,128)}, f32[1,768]{1,0:T(1,128)}, bf16[768,576]{1,0:T(8,128)(2,1)}, bf16[192,768]{1,0:T(8,128)(2,1)}, f32[8,32]{1,0:T(8,128...) custom-call(bf16[64,768]{1,0:T(8,128)(2,1)} %refs_0_.5, ...), custom_call_target="tpu_custom_call" | custom-call | flops 20000000000 | bytes 10000000 | tf_op jit(solution)/shard_map/pallas_call | solution.py:1060
  415.4 0.9 copy.106
  417.7 1.0 reshape.357
  419.0 1.0 reshape.358
  420.2 1.0 reshape.359
  423.0 7.0 %all-reduce.6.cloned.1.call-done = (bf16[4,96,1024]{2,1,0:T(8,128)(2,1)}, bf16[1,256,768]{2,1,0:T(8,128)(2,1)}) async-done(((bf16[4,96,1024]{2,1,0:T(8,128)(2,1)}, bf16[1,256,768]{2,1,0:T(8,128)(2,1)}), (bf16[4,96,1024]{2,1,0:T(8,128)(2,1)}, bf16[1,256,768]{2,1,0:T(8,128)(2,1)})) %all-reduce.6.cloned.1.call-update) | async-done | bytes 1179664 | tf_op jit(solution)/shard_map/psum | solution.py:1665
  430.7 47.8 %shard_map.553 = (bf16[4,96,576]{2,1,0:T(8,128)(2,1)}, bf16[1,96,768]{2,1,0:T(8,128)(2,1)}, bf16[4,96,576]{2,1,0:T(8,128)(2,1)}, bf16[4,16,672]{2,1,0:T(8,128)(2,1)}, bf16[1,96,768]{2,1,0:T(8,128)(2,1)}) custom-call(bf16[4,2,96,576]{3,2,1,0:T(8,128)(2,1)} %bitcast.133, bf16[4,2,16,672]{3,2,1,0:T(8,128)(2,1)} %broadcast_in_dim.26.refs_1_, ...), custom_call_target="tpu_custom_call" | custom-call | flops 20000000000 | bytes 10000000 | tf_op jit(solution)/shard_map/pallas_call | solution.py:1019
  480.6 1.1 convert_element_type.76
  482.1 1.0 reshape.349
  483.3 1.0 reshape.350
  484.5 1.0 reshape.351
  486.0 1.0 reshape.354
  487.3 1.0 reshape.355
  488.5 1.0 reshape.356
  489.8 0.9 copy.104
  (187 shorter events, 28.8 us)
Async XLA Ops:
  7.2 2.5 copy-start.17
  7.2 2.8 copy-start.18
  7.2 3.0 copy-start.19
  7.2 354.7 %all-reduce.8.cloned.1.call-start = ((), (), s32[]{:S(2)}) async-start(), calls=%async_computation.1 | async-start | bytes 3637248 | tf_op jit(solution)/shard_map/psum | solution.py:1665
  8.5 2.0 copy-start.20
  10.4 1.7 copy-start.32
  12.9 23.8 %copy-start.24 = (s32[2048]{0:T(1024)S(1)}, s32[2048]{0:T(1024)}, u32[]{:S(2)}) copy-start(s32[2048]{0:T(1024)} %param.37) | copy-start | bytes 24580
  12.9 23.9 %copy-start.25 = (s32[2048]{0:T(1024)S(1)}, s32[2048]{0:T(1024)}, u32[]{:S(2)}) copy-start(s32[2048]{0:T(1024)} %param.38) | copy-start | bytes 24580
  12.9 26.2 %copy-start.26 = (s32[2,257]{1,0:T(2,128)S(1)}, s32[2,257]{1,0:T(2,128)}, u32[]{:S(2)}) copy-start(s32[2,257]{1,0:T(2,128)} %param.39) | copy-start | bytes 6172
  35.6 6.4 %copy-start.21 = (bf16[96,768]{1,0:T(8,128)(2,1)S(1)}, bf16[96,768]{1,0:T(8,128)(2,1)}, u32[]{:S(2)}) copy-start(bf16[96,768]{1,0:T(8,128)(2,1)} %param.59) | copy-start | bytes 442372
  35.6 6.7 %copy-start.22 = (bf16[96,768]{1,0:T(8,128)(2,1)S(1)}, bf16[96,768]{1,0:T(8,128)(2,1)}, u32[]{:S(2)}) copy-start(bf16[96,768]{1,0:T(8,128)(2,1)} %param.60) | copy-start | bytes 442372
  35.6 6.9 %copy-start.23 = (bf16[96,768]{1,0:T(8,128)(2,1)S(1)}, bf16[96,768]{1,0:T(8,128)(2,1)}, u32[]{:S(2)}) copy-start(bf16[96,768]{1,0:T(8,128)(2,1)} %param.58) | copy-start | bytes 442372
  42.0 2.7 copy-start.4
  42.0 2.7 copy-start.5
  266.5 163.5 %all-reduce.6.cloned.1.call-start = ((), (), s32[]{:S(2)}) async-start(), calls=%async_computation | async-start | bytes 2359296 | tf_op jit(solution)/shard_map/psum | solution.py:1665
  267.5 60.1 %copy-start.30 = (f32[1,768]{1,0:T(1,128)S(1)}, f32[1,768]{1,0:T(1,128)}, u32[]{:S(2)}) copy-start(f32[1,768]{1,0:T(1,128)} %get-tuple-element.193) | copy-start | bytes 9220
  267.5 60.2 %copy-start.29 = (f32[1,768]{1,0:T(1,128)S(1)}, f32[1,768]{1,0:T(1,128)}, u32[]{:S(2)}) copy-start(f32[1,768]{1,0:T(1,128)} %get-tuple-element.194) | copy-start | bytes 9220
  267.5 60.3 %copy-start.28 = (f32[1,768]{1,0:T(1,128)S(1)}, f32[1,768]{1,0:T(1,128)}, u32[]{:S(2)}) copy-start(f32[1,768]{1,0:T(1,128)} %get-tuple-element.196) | copy-start | bytes 9220
  267.5 60.4 %copy-start.27 = (f32[1,768]{1,0:T(1,128)S(1)}, f32[1,768]{1,0:T(1,128)}, u32[]{:S(2)}) copy-start(f32[1,768]{1,0:T(1,128)} %get-tuple-element.197) | copy-start | bytes 9220
  361.9 50.9 %copy-start.1 = (bf16[4,96,1024]{2,1,0:T(8,128)(2,1)S(1)}, bf16[4,96,1024]{2,1,0:T(8,128)(2,1)}, u32[]{:S(2)}) copy-start(bf16[4,96,1024]{2,1,0:T(8,128)(2,1)} %get-tuple-element.185) | copy-start | bytes 2359300
  412.8 2.3 copy-start.31
  418.7 2.6 copy-start.14
  418.7 3.3 copy-start.8
  483.1 2.5 copy-start.3
  487.0 2.5 copy-start
  489.8 1.9 copy-start.16
  489.8 2.7 copy-start.15
  490.8 2.4 copy-start.9
  490.8 3.4 copy-start.10
  491.7 3.1 copy-start.11
  491.7 3.8 copy-start.13
  491.7 4.5 copy-start.12
  (10 other events, 14.7 us)
Sparse Core Ops, SparseCore 0:
  266.7 95.2 all-reduce.7
  364.4 65.5 all-reduce.5

commit v5 on v4

--- a/solution.py
+++ b/solution.py
@@ -904,13 +904,24 @@
         return list(got)
 
 
+FOLD_PIECE = 56 * 1024
+
+
 class FoldPlanes:
     def __init__(self, arrays):
         self.operands = list(arrays)
         self.in_specs = [IN_VMEM] * len(arrays)
         self.outs = [(w.shape, jnp.bfloat16) for w in arrays]
         self.out_specs = [IN_VMEM] * len(arrays)
-        self.pieces = [(index, piece) for index, w in enumerate(arrays) for piece in range(w.shape[0])]
+        self.pieces = []
+        for index, w in enumerate(arrays):
+            cuts = next(c for c in (1, 2, 3, 4, 6, 8) if w.shape[1] // c * w.shape[2] <= FOLD_PIECE or c == 8)
+            if w.shape[0] * w.shape[1] * w.shape[2] <= FOLD_PIECE:
+                self.pieces.append((index, slice(None), pl.ds(0, w.shape[1])))
+                continue
+            rows = w.shape[1] // cuts
+            self.pieces += [(index, lead, pl.ds(c * rows, rows)) for lead in range(w.shape[0]) for c in range(cuts)]
+        self.inner_done = self.across_done = 0
         self.scratch = [pltpu.VMEM(w.shape, jnp.bfloat16) for _ in range(3) for w in arrays] + [DMA((len(self.pieces),))] * 6
 
     def bind(self, ins, outs, scratch):
@@ -926,11 +937,12 @@
         )
 
     def hops(self, place, number):
-        index, piece = self.pieces[number]
+        index, lead, rows = self.pieces[number]
         part = place.part
         inward, across, outward = (place.at_plane(p) for p in (1 + part // 3, 3 - part, 3 * (part - 1)))
-        ref, inner, sums = self.ins[index].at[piece], self.inner[index].at[piece], self.sums[index].at[piece]
-        other, total = self.across[index].at[piece], self.totals[index].at[piece]
+        ref, inner, sums, other, total = (
+            side[index].at[lead, rows] for side in (self.ins, self.inner, self.sums, self.across, self.totals)
+        )
         return (ref, inner, inward), (sums, other, across), (total, total, outward)
 
     def roles(self, place):
@@ -955,15 +967,31 @@
         outward[0][...] = low(across[0][...].astype(jnp.float32) + across[1][...].astype(jnp.float32))
         self.copy(2, number, *outward).start()
 
+    def of(self, first, last):
+        return [n for n, piece in enumerate(self.pieces) if first <= piece[0] < last]
+
     def serve(self, place, inner, across):
+        inners = list(range(self.inner_done, min(self.inner_done + inner, len(self.pieces))))
+        self.inner_done += len(inners)
+        others = list(range(self.across_done, min(self.across_done + across, len(self.pieces))))
+        self.across_done += len(others)
+
         @self.roles(place)[0]
         def _():
-            inners, others = list(inner), list(across)
-            while inners or others:
-                if inners:
-                    self.add_inner(place, inners.pop(0))
-                if others and (not inners or len(inners) < len(others) + 2):
-                    self.add_across(place, others.pop(0))
+            for turn in range(max(len(inners), len(others))):
+                if turn < len(inners):
+                    self.add_inner(place, inners[turn])
+                if turn < len(others):
+                    self.add_across(place, others[turn])
+
+    def finish(self, place, lag):
+        left = len(self.pieces) - self.inner_done
+        behind = self.inner_done - self.across_done
+        if behind > lag:
+            self.serve(place, 0, behind - lag)
+        self.serve(place, lag - min(behind, lag), 0)
+        self.serve(place, left, left)
+        self.serve(place, 0, len(self.pieces))
 
     def end(self, place):
         in_middle, at_end = self.roles(place)
@@ -984,48 +1012,6 @@
 
     def result(self, got):
         return list(got)
-
-
-def finish_kernel(sizes, give, fold, before, *refs):
-    refs = list(refs)
-
-    def take(count):
-        taken, refs[:] = refs[:count], refs[count:]
-        return taken
-
-    give_ins, ready = take(len(give.operands)), take(before)
-    totals = take(len(fold.outs))
-    given = take(len(give.outs))
-    give.bind(give_ins, given, take(len(give.scratch)))
-    fold.bind(ready + given, totals, take(len(fold.scratch)))
-    place = Place(*sizes)
-    place.greet(planes=True)
-    early = [n for n, (index, _) in enumerate(fold.pieces) if index < before]
-    last = [n for n, (index, _) in enumerate(fold.pieces) if index >= before]
-    first = early[: len(early) // 2]
-    give.begin(place)
-    fold.start(place, early)
-    give.middle(place)
-    fold.serve(place, first, [])
-    give.end(place)
-    fold.start(place, last)
-    fold.serve(place, early[len(first) :] + last, early + last)
-    fold.end(place)
-
-
-def finish(sizes, collective_id, give, arrays):
-    fold = FoldPlanes(list(arrays) + [jax.ShapeDtypeStruct(shape, dtype) for shape, dtype in give.outs])
-    count = len(arrays)
-    got = pl.pallas_call(
-        functools.partial(finish_kernel, sizes, give, fold, count),
-        out_shape=tuple(jax.ShapeDtypeStruct(shape, dtype) for shape, dtype in fold.outs),
-        in_specs=[IN_VMEM] * (len(give.operands) + count),
-        out_specs=(IN_VMEM,) * len(fold.outs),
-        scratch_shapes=[pltpu.VMEM(shape, dtype) for shape, dtype in give.outs] + give.scratch + fold.scratch,
-        compiler_params=pltpu.CompilerParams(collective_id=collective_id, has_side_effects=True, vmem_limit_bytes=VMEM_BYTES),
-        cost_estimate=pl.CostEstimate(flops=20_000_000_000, bytes_accessed=10_000_000, transcendentals=0),
-    )(*give.operands, *arrays)
-    return list(got[count:]), list(got[:count])
 
 
 def stage(sizes, collective_id, kernel, operands, outs, scratch, copies, job=None):
@@ -1112,60 +1098,34 @@
 
 
 def feed_both_kernel(
-    gain_at, place, run, x_ref, cot_ref, gains_ref, gu_ref, down_ref,
-    y_ref, dx_ref, dgain_ref, dgu_ref, ddown_ref,
-    n_buf, d_buf, py_buf, ry_buf, pn_buf, rn_buf, sent, got,
+    sizes, gain_at, give, x_ref, cot_ref, gains_ref, gu_ref, down_ref,
+    y_ref, dx_ref, dgain_ref, cols_ref, rows_ref,
+    n_buf, d_buf, py_buf, ry_buf, pn_buf, rn_buf, dgu_buf, ddown_buf, sent, got, *give_scratch,
 ):
+    place = Place(*sizes)
+    give.bind([dgu_buf, ddown_buf], [cols_ref, rows_ref], give_scratch)
     place.greet()
     x = x_ref[...]
     d_buf[place.group] = cot_ref[...]
     pending = spread_start(place, d_buf, sent.at[1], got.at[1])
     n_buf[place.group] = low(rms_norm(x, gains_ref[gain_at]))
     pending += spread_start(place, n_buf, sent.at[0], got.at[0])
-    run("begin")
+    spread_wait(place, d_buf, sent.at[1], got.at[1])
     spread_wait(place, n_buf, sent.at[0], got.at[0])
-    spread_wait(place, d_buf, sent.at[1], got.at[1])
     n, dyb = all_rows(n_buf), all_rows(d_buf)
     h, dgu = feed_back_part(n, dyb, gu_ref, down_ref)
     pending += collect_start(place, nt(dgu, gu_ref[...]), pn_buf, rn_buf, sent.at[2], got.at[2])
+    dgu_buf[...] = low(tn(n, dgu)).reshape(dgu_buf.shape)
+    ddown_buf[...] = low(tn(h, dyb)).reshape(ddown_buf.shape)
+    give.begin(place)
     pending += collect_start(place, nn(h, down_ref[...]), py_buf, ry_buf, sent.at[3], got.at[3])
-    dgu_ref[...] = low(tn(n, dgu))
-    ddown_ref[...] = low(tn(h, dyb))
-    run("middle")
     dn = collect_wait(place, pn_buf, rn_buf, sent.at[2], got.at[2])
+    give.middle(place)
     back, dgain = norm_back(x, gains_ref[gain_at], dn)
     dx_ref[...] = cot_ref[...].astype(jnp.float32) + back
     dgain_ref[...] = dgain
     y_ref[...] = x + collect_wait(place, py_buf, ry_buf, sent.at[3], got.at[3])
-    run("end")
-    for copy in pending:
-        copy.wait_send()
-
-
-def feed_back_kernel(
-    gain_at, final_at, place, run, x_ref, y_ref, cot_ref, dlast_ref, gains_ref, n_ref, gu_ref, down_ref,
-    dx_ref, dgain_ref, dfinal_ref, dgu_ref, ddown_ref,
-    d_buf, pn_buf, rn_buf, sent, got,
-):
-    place.greet()
-    back, dfinal = norm_back(y_ref[...], gains_ref[final_at], dlast_ref[...])
-    dfinal_ref[...] = dfinal
-    dy = cot_ref[...].astype(jnp.float32) + back
-    d_buf[place.group] = low(dy)
-    pending = spread_start(place, d_buf, sent.at[0], got.at[0])
-    run("begin")
-    spread_wait(place, d_buf, sent.at[0], got.at[0])
-    n, dyb = n_ref[...], all_rows(d_buf)
-    h, dgu = feed_back_part(n, dyb, gu_ref, down_ref)
-    pending += collect_start(place, nt(dgu, gu_ref[...]), pn_buf, rn_buf, sent.at[1], got.at[1])
-    dgu_ref[...] = low(tn(n, dgu))
-    ddown_ref[...] = low(tn(h, dyb))
-    run("middle")
-    dn = collect_wait(place, pn_buf, rn_buf, sent.at[1], got.at[1])
-    back, dgain = norm_back(x_ref[...], gains_ref[gain_at], dn)
-    dx_ref[...] = dy + back
-    dgain_ref[...] = dgain
-    run("end")
+    give.end(place)
     for copy in pending:
         copy.wait_send()
 
@@ -1388,7 +1348,7 @@
     return results, given
 
 
-def mix_back_part(place, q, do, kv_ref, lse_ref, bm_ref, biased, dkv_ref, p_ref, dp_ref, ds_ref, pb_ref, ot_ref):
+def mix_back_part(place, q, do, o, kv_ref, lse_ref, bm_ref, dkv_ref, ds_ref):
     chunks, cores, parts, block, lanes = kv_ref.shape
     rows = chunk_rows(kv_ref)
     queries, width = q.shape
@@ -1400,52 +1360,45 @@
     across = [slice(head * queries, (head + 1) * queries) for head in range(heads)]
     masked_q = [only_lanes(q, head * HD, HD) for head in range(heads)]
     masked_do = [only_lanes(do_wide, lead + head * HD, HD) for head in range(heads)]
+    q_wide = masked_q
+    if lead:
+        none = jnp.zeros((queries, lead), q.dtype)
+        q_wide = [jnp.concatenate([one, none], axis=1) for one in masked_q]
+    of_head = lax.broadcasted_iota(jnp.int32, (8, width), 1) // HD
+    of_row = lax.broadcasted_iota(jnp.int32, (8, width), 0)
+    inners = lax.dot_general(
+        jnp.where(of_head == of_row, 1.0, 0.0), do.astype(jnp.float32) * o.astype(jnp.float32),
+        (((1,), (1,)), ((), ())), precision=HIGHEST, preferred_element_type=jnp.float32,
+    )
     nothing = jnp.zeros((1, queries), jnp.float32)
-    if biased:
-        none = jnp.zeros((BLOCK_PAD, heads * queries), jnp.bfloat16)
-        ds_ref[0:BLOCK_PAD, :] = none
-        ds_ref[BLOCK_PAD + chunks * rows :, :] = none
+    if ds_ref is not None:
+        empty = jnp.zeros((BLOCK_PAD, heads * queries), jnp.bfloat16)
+        ds_ref[0:BLOCK_PAD, :] = empty
+        ds_ref[BLOCK_PAD + chunks * rows :, :] = empty
         of_lane = lax.broadcasted_iota(jnp.int32, (1, queries), 1) // block
         lane_start = ((cores * of_lane + place.core) * parts + place.part) * block
 
-    def first(chunk, inners):
+    def chunk_step(chunk, carried):
+        at = pl.multiple_of(chunk * rows, rows)
         keys, values = key_side(kv_ref, chunk), value_side(kv_ref, chunk)
-        inside = pl.ds(pl.multiple_of(chunk * rows, rows), rows)
-        new = []
+        keys_t = low(nt(identity(width), keys))
+        new, dk, dv = [], None, None
         for head in range(heads):
+            left, right, back = carried[head]
             scores = nt(keys, masked_q[head]) + bias_rows(bm_ref, head, chunk, rows)
             p = jnp.exp(scores - lse_ref[:, across[head]])
             dp = nt(values, masked_do[head])
-            p_ref[inside, across[head]] = p
-            dp_ref[inside, across[head]] = dp
-            pb_ref[inside, across[head]] = low(p)
-            new.append(inners[head] + jnp.sum(p * dp, axis=0, keepdims=True))
-        return tuple(new)
-
-    inners = lax.fori_loop(0, chunks, first, (nothing,) * heads)
-    stacked_q = jnp.concatenate(masked_q, axis=0)
-    if lead:
-        stacked_q = jnp.concatenate([stacked_q, jnp.zeros((stacked_q.shape[0], lead), stacked_q.dtype)], axis=1)
-    stacked_do = jnp.concatenate(masked_do, axis=0)
-
-    def second(chunk, carried):
-        at = pl.multiple_of(chunk * rows, rows)
-        inside, padded = pl.ds(at, rows), pl.ds(pl.multiple_of(BLOCK_PAD + at, 128), rows)
-        keys_t = low(nt(identity(width), key_side(kv_ref, chunk)))
-        new = []
-        for head in range(heads):
-            left, right, back = carried[head]
-            ds = low(p_ref[inside, across[head]] * (dp_ref[inside, across[head]] - inners[head]))
-            ds_ref[padded, across[head]] = ds
-            back = back + nn(keys_t[head * HD : (head + 1) * HD], ds)
-            if biased:
+            ds = low(p * (dp - inners[head : head + 1, :]))
+            if ds_ref is not None:
+                ds_ref[pl.ds(pl.multiple_of(BLOCK_PAD + at, 128), rows), across[head]] = ds
                 wide = ds.astype(jnp.float32)
                 places = lax.broadcasted_iota(jnp.int32, wide.shape, 0) + (at + BLOCK_PAD)
                 left = left + jnp.sum(jnp.where(places < lane_start, wide, 0.0), axis=0, keepdims=True)
                 right = right + jnp.sum(jnp.where(places >= lane_start + strip, wide, 0.0), axis=0, keepdims=True)
+            back = back + nn(keys_t[head * HD : (head + 1) * HD], ds)
             new.append((left, right, back))
-        dk = nn(ds_ref[padded, :], stacked_q)
-        dv = nn(pb_ref[inside, :], stacked_do)
+            more_k, more_v = nn(ds, q_wide[head]), nn(low(p), masked_do[head])
+            dk, dv = (more_k, more_v) if dk is None else (dk + more_k, dv + more_v)
         if lead:
             shared = dk[:, first_value:] + dv[:, : 2 * lead]
             both = jnp.concatenate([dk[:, :first_value], shared, dv[:, 2 * lead :]], axis=1)
@@ -1455,10 +1408,8 @@
         return tuple(new)
 
     start = (nothing, nothing, jnp.zeros((HD, queries), jnp.float32))
-    done = lax.fori_loop(0, chunks, second, (start,) * heads)
-    for head in range(heads):
-        ot_ref[head * HD : (head + 1) * HD, :] = low(done[head][2])
-    return low(nt(identity(queries), ot_ref[...])), done
+    done = lax.fori_loop(0, chunks, chunk_step, (start,) * heads)
+    return [one[2] for one in done], [one[:2] for one in done]
 
 
 def table_grads(place, block, done, ds_ref, ahead_ref, rel_ref):
@@ -1470,7 +1421,7 @@
     backwards = jnp.where(rows + cols == block - 1, 1.0, 0.0)
     at = lax.broadcasted_iota(jnp.int32, (1, width), 1)
     sums = []
-    for head, (left, right, _) in enumerate(done):
+    for head, (left, right) in enumerate(done):
         total = jnp.zeros((strip, block), jnp.float32)
         for number in range(queries // block):
             low_at = head * queries + number * block
@@ -1484,96 +1435,376 @@
         left, right = (jnp.sum(side, axis=1, keepdims=True) for side in (left, right))
         sums.append(by_distance + jnp.where(at == 0, left, 0.0) + jnp.where(at == width - 2, right, 0.0))
     sums = jnp.concatenate(sums + [jnp.zeros((8 - len(sums), width), jnp.float32)], axis=0)
+    by_bucket = lax.dot_general(
+        sums, ahead_ref[...], (((1,), (1,)), ((), ())), precision=HIGHEST, preferred_element_type=jnp.float32
+    )
+    head_rows = lax.broadcasted_iota(jnp.int32, (8, 128), 0)
+    head_lanes = lax.broadcasted_iota(jnp.int32, (8, 128), 1)
+    lanes_of = (head_lanes == head_rows + place.group * len(done)) & (head_rows < len(done))
     rel_ref[...] = lax.dot_general(
-        sums, ahead_ref[...], (((1,), (1,)), ((), ())), precision=HIGHEST, preferred_element_type=jnp.float32
-    )
-
-
-def attend_back_kernel(cross, gain_at, which, place, run, *refs):
-    refs = list(refs)
-
-    def take(count):
-        taken, refs[:] = refs[:count], refs[count:]
+        by_bucket, jnp.where(lanes_of, 1.0, 0.0), (((0,), (0,)), ((), ())), precision=HIGHEST, preferred_element_type=jnp.float32
+    )
+
+
+class AttendBack:
+    OPERANDS = 11
+
+    def __init__(self, place, ins, grads, scratch, cross):
+        self.place, self.cross = place, cross
+        self.x, self.n, self.q, self.kv, self.o, self.lse, self.w, self.wo, self.bm, self.source, self.ahead = ins
+        self.dw, self.dwo = grads
+        self.dkv, self.sib, self.zout, self.zin, self.d_buf, self.pn, self.rn, self.dq = scratch[:8]
+        scratch = scratch[8:]
+        self.pm, self.rm = (scratch.pop(0), scratch.pop(0)) if cross else (None, None)
+        self.ds = None if cross else scratch.pop(0)
+        self.sent, self.got = scratch
+        self.kv_width = self.kv.shape[4]
+        self.pending = []
+
+    def begin(self, dy):
+        self.d_buf[self.place.group] = low(dy)
+        self.pending += spread_start(self.place, self.d_buf, self.sent.at[0], self.got.at[0])
+
+    def arrive(self):
+        spread_wait(self.place, self.d_buf, self.sent.at[0], self.got.at[0])
+
+    def compute(self):
+        place, sent, got = self.place, self.sent, self.got
+        do = low(nt(all_rows(self.d_buf), self.wo[...]))
+        back, self.edges = mix_back_part(
+            place, self.q[...], do, self.o[...], self.kv, self.lse, self.bm, self.dkv, self.ds
+        )
+        self.pending.append(
+            send(self.dkv.at[:, 1 - place.core], self.sib, sent.at[1, 0], got.at[1, 0], place.sibling())
+        )
+        self.dq[...] = low(nt(identity(self.q.shape[0]), low(jnp.concatenate(back, axis=0))))
+        if self.cross:
+            share = nt(self.dq[...], self.w[:, self.kv_width :])
+            self.pending += collect_start(place, share, self.pn, self.rn, sent.at[3], got.at[3])
+
+    def exchange(self):
+        place, sent, got = self.place, self.sent, self.got
+        arrived(self.sib, sent.at[1, 0], got.at[1, 0], place.sibling())
+        for step in list(range(1, place.parts)) + [0]:
+            to = place.plane(step)
+            self.zout[to] = low(self.dkv[:, place.core, to].astype(jnp.float32) + self.sib[:, to].astype(jnp.float32))
+            if step:
+                self.pending.append(
+                    send(self.zout.at[to], self.zin.at[place.part], sent.at[2, step], got.at[2, step], place.at_plane(to))
+                )
+
+    def by_rows(self, grad):
+        return low(grad).reshape(self.dw.shape[:3] + grad.shape[1:])
+
+    def query_grads(self, rel):
+        self.dwo[...] = low(tn(self.o[...], all_rows(self.d_buf))).reshape(self.dwo.shape)
+        self.dw[:, :, :, self.kv_width :] = self.by_rows(tn(self.n[...], self.dq[...]))
+        if not self.cross:
+            table_grads(self.place, self.x.shape[0], self.edges, self.ds, self.ahead, rel)
+
+    def keys(self):
+        place, sent, got = self.place, self.sent, self.got
+        total = self.zout[place.part].astype(jnp.float32)
+        for step in range(1, place.parts):
+            source = place.plane_behind(step)
+            arrived(self.zin.at[source], sent.at[2, step], got.at[2, step], place.at_plane(source))
+            total = total + self.zin[source].astype(jnp.float32)
+        self.dkv_own = low(total).reshape(self.q.shape[0], self.kv_width)
+        share = nt(self.dkv_own, self.w[:, : self.kv_width])
+        if self.cross:
+            self.pending += collect_start(place, share, self.pm, self.rm, sent.at[4], got.at[4])
+        else:
+            share = share + nt(self.dq[...], self.w[:, self.kv_width :])
+            self.pending += collect_start(place, share, self.pn, self.rn, sent.at[3], got.at[3])
+
+    def key_grads(self):
+        self.dw[:, :, :, : self.kv_width] = self.by_rows(tn(self.source[...], self.dkv_own))
+
+    def source_grad(self):
+        return collect_wait(self.place, self.pm, self.rm, self.sent.at[4], self.got.at[4])
+
+    def normed_grad(self):
+        return collect_wait(self.place, self.pn, self.rn, self.sent.at[3], self.got.at[3])
+
+    def wait(self):
+        for copy in self.pending:
+            copy.wait_send()
+
+
+def attend_back_scratch(sizes, kv, block, model, width, cross):
+    groups, cores, parts = sizes
+    tokens = groups * block
+    turned, buffer = (parts, groups, block, 2 * width), (groups, block, model)
+    shapes = [kv, (groups, parts, block, 2 * width), turned, turned, buffer, buffer, buffer, (tokens, width)]
+    if cross:
+        shapes += [buffer, buffer]
+    else:
+        shapes.append((cores * parts * tokens + 2 * BLOCK_PAD, width // HD * tokens))
+    return [pltpu.VMEM(shape, jnp.bfloat16) for shape in shapes] + [DMA((5, max(groups, parts)))] * 2
+
+
+def give_on(sizes, cols, rows):
+    job = GiveRows.__new__(GiveRows)
+    job.cols, job.rows = len(cols), len(rows)
+    own = [(s[0],) + s[2:] for s in cols] + [(1,) + s[1:] for s in rows]
+    job.outs = [(shape, jnp.bfloat16) for shape in own]
+    job.scratch = [pltpu.VMEM(shape, jnp.bfloat16) for shape in own + own[: job.cols]]
+    job.scratch += [DMA((job.cols, sizes[0]))] * 4 + [DMA((job.rows,))] * 2
+    return job
+
+
+class Taker:
+    def __init__(self, refs):
+        self.refs = list(refs)
+
+    def __call__(self, count):
+        taken, self.refs = self.refs[:count], self.refs[count:]
         return taken
 
-    x_ref, gain_ref, dy_ref, n_ref, q_ref, kv_ref, o_ref, lse_ref, w_ref, wo_ref, bm_ref = take(11)
-    memory_ref, ahead_ref = (take(1)[0], None) if cross else (None, take(1)[0])
-    dx_ref, dgain_ref, dw_ref, dwo_ref = take(4)
-    dmem_ref, rel_ref = (take(1)[0], None) if cross else (None, take(1)[0])
-    p_ref, dp_ref, ds_ref, pb_ref, ot_ref, dkv_ref, sib_ref, zout_ref, zin_ref, d_buf, pn_buf, rn_buf = take(12)
-    pm_buf, rm_buf = take(2) if cross else (None, None)
-    sent, got = take(2)
+
+def decoder_back_kernel(sizes, gain_at, plans, *refs):
+    give_b, give_c, fold, cross_scratch, self_scratch = plans
+    dec1, dec2, enc2, final = gain_at
+    take = Taker(refs)
+    gains, grad_cx = take(2)
+    cross_ins, self_ins = take(AttendBack.OPERANDS), take(AttendBack.OPERANDS)
+    ex, enc_out, enc_cot, en2, gu, down, *a_ins = take(6 + len(fold.outs) - len(give_b.outs))
+    dec_in_grad, grad_ex, dg_d1, dg_d2, dg_e2, dg_ef, rel_d, dw_d, dwo_d = take(9)
+    totals, c_outs = take(len(fold.outs)), take(len(give_c.outs))
+    dw_c, dwo_c, dgu, ddown, grad_dx = take(5)
+    f_buf, pf, rf, f_sent, f_got = take(5)
+    place = Place(*sizes)
+    cross = AttendBack(place, cross_ins, (dw_c, dwo_c), take(len(cross_scratch)), True)
+    own = AttendBack(place, self_ins, (dw_d, dwo_d), take(len(self_scratch)), False)
+    b_outs = take(len(give_b.outs))
+    fold.bind(a_ins + b_outs, totals, take(len(fold.scratch)))
+    give_b.bind([dw_c, dwo_c], b_outs, take(len(give_b.scratch)))
+    give_c.bind([dgu, ddown], c_outs, take(len(give_c.scratch)))
+    of_a, of_b = fold.of(0, len(a_ins)), fold.of(len(a_ins), len(fold.outs))
     place.greet(planes=True)
-    dy = dy_ref[...]
-    d_buf[place.group] = low(dy)
-    pending = spread_start(place, d_buf, sent.at[0], got.at[0])
-    run("begin")
-    spread_wait(place, d_buf, sent.at[0], got.at[0])
-    dyb = all_rows(d_buf)
-    do = low(nt(dyb, wo_ref[...]))
-    dq, done = mix_back_part(
-        place, q_ref[...], do, kv_ref, lse_ref, bm_ref, not cross, dkv_ref, p_ref, dp_ref, ds_ref, pb_ref, ot_ref
-    )
-    mine = place.core
-    pending.append(send(dkv_ref.at[:, 1 - mine], sib_ref, sent.at[1, 0], got.at[1, 0], place.sibling()))
-    kv_width = kv_ref.shape[4]
-    dn_share = nt(dq, w_ref[:, kv_width:])
-    if cross:
-        pending += collect_start(place, dn_share, pn_buf, rn_buf, sent.at[3], got.at[3])
-    arrived(sib_ref, sent.at[1, 0], got.at[1, 0], place.sibling())
-    for step in list(range(1, place.parts)) + [0]:
-        to = place.plane(step)
-        zout_ref[to] = low(dkv_ref[:, mine, to].astype(jnp.float32) + sib_ref[:, to].astype(jnp.float32))
-        if step:
-            pending.append(send(zout_ref.at[to], zin_ref.at[place.part], sent.at[2, step], got.at[2, step], place.at_plane(to)))
-    run("middle")
-    dwo_ref[...] = low(tn(o_ref[...], dyb))
-    dw_ref[:, kv_width:] = low(tn(n_ref[...], dq))
-    if not cross:
-        table_grads(place, dy_ref.shape[0], done, ds_ref, ahead_ref.at[which], rel_ref)
-    total = zout_ref[place.part].astype(jnp.float32)
-    for step in range(1, place.parts):
-        source = place.plane_behind(step)
-        arrived(zin_ref.at[source], sent.at[2, step], got.at[2, step], place.at_plane(source))
-        total = total + zin_ref[source].astype(jnp.float32)
-    dkv = low(total).reshape(q_ref.shape[0], kv_width)
-    if cross:
-        pending += collect_start(place, nt(dkv, w_ref[:, :kv_width]), pm_buf, rm_buf, sent.at[4], got.at[4])
-        dw_ref[:, :kv_width] = low(tn(memory_ref[...], dkv))
-        dmem_ref[...] = collect_wait(place, pm_buf, rm_buf, sent.at[4], got.at[4])
-    else:
-        share = dn_share + nt(dkv, w_ref[:, :kv_width])
-        pending += collect_start(place, share, pn_buf, rn_buf, sent.at[3], got.at[3])
-        dw_ref[:, :kv_width] = low(tn(n_ref[...], dkv))
-    dn = collect_wait(place, pn_buf, rn_buf, sent.at[3], got.at[3])
-    back, dgain = norm_back(x_ref[...].astype(jnp.float32), gain_ref[gain_at], dn)
-    dx_ref[...] = dy + back
-    dgain_ref[...] = dgain
-    run("end")
+    cross.begin(grad_cx[...])
+    fold.start(place, of_a)
+    cross.arrive()
+    fold.serve(place, 2, 0)
+    cross.compute()
+    fold.serve(place, 3, 2)
+    cross.exchange()
+    fold.serve(place, 2, 2)
+    back, dg = norm_back(cross.x[...].astype(jnp.float32), gains[dec2], cross.normed_grad())
+    dg_d2[...] = dg
+    grad_dx[...] = grad_cx[...] + back
+    own.begin(grad_dx[...])
+    cross.query_grads(None)
+    own.arrive()
+    fold.serve(place, len(of_a) - 7, 3)
+    own.compute()
+    fold.serve(place, 0, len(of_a) - 7)
+    cross.keys()
+    own.exchange()
+    cross.key_grads()
+    give_b.begin(place)
+    back, dg = norm_back(enc_out[...], gains[final], cross.source_grad())
+    dg_ef[...] = dg
+    dy = enc_cot[...].astype(jnp.float32) + back
+    f_buf[place.group] = low(dy)
+    pending = spread_start(place, f_buf, f_sent.at[0], f_got.at[0])
+    give_b.middle(place)
+    own.query_grads(rel_d)
+    spread_wait(place, f_buf, f_sent.at[0], f_got.at[0])
+    give_b.end(place)
+    fold.start(place, of_b)
+    n, dyb = en2[...], all_rows(f_buf)
+    h, dgu_value = feed_back_part(n, dyb, gu, down)
+    pending += collect_start(place, nt(dgu_value, gu[...]), pf, rf, f_sent.at[1], f_got.at[1])
+    dgu[...] = low(tn(n, dgu_value)).reshape(dgu.shape)
+    ddown[...] = low(tn(h, dyb)).reshape(ddown.shape)
+    give_c.begin(place)
+    fold.serve(place, 2, 0)
+    dn = collect_wait(place, pf, rf, f_sent.at[1], f_got.at[1])
+    back, dg = norm_back(ex[...], gains[enc2], dn)
+    dg_e2[...] = dg
+    grad_ex[...] = dy + back
+    give_c.middle(place)
+    fold.serve(place, 2, 1)
+    own.keys()
+    own.key_grads()
+    fold.finish(place, 2)
+    back, dg = norm_back(own.x[...].astype(jnp.float32), gains[dec1], own.normed_grad())
+    dg_d1[...] = dg
+    dec_in_grad[...] = grad_dx[...] + back
+    give_c.end(place)
+    fold.end(place)
+    cross.wait()
+    own.wait()
     for copy in pending:
         copy.wait_send()
 
 
-def attend_back(sizes, collective_id, x, gains, gain_at, dy, kept, w, wo, ahead, which, job=None):
-    cross = ahead is None
+def encoder_back_kernel(sizes, gain_at, plans, *refs):
+    give_d, give_e, fold, before, scratch = plans
+    take = Taker(refs)
+    gains, grad_ex = take(2)
+    ins = take(AttendBack.OPERANDS)
+    dg_d1, dg_d2, dg_d3, dg_e2, dg_ef, rel_d = take(6)
+    ready, d_ins = take(before), take(give_d.cols + give_d.rows)
+    (enc_in_grad,) = take(1)
+    totals = take(len(fold.outs))
+    dw_e, dwo_e, small, rel_e = take(4)
+    place = Place(*sizes)
+    own = AttendBack(place, ins, (dw_e, dwo_e), take(len(scratch)), False)
+    d_outs, e_outs = take(len(give_d.outs)), take(len(give_e.outs))
+    give_d.bind(d_ins, d_outs, take(len(give_d.scratch)))
+    give_e.bind([dw_e, small, dwo_e], e_outs, take(len(give_e.scratch)))
+    fold.bind(ready + d_outs + e_outs, totals, take(len(fold.scratch)))
+    of_c = fold.of(0, before)
+    of_d, of_e = fold.of(before, before + len(d_outs)), fold.of(before + len(d_outs), len(fold.outs))
+    place.greet(planes=True)
+    own.begin(grad_ex[...])
+    fold.start(place, of_c)
+    give_d.begin(place)
+    give_d.middle(place)
+    own.arrive()
+    fold.serve(place, 2, 0)
+    own.compute()
+    fold.serve(place, 3, 2)
+    own.exchange()
+    give_d.end(place)
+    fold.start(place, of_d)
+    fold.serve(place, 2, 2)
+    own.query_grads(rel_e)
+    fold.serve(place, 2, 2)
+    own.keys()
+    fold.serve(place, len(of_c) - 9, 3)
+    own.key_grads()
+    dn = own.normed_grad()
+    back, dg_e1 = norm_back(own.x[...].astype(jnp.float32), gains[gain_at], dn)
+    enc_in_grad[...] = grad_ex[...] + back
+    devices = place.groups * place.cores
+    share = dg_e1.shape[1] // devices
+    small[...] = jnp.zeros_like(small)
+    all_gains = jnp.concatenate([dg_e1, dg_e2[...], dg_ef[...], dg_d1[...], dg_d2[...], dg_d3[...]], axis=0)
+    count = all_gains.shape[0]
+    each = rel_e.shape[0] // devices
+    tables = [rel_e[...].reshape(devices, each, 128), rel_d[...].reshape(devices, each, 128)]
+    for device in range(devices):
+        piece = jnp.concatenate([all_gains[:, device * share : (device + 1) * share], jnp.zeros((count, 128 - share), jnp.float32)], axis=1)
+        rows = jnp.concatenate([piece, tables[0][device], tables[1][device]], axis=0)
+        rows = jnp.concatenate([rows, jnp.zeros((16 - rows.shape[0], 128), jnp.float32)], axis=0)
+        small[device // place.cores, device % place.cores] = low(rows)
+    give_e.begin(place)
+    fold.serve(place, 2, len(of_c) - 9)
+    give_e.middle(place)
+    fold.serve(place, len(of_d) - 2, 2)
+    give_e.end(place)
+    fold.start(place, of_e)
+    fold.finish(place, 2)
+    fold.end(place)
+    own.wait()
+
+
+def fused(sizes, collective_id, kernel, operands, outs, scratch):
+    return pl.pallas_call(
+        functools.partial(kernel, sizes),
+        out_shape=tuple(jax.ShapeDtypeStruct(shape, dtype) for shape, dtype in outs),
+        in_specs=[IN_VMEM] * len(operands),
+        out_specs=(IN_VMEM,) * len(outs),
+        scratch_shapes=scratch,
+        compiler_params=pltpu.CompilerParams(collective_id=collective_id, has_side_effects=True, vmem_limit_bytes=VMEM_BYTES),
+        cost_estimate=pl.CostEstimate(flops=20_000_000_000, bytes_accessed=10_000_000, transcendentals=0),
+    )(*operands)
+
+
+def kept_operands(x, kept, w, wo, ahead):
+    _, n, q, kv, o, lse, bm, memory = kept
+    if ahead is None:
+        return [x, n, q, kv, o, lse, w, wo, bm, memory, memory]
+    return [x, n, q, kv, o, lse, w, wo, bm, n, ahead]
+
+
+def buffers_of(shapes):
+    return [pltpu.VMEM(shape, jnp.bfloat16) for shape in shapes]
+
+
+def decoder_back(sizes, collective_id, gains, gain_at, grad_cx, cross, own, feed, rows_a):
     groups, cores, parts = sizes
-    _, n, q, kv, o, lse, bm, memory = kept
-    block, model = x.shape
-    tokens, width = q.shape
-    heads = width // HD
-    keys = cores * parts * tokens
     f32, bf16 = jnp.float32, jnp.bfloat16
-    operands = [x, gains, dy, n, q, kv, o, lse, w, wo, bm] + [memory if cross else ahead]
-    outs = [((block, model), f32), ((1, model), f32), (w.shape, bf16), (wo.shape, bf16)]
-    outs.append(((block, model) if cross else (8, ahead.shape[1]), f32))
-    turned = (parts, groups, block, 2 * width)
-    scratch = [
-        pltpu.VMEM((keys, heads * tokens), f32), pltpu.VMEM((keys, heads * tokens), f32),
-        (keys + 2 * BLOCK_PAD, heads * tokens), (keys, heads * tokens), (width, tokens),
-        kv.shape, (groups, parts, block, 2 * width), turned, turned,
-    ] + [(groups, block, model)] * (5 if cross else 3)
-    copies = (5, max(groups, parts))
-    return stage(sizes, collective_id, functools.partial(attend_back_kernel, cross, gain_at, which), operands, outs, scratch, copies, job)
+    block, model = grad_cx.shape
+    share = model // (groups * cores)
+    width = cross[3].shape[0]
+    kv = cross[1][3].shape
+    hidden = feed[5].shape[0]
+    attention = [(groups, cores, share, 3 * width)], [(cores, width // cores, model)]
+    feeds = [(groups, cores, share, 2 * hidden)], [(cores, hidden // cores, model)]
+    give_b, give_c = give_on(sizes, *attention), give_on(sizes, *feeds)
+    fold = FoldPlanes(list(rows_a) + [jax.ShapeDtypeStruct(shape, dtype) for shape, dtype in give_b.outs])
+    cross_scratch = attend_back_scratch(sizes, kv, block, model, width, True)
+    self_scratch = attend_back_scratch(sizes, kv, block, model, width, False)
+    plans = (give_b, give_c, fold, cross_scratch, self_scratch)
+    operands = [gains, grad_cx] + kept_operands(*cross) + kept_operands(*own) + list(feed) + list(rows_a)
+    token, gain = ((block, model), f32), ((1, model), f32)
+    outs = [token, token, gain, gain, gain, gain, ((own[4].shape[0], 128), f32)]
+    outs += [(attention[0][0], bf16), (attention[1][0], bf16)] + fold.outs + give_c.outs
+    buffer = (groups, block, model)
+    scratch = buffers_of(attention[0] + attention[1] + feeds[0] + feeds[1]) + [pltpu.VMEM((block, model), f32)]
+    scratch += buffers_of([buffer] * 3) + [DMA((2, groups))] * 2 + cross_scratch + self_scratch
+    scratch += buffers_of([shape for shape, _ in give_b.outs]) + fold.scratch + give_b.scratch + give_c.scratch
+    got = Taker(fused(sizes, collective_id, lambda s, *refs: decoder_back_kernel(s, gain_at, plans, *refs), operands, outs, scratch))
+    first = got(7)
+    return first, got(2), got(len(rows_a)), got(len(give_b.outs)), got(len(give_c.outs))
+
+
+def encoder_back(sizes, collective_id, gains, gain_at, grad_ex, own, small_grads, ready, grads_d):
+    groups, cores, parts = sizes
+    f32 = jnp.float32
+    block, model = grad_ex.shape
+    share = model // (groups * cores)
+    width = own[3].shape[0]
+    kv = own[1][3].shape
+    give_d = GiveRows.__new__(GiveRows)
+    give_d = give_on(sizes, [grads_d[0].shape], [grads_d[1].shape])
+    cols = [(groups, cores, share, 3 * width), (groups, cores, 16, 128)]
+    rows = [(cores, width // cores, model)]
+    give_e = give_on(sizes, cols, rows)
+    all_outs = [jax.ShapeDtypeStruct(shape, dtype) for shape, dtype in give_d.outs + give_e.outs]
+    fold = FoldPlanes(list(ready) + all_outs)
+    scratch = attend_back_scratch(sizes, kv, block, model, width, False)
+    plans = (give_d, give_e, fold, len(ready), scratch)
+    operands = [gains, grad_ex] + kept_operands(*own) + list(small_grads) + list(ready) + list(grads_d)
+    buffers = buffers_of([cols[0], rows[0], cols[1]]) + [pltpu.VMEM((own[4].shape[0], 128), f32)] + scratch
+    buffers += buffers_of([shape for shape, _ in give_d.outs]) + buffers_of([shape for shape, _ in give_e.outs])
+    buffers += give_d.scratch + give_e.scratch + fold.scratch
+    outs = [((block, model), f32)] + fold.outs
+    got = Taker(fused(sizes, collective_id, lambda s, *refs: encoder_back_kernel(s, gain_at, plans, *refs), operands, outs, buffers))
+    return got(1)[0], got(len(ready)), got(2), got(3)
+
+
+def unpack_kernel(kinds, *refs):
+    take = Taker(refs)
+    ins = take(len(kinds))
+    for ref, pieces in zip(ins, kinds):
+        value = ref[...].astype(jnp.float32)
+        if pieces == 0:
+            take(1)[0][...] = value[0]
+            continue
+        each = value.shape[2] // pieces
+        for piece, out in enumerate(take(pieces)):
+            out[...] = jnp.concatenate([one[:, piece * each : (piece + 1) * each] for one in value], axis=1)
+
+
+def unpack(arrays, kinds):
+    outs = []
+    for array, pieces in zip(arrays, kinds):
+        if pieces == 0:
+            outs.append(jax.ShapeDtypeStruct(array.shape[1:], jnp.float32))
+        for _ in range(pieces):
+            outs.append(jax.ShapeDtypeStruct((array.shape[1], array.shape[0] * array.shape[2] // pieces), jnp.float32))
+    return pl.pallas_call(
+        functools.partial(unpack_kernel, kinds),
+        out_shape=tuple(outs),
+        in_specs=[IN_VMEM] * len(arrays),
+        out_specs=(IN_VMEM,) * len(outs),
+        compiler_params=pltpu.CompilerParams(vmem_limit_bytes=VMEM_BYTES),
+    )(*arrays)
 
 
 def fast_device(
@@ -1583,20 +1814,22 @@
     dec_norm3, dec_gate, dec_up, dec_down,
 ):
     groups, cores, parts = sizes = lax.axis_size(HG), lax.axis_size(CORE), lax.axis_size(SP)
-    my_group, my_core, my_part = lax.axis_index(HG), lax.axis_index(CORE), lax.axis_index(SP)
+    my_core, my_part = lax.axis_index(CORE), lax.axis_index(SP)
     block, model = enc_in.shape
     devices = groups * cores
     share = model // devices
-    heads = HEADS // groups
-    reach = (buckets.shape[1] - 1) // 2
     bf16, f32 = jnp.bfloat16, jnp.float32
 
     def packed(*weights):
         cut = [w.reshape(w.shape[0], groups, w.shape[1] // groups) for w in weights]
         return jnp.concatenate(cut, axis=2).transpose(1, 0, 2)
 
-    small = jnp.concatenate([enc_norm1, enc_norm2, enc_final, dec_norm1, dec_norm2, dec_norm3, enc_rel, dec_rel])
-    small = jnp.broadcast_to(small, (groups, 16, small.shape[0]))
+    rel_len = enc_rel.shape[0]
+    all_gains = jnp.stack([enc_norm1, enc_norm2, enc_final, dec_norm1, dec_norm2, dec_norm3])
+    all_rels = jnp.concatenate([enc_rel, dec_rel]).reshape(-1, HEADS)
+    small = jnp.concatenate([jnp.pad(w, ((0, 0), (0, 128 - w.shape[1]))) for w in (all_gains, all_rels)])
+    each = all_rels.shape[0] // 2
+    small = jnp.broadcast_to(jnp.pad(small, ((0, 16 - small.shape[0]), (0, 0))), (groups, 16, 128))
     (small, enc_kvq, dec_kvq), (enc_wo, dec_wo) = job_alone(
         sizes,
         1,
@@ -1611,13 +1844,11 @@
         [packed(enc_gate, enc_up), packed(cross_key, cross_value, cross_query), packed(dec_gate, dec_up)],
         [enc_down, cross_proj, dec_down],
     )
-    small = small.reshape(devices, 16, -1)[:, 0]
-    gains = small[:, : 6 * share].reshape(devices, 6, share).transpose(1, 0, 2).reshape(6, 1, model).astype(f32)
-    rel_len = enc_rel.shape[0]
-    rels = small[:, 6 * share :].reshape(devices, 2, rel_len).transpose(1, 0, 2).reshape(2, -1, HEADS)
-    rels = jnp.pad(rels, ((0, 0), (0, 0), (0, 128 - HEADS)))
-
-    bucket_count = devices * rel_len // HEADS
+    small = small.reshape(devices, 16, 128)
+    gains = small[:, :6, :share].transpose(1, 0, 2).reshape(6, 1, model).astype(f32)
+    rels = small[:, 6 : 6 + 2 * each].reshape(devices, 2, each, 128).transpose(1, 0, 2, 3).reshape(2, devices * each, 128)
+
+    bucket_count = devices * each
     numbers = jnp.arange(bucket_count, dtype=jnp.int32)[None, :, None]
     long = jnp.pad(buckets, ((0, 0), (block - 1, block)), mode="edge")[:, None, :]
     ahead = (long == numbers).astype(f32)
@@ -1645,7 +1876,6 @@
     ex, dx = enc_kept[0], dec_kept[0]
     tokens, hidden = groups * block, enc_wd.shape[0]
     token_f32, token_bf16, gain_f32 = ((block, model), f32), ((block, model), bf16), ((1, model), f32)
-    gu_grad, down_grad = ((model, 2 * hidden), bf16), ((hidden, model), bf16)
     buffer = (groups, block, model)
     (enc_out, memory, en2), _ = stage(
         sizes, 3, functools.partial(feed_forward_kernel, 1, 2), [ex, gains, enc_gu, enc_wd],
@@ -1653,65 +1883,39 @@
     )
     (cross_kept,), _ = attend(sizes, 4, (4,), [(dx, gains, cross_kvq, cross_wo, enc_k_ids, dec_q_ids, memory)])
     cx = cross_kept[0]
-    (dec_out, grad_cx, dg_d3, dw_dgu, dw_ddown), _ = stage(
-        sizes, 5, functools.partial(feed_both_kernel, 5), [cx, dec_cot, gains, dec_gu, dec_wd],
-        [token_f32, token_f32, gain_f32, gu_grad, down_grad], [buffer] * 6, (4, groups),
-    )
-
-    tie = lax.optimization_barrier
-
-    def summed(grads, before):
-        grads, _ = tie((grads, before))
-        return [lax.psum(g, SP) for g in grads]
-
-    (grad_dx, dg_d2, dw_ckvq, dw_co, dmem), rows_a = attend_back(
-        sizes, 6, dx, gains, 4, grad_cx, cross_kept, cross_kvq, cross_wo, None, None, GiveRows(sizes, [dw_dgu], [dw_ddown])
-    )
-    (grad_ex, dg_e2, dg_ef, dw_egu, dw_edown), rows_b = stage(
-        sizes, 7, functools.partial(feed_back_kernel, 1, 2), [ex, enc_out, enc_cot, dmem, gains, en2, enc_gu, enc_wd],
-        [token_f32, gain_f32, gain_f32, gu_grad, down_grad], [buffer] * 3, (2, groups),
-        GiveRows(sizes, [dw_ckvq], [dw_co]),
-    )
-    sum_ab = summed(rows_a + rows_b, [small])
-    grad_dx, grad_ex = tie((grad_dx, grad_ex))
-    (dec_in_grad, dg_d1, dw_dkvq, dw_do, dec_tab), rows_c = attend_back(
-        sizes, 8, dec_in, gains, 3, grad_dx, dec_kept, dec_kvq, dec_wo, ahead, 1, GiveRows(sizes, [dw_egu], [dw_edown])
-    )
-    grad_ex, sum_ab = tie((grad_ex, sum_ab))
-    sum_c = summed(rows_c, sum_ab)
-    (enc_in_grad, dg_e1, dw_ekvq, dw_eo, enc_tab), rows_d = attend_back(
-        sizes, 9, enc_in, gains, 0, grad_ex, enc_kept, enc_kvq, enc_wo, ahead, 0, GiveRows(sizes, [dw_dkvq], [dw_do])
-    )
-
-    def rel_grad(mine):
-        full = lax.dynamic_update_slice_in_dim(jnp.zeros((HEADS, bucket_count), f32), mine[:heads], my_group * heads, 0)
-        return full.T.reshape(-1)
-
-    small_grads = [dg_e1, dg_e2, dg_ef, dg_d1, dg_d2, dg_d3, rel_grad(enc_tab), rel_grad(dec_tab)]
-    packed_small = jnp.concatenate([v.reshape(devices, 1, -1) for v in small_grads], axis=2)
-    packed_small = jnp.broadcast_to(packed_small, (devices, 16, packed_small.shape[2]))
-    packed_small = packed_small.reshape(devices * 16, -1).astype(bf16)
-    dw_ekvq, sum_c = tie((dw_ekvq, sum_c))
-    sum_e, sum_d = finish(sizes, 10, GiveRows(sizes, [dw_ekvq, packed_small], [dw_eo]), rows_d)
-
-    def unpacked(whole, pieces):
-        each = whole.shape[2] // pieces
-        whole = whole.astype(f32)
-        return [whole[:, :, i * each : (i + 1) * each].transpose(1, 0, 2).reshape(share, groups * each) for i in range(pieces)]
-
-    dgu_rows, d_wd, cross_rows, c_wo = sum_ab
+    give_a = give_on(sizes, [(groups, cores, share, 2 * hidden)], [(cores, hidden // cores, model)])
+    dec_out, grad_cx, dg_d3, *rows_a = fused(
+        sizes, 5, lambda s, *refs: feed_both_kernel(s, 5, give_a, *refs), [cx, dec_cot, gains, dec_gu, dec_wd],
+        [token_f32, token_f32, gain_f32] + give_a.outs,
+        buffers_of([buffer] * 6 + [(groups, cores, share, 2 * hidden), (cores, hidden // cores, model)])
+        + [DMA((4, groups))] * 2
+        + give_a.scratch,
+    )
+
+    (dec_in_grad, grad_ex, dg_d1, dg_d2, dg_e2, dg_ef, rel_d), grads_d, sum_a, sum_b, rows_c = decoder_back(
+        sizes, 6, gains, (3, 4, 1, 2), grad_cx,
+        (dx, cross_kept, cross_kvq, cross_wo, None), (dec_in, dec_kept, dec_kvq, dec_wo, ahead[1]),
+        (ex, enc_out, enc_cot, en2, enc_gu, enc_wd), rows_a,
+    )
+    enc_in_grad, sum_c, sum_d, sum_e = encoder_back(
+        sizes, 7, gains, 0, grad_ex, (enc_in, enc_kept, enc_kvq, enc_wo, ahead[0]),
+        (dg_d1, dg_d2, dg_d3, dg_e2, dg_ef, rel_d), rows_c, grads_d,
+    )
+
+    dgu_rows, d_wd = sum_a
+    cross_rows, c_wo = sum_b
     egu_rows, e_wd = sum_c
     dkvq_rows, d_wo = sum_d
     ekvq_rows, small_rows, e_wo = sum_e
-    d_wd, c_wo, e_wd, d_wo, e_wo = [g[0].astype(f32) for g in (d_wd, c_wo, e_wd, d_wo, e_wo)]
-    e_wk, e_wv, e_wq = unpacked(ekvq_rows, 3)
-    e_wg, e_wu = unpacked(egu_rows, 2)
-    d_wk, d_wv, d_wq = unpacked(dkvq_rows, 3)
-    c_wk, c_wv, c_wq = unpacked(cross_rows, 3)
-    d_wg, d_wu = unpacked(dgu_rows, 2)
-    own = jnp.sum(small_rows[:, 0].astype(f32), axis=0)
-    s = [own[i * share : (i + 1) * share] for i in range(6)]
-    e_rel, d_rel = own[6 * share : 6 * share + rel_len], own[6 * share + rel_len :]
+    (
+        e_wk, e_wv, e_wq, e_wg, e_wu, d_wk, d_wv, d_wq, c_wk, c_wv, c_wq, d_wg, d_wu, d_wd, c_wo, e_wd, d_wo, e_wo
+    ) = unpack(
+        [ekvq_rows, egu_rows, dkvq_rows, cross_rows, dgu_rows, d_wd, c_wo, e_wd, d_wo, e_wo],
+        (3, 2, 3, 3, 2, 0, 0, 0, 0, 0),
+    )
+    own = jnp.sum(small_rows.astype(f32), axis=0)
+    s = [own[i, :share] for i in range(6)]
+    e_rel, d_rel = [own[6 + i * each : 6 + (i + 1) * each, :HEADS].reshape(rel_len) for i in range(2)]
     return (
         enc_out, dec_out, enc_in_grad, dec_in_grad,
         s[0], e_wq, e_wk, e_wv, e_wo, e_rel, s[1], e_wg, e_wu, e_wd, s[2],

time: 508 us -> 420 us (0.83)
  waiting for transfers between devices: 41 us -> 0 us
  local copies, waits for them, and re-layouts: 36.7 us -> 19.8 us
  between operations: 14.9 us -> 1.44 us
  other arithmetic: 12.9 us -> 5.05 us
  Pallas kernels: 398 us -> 391 us
    pallas_call x9 -> x4, Pallas kernels: 350 us -> 140 us  [stage(): pl.pallas_call(body, out_shape=tuple((jax.ShapeDtypeStruct(shape, dtype)...]
    pallas_call x1 -> x4, Pallas kernels: 47.8 us -> 250 us  [the longest x3 245 us: fused(): pl.pallas_call(functools.partial(kernel, sizes), out_shape=tuple((jax.Sha...]
    psum x2 -> x0, waiting for transfers between devices: 41 us -> none  [summed(): return [lax.psum(g, SP) for g in grads]]
    reshape x15 -> x2, local copies, waits for them, and re-layouts: 12.7 us -> 1.19 us  [fast_device(): own[6 + i * each:6 + (i + 1) * each, :HEADS].reshape(rel_len)]
    convert_element_type x11 -> x1, other arithmetic: 5.63 us -> 0.01 us  [fast_device(): small[:, :6, :share].transpose(1, 0, 2).reshape(6, 1, model).astype(f32)]
  transfers between devices with their start and end apart: 2 -> 0, of which waited for: 2 -> 0; matrix products, arithmetic and copies ran while one was open for 2% -> 0% of each run, Pallas kernels for 22% -> 0%
where the time goes in v5:
time: 420 us; the launch traced here: 417 us
  Pallas kernels  391 us (93%)
  local copies, waits for them, and re-layouts  19.8 us (5%)
  other arithmetic  5.05 us (1%)
    pallas_call x3, Pallas kernels, fused(): pl.pallas_call(functools.partial(kernel, sizes), out_shape=tuple((jax.Sha...  245 us
    pallas_call x4, Pallas kernels, stage(): pl.pallas_call(body, out_shape=tuple((jax.ShapeDtypeStruct(shape, dtype)...  140 us

profile of v5, /device:TPU:0, one launch (start us, length us, event | category | flops | bytes accessed | tf_op | source)
XLA Modules:
  0.0 417.1 jit_solution(17244310278483438505)
XLA Ops:
  0.7 0.8 reshape.205
  1.5 0.8 reshape.213
  2.3 0.6 reshape.214.refs_13_.refs_5_
  3.0 0.6 reshape.206.refs_5_
  3.6 1.1 reshape.197
  4.8 1.1 reshape.198
  7.0 1.3 maximum_bitcast_fusion.2
  8.6 0.6 broadcast_in_dim.18.refs_0_
  9.2 22.0 %shard_map.544 = (bf16[4,2,16,128]{3,2,1,0:T(8,128)(2,1)}, bf16[4,2,96,576]{3,2,1,0:T(8,128)(2,1)}, bf16[4,2,96,576]{3,2,1,0:T(8,128)(2,1)}, bf16[2,96,768]{2,1,0:T(8,128)(2,1)}, bf16[2,96,768]{2,1,0:T(8,128)(2,1)}) custom-call(bf16[4,16,128]{2,1,0:T(8,128)(2,1)} %broadcast_in_dim.18.refs_0_, bf16[4,96,576]{2,1,0:T(8,128)(2,1)} %get-tuple-element.206.refs_1_, ...), custom_call_target="tpu_custom_call" | custom-call | flops 20000000000 | bytes 10000000 | tf_op jit(solution)/shard_map/pallas_call | solution.py:1046
  31.3 0.7 slice.68
  32.0 0.7 reshape.232.refs_1_.refs_9_.refs_2_.refs_0_
  32.7 0.8 slice.69
  33.5 0.6 copy.72
  34.4 0.8 reverse.2
  35.4 0.6 fusion.refs_7_.refs_15_
  36.1 1.0 maximum_bitcast_fusion.refs_16_
  37.3 1.0 maximum_bitcast_fusion.1.refs_18_
  38.3 1.4 copy.80.refs_4_
  40.3 0.9 maximum_bitcast_fusion.4.refs_17_
  41.3 1.3 copy.81.refs_12_
  42.6 66.6 %shard_map.545 = (f32[64,768]{1,0:T(8,128)}, bf16[256,768]{1,0:T(8,128)(2,1)}, bf16[256,192]{1,0:T(8,128)(2,1)}, bf16[4,2,4,64,384]{4,3,2,1,0:T(8,128)(2,1)}, bf...) custom-call(bf16[64,768]{1,0:T(8,128)(2,1)} %refs_2_.1, ...), custom_call_target="tpu_custom_call" | custom-call | flops 20000000000 | bytes 10000000 | tf_op jit(solution)/shard_map/pallas_call | solution.py:1046
  109.2 16.2 %shard_map.546 = (f32[64,768]{1,0:T(8,128)}, bf16[64,768]{1,0:T(8,128)(2,1)}, bf16[256,768]{1,0:T(8,128)(2,1)}) custom-call(f32[64,768]{1,0:T(8,128)} %get-tuple-element.117.refs_0_.refs_24_, f32[6,1,768]{2,1,0:T(1,128)} %reshape.232.refs_1_.refs_9_.refs_2_.refs_0_, bf16[768,1024]{1,0:T(8,128)(2,1)} %bitcast.82, bf16[512,768]{1,0:T(8,128)(2,1)} %bitcast.91), custom_call_target="tpu_custom_call" | custom-call | flops 20000000000 | bytes 10000000 | tf_op jit(solution)/shard_map/pallas_call | solution.py:1046
  125.4 35.6 %shard_map.547 = (f32[64,768]{1,0:T(8,128)}, bf16[256,768]{1,0:T(8,128)(2,1)}, bf16[256,192]{1,0:T(8,128)(2,1)}, bf16[4,2,4,64,384]{4,3,2,1,0:T(8,128)(2,1)}, bf...) custom-call(f32[64,768]{1,0:T(8,128)} %get-tuple-element.121.refs_0_.refs_2, ...), custom_call_target="tpu_custom_call" | custom-call | flops 20000000000 | bytes 10000000 | tf_op jit(solution)/shard_map/pallas_call | solution.py:1046
  160.9 36.9 %shard_map.548 = (f32[64,768]{1,0:T(8,128)}, f32[64,768]{1,0:T(8,128)}, f32[1,768]{1,0:T(1,128)}, bf16[4,96,1024]{2,1,0:T(8,128)(2,1)}, bf16[1,256,768]{2,1,0:T(8,128)(2,1)}) custom-call(f32[64,768]{1,0:T(8,128)} %get-tuple-element.125.refs_0_, bf16[64,768]{1,0:T(8,128)(2,1)} %refs_1_.1, f32[6,1,768]{2,1,0:T(1,128)} %reshape.232.refs_1_.refs_9_.refs_2_.refs_0_, ...), custom_call_target="tpu_custom_call" | custom-call | flops 20000000000 | bytes 10000000 | tf_op jit(solution)/shard_map/pallas_call | solution.py:1706
  198.1 0.6 slice_bitcast_fusion
  198.7 112.7 %shard_map.549 = (f32[64,768]{1,0:T(8,128)}, f32[64,768]{1,0:T(8,128)}, f32[1,768]{1,0:T(1,128)}, f32[1,768]{1,0:T(1,128)}, f32[1,768]{1,0:T(1,128)}, /*index=5*...) custom-call(f32[6,1,768]{2,1,0:T(1,128)} %reshape.232.refs_1_.refs_9, ...), custom_call_target="tpu_custom_call" | custom-call | flops 20000000000 | bytes 10000000 | tf_op jit(solution)/shard_map/pallas_call | solution.py:1706
  311.4 95.2 %shard_map.550 = (f32[64,768]{1,0:T(8,128)}, bf16[4,96,1024]{2,1,0:T(8,128)(2,1)}, bf16[1,256,768]{2,1,0:T(8,128)(2,1)}, bf16[4,96,576]{2,1,0:T(8,128)(2,1)}, bf...) custom-call(f32[6,1,768]{2,1,0:T(1,128)} %reshape.232.refs_1_.refs_9, ...), custom_call_target="tpu_custom_call" | custom-call | flops 20000000000 | bytes 10000000 | tf_op jit(solution)/shard_map/pallas_call | solution.py:1706
  406.8 5.6 %shard_map.551 = (f32[96,768]{1,0:T(8,128)}, f32[96,768]{1,0:T(8,128)}, f32[96,768]{1,0:T(8,128)}, f32[96,2048]{1,0:T(8,128)}, f32[96,2048]{1,0:T(8,128)}, /*ind...) custom-call(bf16[4,96,576]{2,1,0:T(8,128)(2,1)} %get-tuple-element.1, ...), custom_call_target="tpu_custom_call" | custom-call | tf_op jit(solution)/shard_map/pallas_call | solution.py:1801
  414.1 0.7 copy.98
  414.8 0.7 copy.99
  415.5 0.7 copy.100
  416.2 0.7 copy.101
  (95 shorter events, 4.6 us)
Async XLA Ops:
  0.7 5.3 %copy-start.8 = (bf16[96,768]{1,0:T(8,128)(2,1)S(1)}, bf16[96,768]{1,0:T(8,128)(2,1)}, u32[]{:S(2)}) copy-start(bf16[96,768]{1,0:T(8,128)(2,1)} %param.41) | copy-start | bytes 442372
  0.7 5.5 %copy-start.9 = (bf16[96,768]{1,0:T(8,128)(2,1)S(1)}, bf16[96,768]{1,0:T(8,128)(2,1)}, u32[]{:S(2)}) copy-start(bf16[96,768]{1,0:T(8,128)(2,1)} %param.53) | copy-start | bytes 442372
  0.7 5.8 %copy-start.10 = (bf16[96,768]{1,0:T(8,128)(2,1)S(1)}, bf16[96,768]{1,0:T(8,128)(2,1)}, u32[]{:S(2)}) copy-start(bf16[96,768]{1,0:T(8,128)(2,1)} %param.54) | copy-start | bytes 442372
  4.8 2.0 copy-start.11
  6.7 1.7 copy-start.25
  6.7 1.7 copy-start.26
  6.7 1.8 copy-start.19
  6.7 1.8 copy-start.20
  6.7 1.8 copy-start.21
  6.7 1.8 copy-start.22
  6.7 1.8 copy-start.23
  6.8 1.8 copy-start.24
  9.2 24.9 %copy-start.17 = (s32[2,257]{1,0:T(2,128)S(1)}, s32[2,257]{1,0:T(2,128)}, u32[]{:S(2)}) copy-start(s32[2,257]{1,0:T(2,128)} %param.39) | copy-start | bytes 6172
  9.2 26.8 %copy-start = (bf16[96,2048]{1,0:T(8,128)(2,1)S(1)}, bf16[96,2048]{1,0:T(8,128)(2,1)}, u32[]{:S(2)}) copy-start(bf16[96,2048]{1,0:T(8,128)(2,1)} %param.48) | copy-start | bytes 1179652
  9.2 26.8 %copy-start.1 = (bf16[96,2048]{1,0:T(8,128)(2,1)S(1)}, bf16[96,2048]{1,0:T(8,128)(2,1)}, u32[]{:S(2)}) copy-start(bf16[96,2048]{1,0:T(8,128)(2,1)} %param.47) | copy-start | bytes 1179652
  36.0 1.1 copy-start.2
  36.0 1.2 copy-start.3
  37.2 1.1 copy-start.15
  37.2 2.4 copy-start.12
  37.2 2.6 copy-start.13
  38.3 1.8 copy-start.14
  39.6 1.7 copy-start.16
  406.7 5.7 %copy-start.18 = (bf16[4,16,128]{2,1,0:T(8,128)(2,1)S(1)}, bf16[4,16,128]{2,1,0:T(8,128)(2,1)}, u32[]{:S(2)}) copy-start(bf16[4,16,128]{2,1,0:T(8,128)(2,1)} %get-tuple-element.165) | copy-start | bytes 49156
  406.7 7.4 %copy-start.4 = (f32[64,768]{1,0:T(8,128)S(1)}, f32[64,768]{1,0:T(8,128)}, u32[]{:S(2)}) copy-start(f32[64,768]{1,0:T(8,128)} %get-tuple-element.244.refs_25_) | copy-start | bytes 589828
  406.7 8.1 %copy-start.5 = (f32[64,768]{1,0:T(8,128)S(1)}, f32[64,768]{1,0:T(8,128)}, u32[]{:S(2)}) copy-start(f32[64,768]{1,0:T(8,128)} %get-tuple-element.245) | copy-start | bytes 589828
  406.7 8.8 %copy-start.7 = (f32[64,768]{1,0:T(8,128)S(1)}, f32[64,768]{1,0:T(8,128)}, u32[]{:S(2)}) copy-start(f32[64,768]{1,0:T(8,128)} %get-tuple-element.246) | copy-start | bytes 589828
  406.7 9.4 %copy-start.6 = (f32[64,768]{1,0:T(8,128)S(1)}, f32[64,768]{1,0:T(8,128)}, u32[]{:S(2)}) copy-start(f32[64,768]{1,0:T(8,128)} %get-tuple-element.247) | copy-start | bytes 589828
